TPU v7x, 32 devices: a whole 2x2x4 slice. The times are simulated.
32 devices in a mesh: groups: 2 (over y), beam: 16 (over z, x, core).
Axes of the slice: x: 2, y: 2, z: 4, core: 2. Of those that a mesh axis runs over, the one named last changes fastest.
Arguments:
- potential: float32 [4, 512, 512], P('groups', 'beam'), parts along dimension 0, may hold values from -5 to 5
- beam_tilts: int32 [16, 2], replicated, may hold values from -16 to 16
- aperture: float32 [16], replicated, may hold values from 0.3 to 3
- aberration: float32 [16], replicated, may hold values from -3.140625 to 3.140625
- probe_spots: int32 [8, 32, 2], P('groups'), parts along dimension 0, may hold values from 0 to 127
- crop_anchor: int32 [4], P('groups'), parts along dimension 0, may hold values from 0 to 256
Outputs:
- diffraction: float32 [1024, 32, 128], P(('groups', 'beam')), parts along dimension 0
There are 2 independent parts, one for each index of `groups`. A program takes and returns all parts, laid end to end along the dimension named above; an argument that names none is the same for every part. Nothing has to cross between parts.
Inputs may be any that keep to these rules, and one draw needn't show every extreme that they name: `probe_spots`: positions inside a tile. `crop_anchor`: the window lies inside the grid.
All inputs are finite; a program needn't handle non-finite values.
Results may differ from a plain program's by a relative error of at most 0.0003.
Values sent between devices are 32-bit elements; how exact they have to be, the bound alone decides.
No kernel may reach another device: no remote copies, remote signals or barrier semaphores. Data moves between devices by JAX's collectives and lax.ppermute only.
A program may use at most 64 MiB of HBM per device.

v0:
```python
import jax
import jax.numpy as jnp
from jax import lax
from jax.sharding import PartitionSpec as P

CROP = 256
TILE = 128


precise = lax.Precision.HIGHEST


def dft_factors(row_count, col_count, period, direction):
    product = (
        jnp.arange(row_count, dtype=jnp.int32)[:, None]
        * jnp.arange(col_count, dtype=jnp.int32)[None, :]
    )
    phase_angle = 2.0 * jnp.pi / period * jnp.remainder(product, period).astype(jnp.float32)
    return (jnp.cos(phase_angle), direction * jnp.sin(phase_angle))


def complex_einsum(formula, left_real, left_imag, right_real, right_imag):
    real_real = jnp.einsum(formula, left_real, right_real, precision=precise)
    imag_imag = jnp.einsum(formula, left_imag, right_imag, precision=precise)
    real_imag = jnp.einsum(formula, left_real, right_imag, precision=precise)
    imag_real = jnp.einsum(formula, left_imag, right_real, precision=precise)
    return (real_real - imag_imag, real_imag + imag_real)


def twiddle(values_real, values_imag, table_real, table_imag):
    return (
        values_real * table_real - values_imag * table_imag,
        values_real * table_imag + values_imag * table_real,
    )


def rows_forward(field_real, field_imag):
    length, breadth = field_real.shape
    inner_size = length // 32
    blocks_real = field_real.reshape(32, inner_size, breadth)
    blocks_imag = field_imag.reshape(32, inner_size, breadth)
    first_real, first_imag = dft_factors(32, 32, 32, -1.0)
    part_real, part_imag = complex_einsum(
        "mnc,mj->jnc", blocks_real, blocks_imag, first_real, first_imag
    )
    turn_real, turn_imag = dft_factors(32, inner_size, length, -1.0)
    part_real, part_imag = twiddle(
        part_real, part_imag, turn_real[:, :, None], turn_imag[:, :, None]
    )
    second_real, second_imag = dft_factors(inner_size, inner_size, inner_size, -1.0)
    done_real, done_imag = complex_einsum(
        "jnc,nk->kjc", part_real, part_imag, second_real, second_imag
    )
    return (done_real.reshape(length, breadth), done_imag.reshape(length, breadth))


def rows_inverse(field_real, field_imag):
    length, breadth = field_real.shape
    inner_size = length // 32
    blocks_real = field_real.reshape(inner_size, 32, breadth)
    blocks_imag = field_imag.reshape(inner_size, 32, breadth)
    first_real, first_imag = dft_factors(inner_size, inner_size, inner_size, 1.0)
    part_real, part_imag = complex_einsum(
        "kjc,kn->njc", blocks_real, blocks_imag, first_real, first_imag
    )
    turn_real, turn_imag = dft_factors(inner_size, 32, length, 1.0)
    part_real, part_imag = twiddle(
        part_real, part_imag, turn_real[:, :, None], turn_imag[:, :, None]
    )
    second_real, second_imag = dft_factors(32, 32, 32, 1.0)
    done_real, done_imag = complex_einsum(
        "njc,jm->mnc", part_real, part_imag, second_real, second_imag
    )
    inverse_scale = 1.0 / length
    return (
        done_real.reshape(length, breadth) * inverse_scale,
        done_imag.reshape(length, breadth) * inverse_scale,
    )


def cols_forward(field_real, field_imag):
    height, length = field_real.shape
    inner_size = length // 8
    blocks_real = field_real.reshape(height, 8, inner_size)
    blocks_imag = field_imag.reshape(height, 8, inner_size)
    first_real, first_imag = dft_factors(8, 8, 8, -1.0)
    part_real, part_imag = complex_einsum(
        "rmn,mj->rjn", blocks_real, blocks_imag, first_real, first_imag
    )
    turn_real, turn_imag = dft_factors(8, inner_size, length, -1.0)
    part_real, part_imag = twiddle(part_real, part_imag, turn_real[None], turn_imag[None])
    second_real, second_imag = dft_factors(inner_size, inner_size, inner_size, -1.0)
    return complex_einsum("rjn,nk->rjk", part_real, part_imag, second_real, second_imag)


def cols_inverse(spec_real, spec_imag):
    height = spec_real.shape[0]
    inner_size = spec_real.shape[2]
    length = 8 * inner_size
    first_real, first_imag = dft_factors(inner_size, inner_size, inner_size, 1.0)
    part_real, part_imag = complex_einsum(
        "rjk,kn->rjn", spec_real, spec_imag, first_real, first_imag
    )
    turn_real, turn_imag = dft_factors(8, inner_size, length, 1.0)
    part_real, part_imag = twiddle(part_real, part_imag, turn_real[None], turn_imag[None])
    second_real, second_imag = dft_factors(8, 8, 8, 1.0)
    done_real, done_imag = complex_einsum(
        "rjn,jm->rmn", part_real, part_imag, second_real, second_imag
    )
    inverse_scale = 1.0 / length
    return (
        done_real.reshape(height, length) * inverse_scale,
        done_imag.reshape(height, length) * inverse_scale,
    )


def propagator_table(length):
    inner_size = length // 8
    index_rows = jnp.arange(length, dtype=jnp.int32)
    freq_rows = jnp.where(index_rows < length // 2, index_rows, index_rows - length)
    index_cols = (
        jnp.arange(8, dtype=jnp.int32)[:, None]
        + 8 * jnp.arange(inner_size, dtype=jnp.int32)[None, :]
    )
    freq_cols = jnp.where(index_cols < length // 2, index_cols, index_cols - length)
    square = freq_rows[:, None, None] ** 2 + freq_cols[None, :, :] ** 2
    phase_angle = jnp.pi / length * jnp.remainder(square, 2 * length).astype(jnp.float32)
    passing = 9 * square < length * length
    return (
        jnp.where(passing, jnp.cos(phase_angle), 0.0),
        jnp.where(passing, -jnp.sin(phase_angle), 0.0),
    )


def per_device(potential, beam_tilts, aperture, aberration, probe_spots, crop_anchor):
    layer_count = potential.shape[0]
    length = potential.shape[2]
    device = lax.axis_index("beam")
    own_tilt = lax.dynamic_slice_in_dim(beam_tilts, device, 1, 0)
    coords = jnp.arange(length, dtype=jnp.int32)
    plane_phase = jnp.remainder(
        own_tilt[0, 0] * coords[:, None] + own_tilt[0, 1] * coords[None, :], length
    )
    plane_angle = 2.0 * jnp.pi / length * plane_phase.astype(jnp.float32)
    wave_real = jnp.cos(plane_angle)
    wave_imag = jnp.sin(plane_angle)
    pass_real, pass_imag = propagator_table(length)
    for layer_index in range(layer_count):
        full_slice = lax.all_gather(potential[layer_index], "beam", axis=0, tiled=True)
        trans_real = jnp.cos(full_slice)
        trans_imag = jnp.sin(full_slice)
        wave_real, wave_imag = twiddle(wave_real, wave_imag, trans_real, trans_imag)
        if layer_index + 1 < layer_count:
            wave_real, wave_imag = rows_forward(wave_real, wave_imag)
            spec_real, spec_imag = cols_forward(wave_real, wave_imag)
            spec_real, spec_imag = twiddle(spec_real, spec_imag, pass_real, pass_imag)
            wave_real, wave_imag = cols_inverse(spec_real, spec_imag)
            wave_real, wave_imag = rows_inverse(wave_real, wave_imag)
    per_side = CROP // TILE
    crop_real = lax.dynamic_slice(
        wave_real, (crop_anchor[0], crop_anchor[1]), (CROP, CROP)
    ).reshape(per_side, TILE, per_side, TILE)
    crop_imag = lax.dynamic_slice(
        wave_imag, (crop_anchor[0], crop_anchor[1]), (CROP, CROP)
    ).reshape(per_side, TILE, per_side, TILE)
    tile_real, tile_imag = dft_factors(TILE, TILE, TILE, -1.0)
    part_real, part_imag = complex_einsum(
        "aybx,xk->aybk", crop_real, crop_imag, tile_real, tile_imag
    )
    spec_real, spec_imag = complex_einsum(
        "aybk,yj->abjk", part_real, part_imag, tile_real, tile_imag
    )
    tile_count = per_side * per_side
    payload = jnp.stack(
        (spec_real.reshape(tile_count * TILE, TILE), spec_imag.reshape(tile_count * TILE, TILE))
    )[:, None]
    arrived = lax.all_to_all(payload, "beam", split_axis=2, concat_axis=1, tiled=True)
    rows_here = arrived.shape[2]
    my_tile = device * rows_here // TILE
    probe_here = lax.dynamic_slice_in_dim(probe_spots, my_tile, 1, 0)[0]
    anchor_rows = crop_anchor[0] + TILE * (my_tile // per_side)
    anchor_cols = crop_anchor[1] + TILE * (my_tile % per_side)
    spot_rows = anchor_rows + probe_here[:, 0]
    spot_cols = anchor_cols + probe_here[:, 1]
    phase_index = jnp.remainder(
        spot_rows[:, None] * beam_tilts[None, :, 0] + spot_cols[:, None] * beam_tilts[None, :, 1],
        length,
    )
    weight_angle = aberration[None, :] - 2.0 * jnp.pi / length * phase_index.astype(jnp.float32)
    weight_real = aperture[None, :] * jnp.cos(weight_angle)
    weight_imag = aperture[None, :] * jnp.sin(weight_angle)
    exit_real, exit_imag = complex_einsum(
        "pb,brk->rpk", weight_real, weight_imag, arrived[0], arrived[1]
    )
    intensity = exit_real * exit_real + exit_imag * exit_imag
    partial_sums = jnp.sum(intensity, axis=(0, 2))
    tile_slots = jnp.where(
        jnp.arange(tile_count, dtype=jnp.int32)[:, None] == my_tile, partial_sums[None, :], 0.0
    )
    totals = lax.psum(tile_slots, "beam")
    own_total = lax.dynamic_slice_in_dim(totals, my_tile, 1, 0)[0]
    mean_level = own_total / (TILE * TILE)
    return intensity / (mean_level[None, :, None] + 1e-06)


def solution(mesh):
    placed = (P("groups", "beam", None), P(), P(), P(), P("groups", None, None), P("groups"))
    return jax.shard_map(
        per_device,
        mesh=mesh,
        in_specs=placed,
        out_specs=P(("groups", "beam"), None, None),
        check_vma=False,
    )
```

profile of v0, /device:TPU:0, one launch (start us, length us, event | category | flops | bytes accessed | tf_op | source)
XLA Modules:
  0.0 222.4 jit_solution(5073884342935992165)
XLA Ops:
  6.5 1.5 fusion.447
  8.1 0.7 all-gather.7.cloned.1.call-update
  9.1 1.3 fusion.449
  13.0 0.8 constant_dynamic-slice_fusion.1
  14.5 1.3 iota_multiply_fusion
  17.0 33.1 %all-gather.5.cloned.1.call-done = f32[1,512,512]{2,1,0:T(8,128)} async-done(((f32[1,32,512]{2,1,0:T(8,128)}), f32[1,512,512]{2,1,0:T(8,128)}) %all-gather.5.cloned.1.call-update) | async-done | bytes 1048592 | tf_op jit(solution)/shard_map/all_gather | solution.py:149
  50.1 4.7 %fusion.445 = (f32[1,512,512]{2,1,0:T(8,128)S(1)}, f32[1,512,512]{2,1,0:T(8,128)S(1)}) fusion(f32[1,512,512]{2,1,0:T(8,128)} %all-gather.5.cloned.1.call-done), kind=kLoop, calls=%fused_computation.502 | loop fusion | bytes 3145728 | tf_op jit(solution)/shard_map/cos | solution.py:150
  54.8 4.8 %fusion.17 = (f32[512,512]{1,0:T(8,128)S(1)}, f32[512,512]{1,0:T(8,128)S(1)}) fusion(f32[1,512,512]{2,1,0:T(8,128)S(1)} %get-tuple-element.20, f32[1,512,512]{2,1,0:T(8,128)S(1)} %get-tuple-element.19, s32[512]{0:T(512)S(1)} %get-tuple-element.35, s32[512]{0:T(512)S(1)} %get-tuple-element.36), kind=kLoop, calls=%fused_computation.52 | loop fusion | flops 5242880 | bytes 4198400 | tf_op jit(solution)/shard_map/add | solution.py:33
  59.6 1.6 fusion.52
  61.2 1.6 fusion.50
  62.8 1.6 convolution_subtract_fusion.7
  64.4 1.8 multiply_add_fusion.3
  66.3 1.5 fusion.44
  67.8 1.5 fusion.46
  69.3 1.5 convolution_subtract_fusion.6
  71.4 2.0 reshape_reshape.6
  73.4 2.6 %copy.140 = f32[512,8,64]{0,1,2:T(8,128)S(1)} copy(f32[512,8,64]{2,1,0:T(8,128)} %reshape_reshape.6) | data formatting | bytes 2097152 | tf_op jit(solution)/shard_map/reshape;reshape | solution.py:84
  76.0 2.1 fusion.202
  78.1 2.0 fusion.208
  80.1 1.5 convolution_add_fusion.6
  82.6 1.2 copy.144
  83.8 2.4 %convolution_add_fusion.5 = f32[8,512,64]{1,0,2:T(8,128)S(1)} fusion(f32[8,512,64]{1,0,2:T(8,128)} %fusion.202, f32[512,8,64]{0,1,2:T(8,128)S(1)} %copy.144), kind=kOutput, calls=%fused_computation.27 | convolution fusion | flops 25428864 | bytes 3145728 | tf_op jit(solution)/shard_map/rmn,mj->rjn/dot_general | solution.py:26
  86.2 1.3 add_bitcast_fusion
  87.5 1.7 fusion.40
  89.2 2.2 fusion.38
  91.4 1.8 convolution_subtract_fusion.4
  93.3 1.8 convolution_add_fusion.4
  95.1 5.8 %fusion.87 = f32[512,8,64]{0,2,1:T(8,128)S(1)} fusion(f32[512,8,64]{0,2,1:T(8,128)S(1)} %convolution_add_fusion.4, f32[512,8,64]{0,2,1:T(8,128)S(1)} %convolution_subtract_fusion.4, s32[8,64]{1,0:T(8,128)S(1)} %fusion.199, s32[512]{0:T(512)S(1)} %fusion.239), kind=kOutput, calls=%fused_computation.149 | convolution fusion | flops 207151104 | bytes 3149824 | tf_op jit(solution)/shard_map/rjk,kn->rjn/dot_general | solution.py:25
  100.9 6.0 %fusion.93 = f32[512,8,64]{0,2,1:T(8,128)S(1)} fusion(f32[512,8,64]{0,2,1:T(8,128)S(1)} %convolution_add_fusion.4, f32[512,8,64]{0,2,1:T(8,128)S(1)} %convolution_subtract_fusion.4, s32[8,64]{1,0:T(8,128)S(1)} %fusion.199, s32[512]{0:T(512)S(1)} %fusion.239), kind=kOutput, calls=%fused_computation.155 | convolution fusion | flops 207151104 | bytes 3149824 | tf_op jit(solution)/shard_map/rjk,kn->rjn/dot_general | solution.py:23
  106.9 5.9 %convolution_subtract_fusion.3 = f32[512,8,64]{0,2,1:T(8,128)S(1)} fusion(f32[512,8,64]{0,2,1:T(8,128)S(1)} %fusion.93, f32[512,8,64]{0,2,1:T(8,128)S(1)} %convolution_add_fusion.4, f32[512,8,64]{0,2,1:T(8,128)S(1)} %convolution_subtract_fusion.4, s32[8,64]{1,0:T(8,128)S(1)} %fusion.199, s32[512]{0:T(512)S(1)} %fusion.239), kind=kOutput, calls=%fused_computation.24 | convolution fusion | flops 207413248 | bytes 4198400 | tf_op jit(solution)/shard_map/rjk,kn->rjn/dot_general | solution.py:24
  112.8 6.5 %multiply_add_fusion.1 = (f32[512,8,64]{0,2,1:T(8,128)S(1)}, f32[512,8,64]{0,2,1:T(8,128)S(1)}) fusion(f32[512,8,64]{0,2,1:T(8,128)S(1)} %convolution_subtract_fusion.3, f32[8,64]{1,0:T(8,128)S(1)} %get-tuple-element.39, f32[8,64]{1,0:T(8,128)S(1)} %get-tuple-element.40, f32[512,8,64]{0,2,1:T(8,128)S(1)} %fusion.87, ...), kind=kOutput, calls=%fused_computation.59 | convolution fusion | flops 208986112 | bytes 6299648 | tf_op jit(solution)/shard_map/rjk,kn->rjn/dot_general | solution.py:26
  119.3 1.5 fusion.32
  120.8 2.5 %fusion.34 = f32[8,512,64]{1,0,2:T(8,128)} fusion(f32[512,8,64]{0,2,1:T(8,128)S(1)} %get-tuple-element.14), kind=kOutput, calls=%fused_computation.85 | convolution fusion | flops 25166720 | bytes 2097152 | tf_op jit(solution)/shard_map/rjn,jm->rmn/dot_general | solution.py:23
  123.3 1.5 fusion.3
  124.9 1.1 copy.159
  126.5 3.3 %fusion.5 = f32[512,8,64]{0,1,2:T(8,128)S(1)} fusion(f32[8,512,64]{1,0,2:T(8,128)} %fusion.34, f32[512,8,64]{0,2,1:T(8,128)} %copy-done.1), kind=kOutput, calls=%fused_computation.22 | convolution fusion | flops 25691008 | bytes 3145728 | tf_op jit(solution)/shard_map/rjn,jm->rmn/dot_general | solution.py:24
  129.8 2.4 %copy.155 = f32[512,8,64]{2,1,0:T(8,128)} copy(f32[512,8,64]{0,1,2:T(8,128)S(1)} %fusion.5) | data formatting | bytes 2097152 | tf_op jit(solution)/shard_map/mul | solution.py:112
  132.1 1.9 mul.1101
  134.1 1.5 fusion.28
  135.6 1.5 fusion.26
  137.1 1.5 convolution_subtract_fusion.1
  138.7 1.7 multiply_add_fusion
  140.4 1.6 fusion.22
  142.0 1.6 fusion.1
  143.7 0.6 copy.165
  144.3 1.6 fusion.20
  145.9 1.8 fusion
  148.4 4.7 %cosine_bitcast_fusion = (f32[512,512]{1,0:T(8,128)S(1)}, f32[512,512]{1,0:T(8,128)S(1)}) fusion(f32[1,512,512]{2,1,0:T(8,128)} %all-gather.7.cloned.1.call-done), kind=kLoop, calls=%fused_computation.56 | loop fusion | bytes 3145728 | tf_op jit(solution)/shard_map/cos | solution.py:150
  153.5 0.6 fusion.64
  154.2 0.6 fusion.66
  154.9 0.6 convolution_subtract_fusion.10
  155.6 0.6 fusion.74
  156.2 0.6 fusion.77
  157.5 0.6 convolution_subtract_fusion.9
  158.2 0.6 convolution_add_fusion.9
  158.8 1.3 pad_maximum_fusion
  160.1 3.9 %all-to-all-start = ((f32[2,1,512,128]{3,1,0,2:T(1,128)}), f32[2,1,512,128]{3,1,0,2:T(1,128)S(1)}, u32[]{:S(2)}, u32[]{:S(2)}) async-start(f32[2,1,512,128]{3,1,0,2:T(1,128)} %bitcast.44), calls=%async_computation | async-start | bytes 1048576 | tf_op jit(solution)/shard_map/all_to_all | solution.py:177
  165.4 12.9 %all-to-all-done = f32[2,1,512,128]{3,1,0,2:T(1,128)S(1)} async-done(((f32[2,1,512,128]{3,1,0,2:T(1,128)}), f32[2,1,512,128]{3,1,0,2:T(1,128)S(1)}, u32[]{:S(2)}, u32[]{:S(2)}) %all-to-all-start) | async-done | bytes 524320 | tf_op jit(solution)/shard_map/all_to_all | solution.py:177
  178.7 0.8 fusion.60
  179.5 0.8 fusion.56
  180.3 0.8 fusion.6
  181.1 0.9 fusion.450
  182.1 32.3 %psum.7 = f32[4,32]{1,0:T(4,128)S(1)} all-reduce(f32[4,32]{1,0:T(4,128)S(1)} %broadcast_select_fusion), channel_id=1, replica_groups=mesh['groups'=2,'beam'=16] {'beam'}, use_global_device_ids=true, to_apply=%region_1.2 | all-reduce | flops 128 | bytes 1024 | tf_op jit(solution)/shard_map/psum | solution.py:200
  214.4 0.9 divide_bitcast_fusion
  (42 shorter events, 5.6 us)
Async XLA Ops:
  6.5 158.8 %copy-start = (s32[4,32,2]{1,2,0:T(2,128)S(1)}, s32[4,32,2]{1,2,0:T(2,128)}, u32[]{:S(2)}) copy-start(s32[4,32,2]{1,2,0:T(2,128)} %param.10) | copy-start | bytes 3076
  6.5 43.6 %all-gather.5.cloned.1.call-start = ((), (), s32[]{:S(2)}) async-start(), calls=%async_computation.1 | async-start | bytes 1114112 | tf_op jit(solution)/shard_map/all_gather | solution.py:149
  8.1 140.3 %all-gather.7.cloned.1.call-start = ((), (), s32[]{:S(2)}) async-start(), calls=%async_computation.2 | async-start | bytes 1114112 | tf_op jit(solution)/shard_map/all_gather | solution.py:149
  83.8 2.4 %copy-start.2 = (f32[8,512,64]{1,0,2:T(8,128)S(1)}, f32[8,512,64]{1,0,2:T(8,128)}, u32[]{:S(2)}) copy-start(f32[8,512,64]{1,0,2:T(8,128)} %fusion.208) | copy-start | bytes 3145732
  119.3 4.0 %copy-start.1 = (f32[512,8,64]{0,2,1:T(8,128)}, f32[512,8,64]{0,2,1:T(8,128)S(1)}, u32[]{:S(2)}) copy-start(f32[512,8,64]{0,2,1:T(8,128)S(1)} %get-tuple-element.13) | copy-start | bytes 3145732
  156.9 8.5 %copy-start.5 = (s32[16,2]{0,1:T(2,128)S(1)}, s32[16,2]{0,1:T(2,128)}, u32[]{:S(2)}) copy-start(s32[16,2]{0,1:T(2,128)} %param.7) | copy-start | bytes 388
  158.1 20.5 %copy-start.3 = (f32[16]{0:T(128)S(1)}, f32[16]{0:T(128)}, u32[]{:S(2)}) copy-start(f32[16]{0:T(128)} %param.8) | copy-start | bytes 196
  158.2 20.5 %copy-start.4 = (f32[16]{0:T(128)S(1)}, f32[16]{0:T(128)}, u32[]{:S(2)}) copy-start(f32[16]{0:T(128)} %param.9) | copy-start | bytes 196
  160.1 18.2 %all-to-all-start = ((f32[2,1,512,128]{3,1,0,2:T(1,128)}), f32[2,1,512,128]{3,1,0,2:T(1,128)S(1)}, u32[]{:S(2)}, u32[]{:S(2)}) async-start(f32[2,1,512,128]{3,1,0,2:T(1,128)} %bitcast.44), calls=%async_computation | async-start | bytes 1048576 | tf_op jit(solution)/shard_map/all_to_all | solution.py:177
Sparse Core Ops, SparseCore 0:
  9.5 40.5 all-gather.4
  52.3 36.8 all-gather.6
where the time goes:
time: 226 us; the launch traced here: 222 us
  matrix products  82.3 us (36%)
  waiting for transfers between devices  46.7 us (21%)
  blocking collectives  32.3 us (14%)
  local copies, waits for them, and re-layouts  28.8 us (13%)
  between operations  19.3 us (9%)
  other arithmetic  9.01 us (4%)
  starting transfers between devices  3.99 us (2%)
    all_gather x2, waiting for transfers between devices, per_device(): lax.all_gather(potential[layer_index], 'beam', axis=0, tiled=True)  33.1 us
    psum x1, blocking collectives, per_device(): totals = lax.psum(tile_slots, 'beam')  32.3 us
    dot_general x11, matrix products, complex_einsum(): imag_real = jnp.einsum(formula, left_imag, right_real, precision=precise)  21.2 us
    dot_general x11, matrix products, complex_einsum(): imag_imag = jnp.einsum(formula, left_imag, right_imag, precision=precise)  20.8 us
    dot_general x11, matrix products, complex_einsum(): real_real = jnp.einsum(formula, left_real, right_real, precision=precise)  20.5 us
    dot_general x11, matrix products, complex_einsum(): real_imag = jnp.einsum(formula, left_real, right_imag, precision=precise)  19.8 us
    all_to_all x1, waiting for transfers between devices, per_device(): lax.all_to_all(payload, 'beam', split_axis=2, concat_axis=1, tiled=True)  12.9 us
    cos x2, local copies, waits for them, and re-layouts, per_device(): trans_real = jnp.cos(full_slice)  9.32 us
  transfers between devices with their start and end apart: 3, of which 2 were waited for; matrix products, arithmetic and copies ran while one was open for 46% of the time, Pallas kernels for 0%

commit v1 on v0

v1 whole, which is shorter than its diff:
```python
import jax
import jax.numpy as jnp
import numpy as np
from jax import lax
from jax.sharding import PartitionSpec as P

CROP = 256
TILE = 128
MAX_TILT = 16

PRECISE = lax.Precision.HIGH


def half_turn_fit():
    nodes = 0.25 * (0.5 + 0.5 * np.cos(np.pi * (np.arange(64) + 0.5) / 64))
    root = np.sqrt(nodes)
    sine = np.polynomial.chebyshev.Chebyshev.fit(nodes, np.sin(np.pi * root) / root, 5, domain=[0, 0.25])
    cosine = np.polynomial.chebyshev.Chebyshev.fit(nodes, np.cos(np.pi * root), 5, domain=[0, 0.25])
    power = np.polynomial.Polynomial
    return (
        [float(c) for c in sine.convert(kind=power).coef],
        [float(c) for c in cosine.convert(kind=power).coef],
    )


SIN_FIT, COS_FIT = half_turn_fit()


def horner(coefs, value):
    total = coefs[-1]
    for coef in coefs[-2::-1]:
        total = total * value + coef
    return total


def cis_turns(turns):
    part = turns - jnp.round(turns)
    square = part * part
    sine = part * horner(SIN_FIT, square)
    cosine = horner(COS_FIT, square)
    return 1.0 - 2.0 * sine * sine, 2.0 * sine * cosine


def cis_index(index, period):
    return cis_turns(jnp.remainder(index, period).astype(jnp.float32) * (1.0 / period))


def mul(a, b):
    return a[0] * b[0] - a[1] * b[1], a[0] * b[1] + a[1] * b[0]


def dot(left, right):
    return jnp.dot(left, right, precision=PRECISE, preferred_element_type=jnp.float32)


def times_table(field, table):
    m, n = field[0].shape[0], table[0].shape[1]
    both = dot(jnp.concatenate(field, 0), jnp.concatenate(table, 1))
    return both[:m, :n] - both[m:, n:], both[:m, n:] + both[m:, :n]


def per_device(potential, beam_tilts, aperture, aberration, probe_spots, crop_anchor, *, devices):
    layer_count, rows, length = potential.shape
    beam_count = beam_tilts.shape[0]
    per_side = CROP // TILE
    tile_count = per_side * per_side
    group = devices // tile_count
    own_beams = beam_count // group
    out_rows = tile_count * TILE // devices
    span = group * rows
    device = lax.axis_index("beam")
    my_tile = device // group
    member = device % group

    def swap(value, bits):
        return lax.ppermute(value, "beam", [(i, i ^ bits) for i in range(devices)])

    parts = length // TILE
    part_rows = rows // parts
    window = lax.dynamic_slice(potential[1], (0, crop_anchor[1]), (rows, CROP))

    def piece_for(tile):
        piece = jnp.where(tile % per_side == 0, window[:, :TILE], window[:, TILE:])
        return jnp.concatenate([piece[q * part_rows:(q + 1) * part_rows] for q in range(parts)], 1)

    def unpack(piece):
        return jnp.concatenate([piece[:, q * TILE:(q + 1) * TILE] for q in range(parts)], 0)

    blocks = [potential[0]]
    pieces = [unpack(piece_for(my_tile))]
    for shift in range(1, tile_count):
        sent = jnp.concatenate((potential[0], piece_for(my_tile ^ shift)), 0)
        got = swap(sent, shift * group)
        blocks.append(got[:rows])
        pieces.append(unpack(got[rows:]))
    anchor_row = crop_anchor[0] + TILE * (my_tile // per_side)
    anchor_col = crop_anchor[1] + TILE * (my_tile % per_side)
    inside = jnp.arange(rows, dtype=jnp.int32)
    wanted = (anchor_row + jnp.remainder(rows * member + inside - anchor_row, span)) // span
    slice_one = pieces[0]
    for shift in range(1, tile_count):
        slice_one = jnp.where((wanted == (my_tile ^ shift))[:, None], pieces[shift], slice_one)
    slice_zero = jnp.stack(blocks)[:, None]
    slice_one = slice_one[None]
    bits = group // 2
    bit_order = []
    while bits >= 1:
        count = slice_zero.shape[1]
        packed = jnp.concatenate(
            (
                slice_zero.reshape(tile_count * count * rows, length),
                jnp.concatenate(
                    [slice_one[:, q * part_rows:(q + 1) * part_rows] for q in range(parts)], 2
                ).reshape(count * part_rows, length),
            ),
            0,
        )
        got = swap(packed, bits)
        other_zero = got[: tile_count * count * rows].reshape(slice_zero.shape)
        other_one = got[tile_count * count * rows:].reshape(count, part_rows, length)
        other_one = jnp.concatenate(
            [other_one[:, :, q * TILE:(q + 1) * TILE] for q in range(parts)], 1
        )
        slice_zero = jnp.concatenate((slice_zero, other_zero), 1)
        slice_one = jnp.concatenate((slice_one, other_one), 0)
        bit_order = bit_order + [b ^ bits for b in bit_order] if bit_order else [0, bits]
        bits //= 2
    if not bit_order:
        bit_order = [0]
    offsets = jnp.asarray(np.array(bit_order, np.int32))
    member_of = member ^ offsets
    half_tiles = tile_count // 2
    slot_tile = my_tile ^ jnp.arange(half_tiles, dtype=jnp.int32)
    grid_row = (
        span * slot_tile[:, None, None] + rows * member_of[None, :, None] + inside[None, None, :]
    ).reshape(length // 2)

    half = length // 2
    kept = (length // 3 + MAX_TILT) // 64 * 64
    if kept < length // 3 + MAX_TILT:
        kept += 64
    kept = min(kept, half)
    base = jnp.arange(kept, dtype=jnp.int32) - kept // 2
    freqs = jnp.concatenate((2 * base, 2 * base + 1))
    wave = cis_turns(slice_zero.reshape(2, half, length) * (0.5 / np.pi))

    def fold(value):
        rows_even, rows_odd = value[0] + value[1], value[0] - value[1]
        stack = jnp.concatenate((rows_even, rows_odd), 0)
        return stack[:, :half] + stack[:, half:], stack[:, :half] - stack[:, half:]

    real_fold, imag_fold = fold(wave[0]), fold(wave[1])
    cols = jnp.arange(half, dtype=jnp.int32)
    spread = []
    for parity in range(2):
        table = cis_index(-cols[:, None] * (2 * base + parity)[None, :], length)
        spread.append(times_table((real_fold[parity], imag_fold[parity]), table))
    spread = [jnp.concatenate((spread[0][c], spread[1][c]), 1) for c in range(2)]
    spectrum = []
    for parity in range(2):
        table = cis_index(-(2 * base + parity)[:, None] * grid_row[None, :], length)
        rows_of = slice(parity * half, (parity + 1) * half)
        spectrum.append(times_table(table, (spread[0][rows_of], spread[1][rows_of])))
    spectrum = [jnp.concatenate((spectrum[0][c], spectrum[1][c]), 0) for c in range(2)]

    tilts = lax.dynamic_slice_in_dim(beam_tilts, member * own_beams, own_beams, 0)
    tile_rows = jnp.remainder((rows * member_of[:, None] + inside[None, :]).reshape(TILE) - anchor_row, span)
    spots_y = anchor_row + tile_rows
    offs_x = jnp.arange(TILE, dtype=jnp.int32)
    spots_x = anchor_col + offs_x
    one = cis_turns(slice_one.reshape(TILE, TILE) * (0.5 / np.pi))
    out_freq = jnp.arange(TILE, dtype=jnp.int32)
    last_x = cis_index(-offs_x[:, None] * out_freq[None, :], TILE)
    last_y = cis_index(-out_freq[:, None] * tile_rows[None, :], TILE)
    scale = 1.0 / (length * length)
    finished = []
    for b in range(own_beams):
        ky = freqs + tilts[b, 0]
        kx = freqs + tilts[b, 1]
        passing = 9 * (ky[:, None] ** 2 + kx[None, :] ** 2) < length * length
        masked = (jnp.where(passing, spectrum[0], 0.0), jnp.where(passing, spectrum[1], 0.0))
        left = cis_index(2 * ky[None, :] * spots_y[:, None] - (ky * ky)[None, :], 2 * length)
        right = cis_index(2 * kx[:, None] * spots_x[None, :] - (kx * kx)[:, None], 2 * length)
        left = (left[0] * scale, left[1] * scale)
        field = times_table(left, masked)
        field = times_table(field, right)
        field = mul(field, one)
        field = times_table(field, last_x)
        field = times_table(last_y, field)
        finished.append(jnp.stack(field))
    finished = jnp.stack(finished).reshape(own_beams * 2, TILE // out_rows, out_rows, TILE)
    finished = finished.transpose(1, 2, 0, 3)

    arrived = []
    for other in range(group):
        block = lax.dynamic_slice_in_dim(finished, member ^ other, 1, 0)[0]
        arrived.append(block if other == 0 else swap(block, other))
    arrived = jnp.concatenate(arrived, 1)
    order = (member ^ np.arange(group, dtype=np.int32))
    pick = (order[:, None] * own_beams + jnp.arange(own_beams, dtype=jnp.int32)[None, :]).reshape(beam_count)
    chosen = pick[:, None] == jnp.arange(beam_count, dtype=jnp.int32)[None, :]
    tilt_y = jnp.sum(jnp.where(chosen, beam_tilts[None, :, 0], 0), 1)
    tilt_x = jnp.sum(jnp.where(chosen, beam_tilts[None, :, 1], 0), 1)
    amplitude = jnp.sum(jnp.where(chosen, aperture[None, :], 0.0), 1)
    phase = jnp.sum(jnp.where(chosen, aberration[None, :], 0.0), 1)
    probe_here = lax.dynamic_slice_in_dim(probe_spots, my_tile, 1, 0)[0]
    spot_rows = anchor_row + probe_here[:, 0]
    spot_cols = anchor_col + probe_here[:, 1]
    index = jnp.remainder(
        spot_rows[:, None] * tilt_y[None, :] + spot_cols[:, None] * tilt_x[None, :], length
    )
    weight = cis_turns(phase[None, :] * (0.5 / np.pi) - index.astype(jnp.float32) * (1.0 / length))
    weight_real, weight_imag = amplitude[None, :] * weight[0], amplitude[None, :] * weight[1]
    probes = weight_real.shape[0]
    to_real = jnp.stack((weight_real, -weight_imag), 2).reshape(probes, 2 * beam_count)
    to_imag = jnp.stack((weight_imag, weight_real), 2).reshape(probes, 2 * beam_count)
    weights = jnp.concatenate((to_real, to_imag), 0)
    exits = jnp.einsum("pb,ybk->ypk", weights, arrived, precision=PRECISE)
    intensity = exits[:, :probes] ** 2 + exits[:, probes:] ** 2
    total = jnp.sum(intensity, (0, 2))[None, :]
    bits = 1
    while bits < group:
        total = total + swap(total, bits)
        bits *= 2
    level = total[0] / (TILE * TILE)
    return intensity / (level[None, :, None] + 1e-06)


def solution(mesh):
    placed = (P("groups", "beam", None), P(), P(), P(), P("groups", None, None), P("groups"))

    def body(*args):
        return per_device(*args, devices=mesh.shape["beam"])

    return jax.shard_map(
        body,
        mesh=mesh,
        in_specs=placed,
        out_specs=P(("groups", "beam"), None, None),
        check_vma=False,
    )
```

time: 226 us -> 64.9 us (0.29); the launches traced: 222 us -> 64.5 us
  matrix products: 82.3 us -> 11 us
  blocking collectives: 32.3 us -> 0 us
  waiting for transfers between devices: 46.7 us -> 15 us
  local copies, waits for them, and re-layouts: 28.8 us -> 3.89 us
  between operations: 19.3 us -> 4.1 us
  other arithmetic: 9.01 us -> 19 us
  starting transfers between devices: 3.99 us -> 11.6 us
    dot_general x44 -> x21, matrix products: 82.3 us -> 11 us  [the longest x20 10.3 us: dot(): jnp.dot(left, right, precision=PRECISE, preferred_element_type=jnp.float32)]
    all_gather x2 -> x0, waiting for transfers between devices: 33.1 us -> none  [per_device(): lax.all_gather(potential[layer_index], 'beam', axis=0, tiled=True)]
    psum x1 -> x0, blocking collectives: 32.3 us -> none  [per_device(): totals = lax.psum(tile_slots, 'beam')]
    ppermute x0 -> x10, waiting for transfers between devices: none -> 15 us  [swap(): return lax.ppermute(value, 'beam', [(i, i ^ bits) for i in range(devices)])]
    all_to_all x1 -> x0, waiting for transfers between devices: 12.9 us -> none  [per_device(): lax.all_to_all(payload, 'beam', split_axis=2, concat_axis=1, tiled=True)]
    ppermute x0 -> x10, starting transfers between devices: none -> 11.6 us  [swap(): return lax.ppermute(value, 'beam', [(i, i ^ bits) for i in range(devices)])]
    mul x5 -> x11, other arithmetic: 1.38 us -> 10.9 us  [the longest x2 5.76 us: per_device(): 2 * kx[:, None] * spots_x[None, :] - (kx * kx)[:, None]]
    cos x3 -> x0, local copies, waits for them, and re-layouts: 9.4 us -> none  [the longest x2 9.32 us: per_device(): trans_real = jnp.cos(full_slice)]
  transfers between devices with their start and end apart: 3 -> 10, of which waited for: 2 -> 6; matrix products, arithmetic and copies ran while one was open for 46% -> 24% of each run, Pallas kernels for 0% -> 0%
where the time goes in v1:
time: 64.9 us; the launch traced here: 64.5 us
  other arithmetic  19 us (29%)
  waiting for transfers between devices  15 us (23%)
  starting transfers between devices  11.6 us (18%)
  matrix products  11 us (17%)
  between operations  4.1 us (6%)
  local copies, waits for them, and re-layouts  3.89 us (6%)
    ppermute x10, waiting for transfers between devices, swap(): return lax.ppermute(value, 'beam', [(i, i ^ bits) for i in range(devices)])  15 us
    ppermute x10, starting transfers between devices, swap(): return lax.ppermute(value, 'beam', [(i, i ^ bits) for i in range(devices)])  11.6 us
    dot_general x20, matrix products, dot(): jnp.dot(left, right, precision=PRECISE, preferred_element_type=jnp.float32)  10.3 us
    mul x2, other arithmetic, per_device(): 2 * kx[:, None] * spots_x[None, :] - (kx * kx)[:, None]  5.76 us
    sub x5, other arithmetic, cis_turns(): return (1.0 - 2.0 * sine * sine, 2.0 * sine * cosine)  3.62 us
    mul x1, other arithmetic, per_device(): 2 * ky[None, :] * spots_y[:, None] - (ky * ky)[None, :]  3.13 us
    slice x1, local copies, waits for them, and re-layouts, per_device(): anchor_row = crop_anchor[0] + TILE * (my_tile // per_side)  1.38 us
  transfers between devices with their start and end apart: 10, of which 6 were waited for; matrix products, arithmetic and copies ran while one was open for 24% of the time, Pallas kernels for 0%

profile of v1, /device:TPU:0, one launch (start us, length us, event | category | flops | bytes accessed | tf_op | source)
XLA Modules:
  0.0 64.5 jit_solution(14041310679920483265)
XLA Ops:
  0.1 1.4 %fusion.321 = (s32[1]{0:T(128)}, s32[1]{0:T(128)}) fusion(s32[2]{0:T(128)} %param.13), kind=kLoop, calls=%fused_computation.668 | loop fusion | bytes 16 | tf_op jit(solution)/shard_map/slice | solution.py:96
  2.7 0.9 %fusion.309 = (f32[1,32,512]{2,1,0:T(8,128)S(1)}, f32[32,512]{1,0:T(8,128)S(1)}, f32[1,32,512]{2,1,0:T(8,128)S(1)}) fusion(f32[2,32,512]{2,1,0:T(8,128)} %param.8), kind=kLoop, calls=%fused_computation.656 | loop fusion | bytes 327680 | tf_op jit(solution)/shard_map/slice | solution.py:89
  4.4 5.2 %collective-permute-start.2 = (f32[40,512]{1,0:T(8,128)S(1)}, f32[40,512]{1,0:T(8,128)S(1)}, u32[]{:S(2)}, u32[]{:S(2)}) collective-permute-start(f32[40,512]{1,0:T(8,128)S(1)} %get-tuple-element.96), channel_id=1, source_target_pairs={{0,12},{1,13},{2,14},{3,15},{4,8},{5,9},{6,10},{7,11},{8,4},{9,5},... | collective-permute-start | bytes 245768 | tf_op jit(solution)/shard_map/ppermute | solution.py:76
  9.6 0.6 collective-permute-start
  10.3 0.7 %xor_multiply_fusion = (s32[4]{0:T(128)S(1)}, s32[4]{0:T(128)S(1)}) fusion(s32[]{:T(128)S(6)} %select_n.274, s32[4]{0:T(128)} %constant.353.clone), kind=kLoop, calls=%fused_computation.617 | loop fusion | flops 16 | bytes 52 | tf_op jit(solution)/shard_map/mul | solution.py:200
  11.9 0.7 %fusion.320 = (s32[1,1]{0,1:T(1,128)}, s32[1,1]{0,1:T(1,128)}, s32[1,1]{0,1:T(1,128)}, s32[1,1]{0,1:T(1,128)}, s32[1,1]{0,1:T(1,128)}, /*index=5*/s32[1,1]{0,1:T(1,128)}, s32[1,1]{0,1:T(1,128)}, s32[1,1]{0,1:T(1,128)}) fusion(s32[4,2]{0,1:T(2,128)S(1)} %constant_dynamic-slice_fusion.5), kind=kLoop, calls=%fused_computation.667 | loop fusion | bytes 64 | tf_op jit(solution)/shard_map/slice | solution.py:178
  13.5 0.1 add.1733
  13.5 0.6 fusion.113
  14.2 2.0 %add_multiply_fusion.25 = (s32[384]{0:T(512)S(1)}, s32[384]{0:T(512)S(1)}, s32[384]{0:T(512)S(1)}) fusion(s32[]{:T(128)} %bitcast.29, s32[192]{0:T(256)S(1)} %get-tuple-element.216, s32[192]{0:T(256)S(1)} %get-tuple-element.215, s32[]{:T(128)} %bitcast.33, s32[]{:T(128)} %bitcast.28), kind=kLoop, calls=%fused_computation.589 | loop fusion | flops 2688 | bytes 6156 | tf_op jit(solution)/shard_map/mul | solution.py:183
  16.2 3.8 %add_multiply_fusion.29 = (s32[384]{0:T(512)S(1)}, s32[384]{0:T(512)S(1)}, s32[384]{0:T(512)S(1)}, s32[384]{0:T(512)S(1)}, s32[384]{0:T(512)S(1)}, /*index=5*/s32[384]{0:T(512)S(1)}) fusion(s32[]{:T(128)} %bitcast.2, s32[192]{0:T(256)S(1)} %get-tuple-element.216, s32[192]{0:T(256)S(1)} %get-tuple-element.215, s32[]{:T(128)} %bitcast.28, s32[]{:T(128)} %bitcast.29, ...), kind=kLoop, calls=%fused_computation.593 | loop fusion | flops 4992 | bytes 10776 | tf_op jit(solution)/shard_map/mul | solution.py:183
  19.9 3.1 %add_multiply_fusion.32 = (s32[384]{0:T(512)S(1)}, s32[384]{0:T(512)S(1)}, s32[384]{0:T(512)S(1)}, s32[384]{0:T(512)S(1)}, s32[384]{0:T(512)S(1)}, /*index=5*/s32[384]{0:T(512)S(1)}, s32[384]{0:T(512)S(1)}) fusion(s32[]{:T(128)} %bitcast.1, s32[192]{0:T(256)S(1)} %get-tuple-element.216, s32[192]{0:T(256)S(1)} %get-tuple-element.215, s32[]{:T(128)} %bitcast.2, ...), kind=kLoop, calls=%fused_computation.596 | loop fusion | flops 4992 | bytes 12308 | tf_op jit(solution)/shard_map/mul | solution.py:182
  23.1 0.3 fusion.238
  23.3 0.2 select_reduce_fusion.1
  23.5 0.2 select_reduce_fusion.3
  23.7 1.2 %fusion.116 = (f32[384,128]{1,0:T(8,128)S(1)}, f32[384,128]{1,0:T(8,128)S(1)}, f32[384,128]{1,0:T(8,128)S(1)}, f32[384,128]{1,0:T(8,128)S(1)}, f32[384,128]{1,0:...) fusion(s32[384]{0:T(512)S(1)} %get-tuple-element.156, ...), kind=kLoop, calls=%fused_computation.242 | loop fusion | flops 8454144 | bytes 1585664 | tf_op jit(solution)/shard_map/sub | solution.py:41
  25.0 0.1 fusion.267
  25.2 1.7 %collective-permute-start.3 = (f32[136,512]{1,0:T(8,128)S(1)}, f32[136,512]{1,0:T(8,128)S(1)}, u32[]{:S(2)}, u32[]{:S(2)}) collective-permute-start(f32[136,512]{1,0:T(8,128)S(1)} %pad_maximum_fusion.10), channel_id=1, source_target_pairs={{0,2},{1,3},{2,0},{3,1},{4,6},{5,7},{6,4},{7,5},{8,10},{9,11},{10,... | collective-permute-start | bytes 835592 | tf_op jit(solution)/shard_map/ppermute | solution.py:76
  27.0 0.6 fusion.112
  27.6 5.5 %collective-permute-done.3 = f32[136,512]{1,0:T(8,128)S(1)} collective-permute-done((f32[136,512]{1,0:T(8,128)S(1)}, f32[136,512]{1,0:T(8,128)S(1)}, u32[]{:S(2)}, u32[]{:S(2)}) %collective-permute-start.3) | collective-permute-done | bytes 278560 | tf_op jit(solution)/shard_map/ppermute | solution.py:76
  33.4 1.2 %fusion.110 = (f32[128,384]{1,0:T(8,128)S(1)}, f32[128,384]{1,0:T(8,128)S(1)}, f32[128,384]{1,0:T(8,128)S(1)}, f32[128,384]{1,0:T(8,128)S(1)}, f32[128,384]{1,0:...) fusion(s32[384]{0:T(512)S(1)} %get-tuple-element.161, ...), kind=kLoop, calls=%fused_computation.236 | loop fusion | flops 8847360 | bytes 1585664 | tf_op jit(solution)/shard_map/mul | solution.py:184
  34.6 0.7 %collective-permute-done.4 = f32[272,512]{1,0:T(8,128)S(1)} collective-permute-done((f32[272,512]{1,0:T(8,128)S(1)}, f32[272,512]{1,0:T(8,128)S(1)}, u32[]{:S(2)}, u32[]{:S(2)}) %collective-permute-start.4) | collective-permute-done | bytes 557088 | tf_op jit(solution)/shard_map/ppermute | solution.py:76
  35.4 0.1 maximum_multiply_fusion
  35.5 1.0 %fusion.16 = (f32[2,256,512]{2,1,0:T(8,128)S(1)}, f32[2,256,512]{2,1,0:T(8,128)S(1)}) fusion(f32[2,256,512]{2,1,0:T(8,128)S(1)} %bitcast.153), kind=kLoop, calls=%fused_computation.20 | loop fusion | flops 7340032 | bytes 3145728 | tf_op jit(solution)/shard_map/sub | solution.py:41
  36.4 0.1 add_bitcast_fusion.1
  36.5 0.1 add_bitcast_fusion
  36.8 0.8 %fusion.17 = f32[1024,384]{0,1:T(8,128)S(1)} fusion(f32[512,256]{1,0:T(8,128)S(1)} %get-tuple-element.21, f32[512,256]{1,0:T(8,128)S(1)} %get-tuple-element.19, f32[256,192]{0,1:T(8,128)S(1)} %get-tuple-element.170, f32[256,192]{0,1:T(8,128)S(1)} %get-tuple-element.169), kind=kOutput, calls=%fused_computation.26 | convolution fusion | flops 604340224 | bytes 3014656 | tf_op jit(solution)/shard_map/dot_general | solution.py:53
  37.6 0.1 slice_subtract_fusion.1
  37.8 0.8 %fusion.21 = f32[1024,384]{0,1:T(8,128)S(1)} fusion(f32[512,256]{1,0:T(8,128)S(1)} %get-tuple-element.22, f32[512,256]{1,0:T(8,128)S(1)} %get-tuple-element.20, f32[256,192]{0,1:T(8,128)S(1)} %get-tuple-element.189, f32[256,192]{0,1:T(8,128)S(1)} %get-tuple-element.190), kind=kOutput, calls=%fused_computation.30 | convolution fusion | flops 604340224 | bytes 3014656 | tf_op jit(solution)/shard_map/dot_general | solution.py:53
  38.6 0.1 slice_subtract_fusion
  38.9 0.7 %fusion.33 = f32[384,768]{1,0:T(8,128)S(1)} fusion(f32[256,384]{0,1:T(8,128)S(1)} %fusion.55, f32[256,384]{0,1:T(8,128)S(1)} %fusion.56, f32[192,256]{1,0:T(8,128)S(1)} %get-tuple-element.166, f32[192,256]{1,0:T(8,128)S(1)} %get-tuple-element.165), kind=kOutput, calls=%fused_computation.51 | convolution fusion | flops 453279744 | bytes 2359296 | tf_op jit(solution)/shard_map/dot_general | solution.py:53
  39.6 0.7 %fusion.29 = f32[384,768]{1,0:T(8,128)S(1)} fusion(f32[512,192]{0,1:T(8,128)S(1)} %get-tuple-element.14, f32[512,192]{0,1:T(8,128)S(1)} %get-tuple-element.12, f32[512,192]{0,1:T(8,128)S(1)} %get-tuple-element.13, f32[512,192]{0,1:T(8,128)S(1)} %get-tuple-element.11, f32[192,256]{1,0:T(8,128)S(1)} %get-tuple-element.187, f32[192,256]{1,0:T(8,128)S(1)} %get-tuple-element.188), kind=kOutput, calls=%fused_computation.43 | convolution fusion | flops 453672960 | bytes 3145728 | tf_op jit(solution)/shard_map/dot_general | solution.py:53
  40.3 0.4 fusion.48
  40.7 0.4 fusion.47
  41.1 0.8 %fusion.4 = f32[256,768]{1,0:T(8,128)S(1)} fusion(f32[384,384]{1,0:T(8,128)S(1)} %get-tuple-element.42, f32[384,384]{1,0:T(8,128)S(1)} %get-tuple-element.38, f32[128,384]{1,0:T(8,128)S(1)} %get-tuple-element.201, f32[128,384]{1,0:T(8,128)S(1)} %get-tuple-element.202), kind=kOutput, calls=%fused_computation.8 | convolution fusion | flops 453378048 | bytes 2359296 | tf_op jit(solution)/shard_map/dot_general | solution.py:53
  42.0 1.0 %fusion = f32[256,768]{1,0:T(8,128)S(1)} fusion(f32[384,384]{1,0:T(8,128)S(1)} %get-tuple-element.41, f32[384,384]{1,0:T(8,128)S(1)} %get-tuple-element.37, f32[128,384]{1,0:T(8,128)S(1)} %get-tuple-element.133, f32[128,384]{1,0:T(8,128)S(1)} %get-tuple-element.132), kind=kOutput, calls=%fused_computation.4 | convolution fusion | flops 453378048 | bytes 2359296 | tf_op jit(solution)/shard_map/dot_general | solution.py:53
  43.1 0.4 fusion.82
  43.5 0.4 fusion.72
  43.9 0.1 multiply_subtract_fusion.3
  44.0 0.3 fusion.205
  44.3 0.3 fusion.209
  44.6 0.3 fusion.213
  45.0 0.3 fusion.217
  45.3 0.8 %fusion.12 = f32[256,768]{1,0:T(8,128)S(1)} fusion(f32[384,384]{1,0:T(8,128)S(1)} %get-tuple-element.44, f32[384,384]{1,0:T(8,128)S(1)} %get-tuple-element.40, f32[128,384]{1,0:T(8,128)S(1)} %get-tuple-element.197, f32[128,384]{1,0:T(8,128)S(1)} %get-tuple-element.198), kind=kOutput, calls=%fused_computation.16 | convolution fusion | flops 453378048 | bytes 2359296 | tf_op jit(solution)/shard_map/dot_general | solution.py:53
  46.1 0.8 %fusion.8 = f32[256,768]{1,0:T(8,128)S(1)} fusion(f32[384,384]{1,0:T(8,128)S(1)} %get-tuple-element.43, f32[384,384]{1,0:T(8,128)S(1)} %get-tuple-element.39, f32[128,384]{1,0:T(8,128)S(1)} %get-tuple-element.199, f32[128,384]{1,0:T(8,128)S(1)} %get-tuple-element.200), kind=kOutput, calls=%fused_computation.12 | convolution fusion | flops 453378048 | bytes 2359296 | tf_op jit(solution)/shard_map/dot_general | solution.py:53
  47.0 0.4 fusion.102
  47.4 0.4 fusion.92
  47.8 0.1 multiply_subtract_fusion.1
  47.9 0.3 fusion.221
  48.2 0.3 fusion.225
  48.5 0.3 fusion.229
  48.9 0.3 fusion.233
  49.4 0.2 collective-permute-start.5
  49.7 1.6 %collective-permute-start.6 = (f32[32,8,128]{2,1,0:T(8,128)S(1)}, f32[32,8,128]{2,1,0:T(8,128)S(1)}, u32[]{:S(2)}, u32[]{:S(2)}) collective-permute-start(f32[32,8,128]{2,1,0:T(8,128)S(1)} %bitcast.162), channel_id=1, source_target_pairs={{0,2},{1,3},{2,0},{3,1},{4,6},{5,7},{6,4},{7,5},{8,10},{9,11},{10,... | collective-permute-start | bytes 393224 | tf_op jit(solution)/shard_map/ppermute | solution.py:76
  51.3 0.3 collective-permute-start.7
  51.7 0.1 fusion.307
  51.9 4.2 %collective-permute-done.6 = f32[32,8,128]{2,1,0:T(8,128)S(1)} collective-permute-done((f32[32,8,128]{2,1,0:T(8,128)S(1)}, f32[32,8,128]{2,1,0:T(8,128)S(1)}, u32[]{:S(2)}, u32[]{:S(2)}) %collective-permute-start.6) | collective-permute-done | bytes 131104 | tf_op jit(solution)/shard_map/ppermute | solution.py:76
  56.1 1.6 %collective-permute-done.7 = f32[32,8,128]{2,1,0:T(8,128)S(1)} collective-permute-done((f32[32,8,128]{2,1,0:T(8,128)S(1)}, f32[32,8,128]{2,1,0:T(8,128)S(1)}, u32[]{:S(2)}, u32[]{:S(2)}) %collective-permute-start.7) | collective-permute-done | bytes 131104 | tf_op jit(solution)/shard_map/ppermute | solution.py:76
  57.8 0.7 %convolution_bitcast_fusion = f32[32,64,128]{2,1,0:T(8,128)S(1)} fusion(f32[32,8,128]{2,1,0:T(8,128)S(1)} %collective-permute-done.7, f32[32,8,128]{2,1,0:T(8,128)S(1)} %collective-permute-done.6, f32[32,8,128]{2,1,0:T(8,128)S(1)} %collective-permute-done.5, f32[32,8,128]{2,1,0:T(8,128)S(1)} %bitcast.160, f32[32,32]{0,1:T(8,128)S(1)} %bitcast.165, ...), kind=kOutput, calls=%fused_computation.3 | convolution fusion | flops 50726912 | bytes 1581056 | tf_op jit(solution)/shard_map/pb,ybk->ypk/dot_general | solution.py:218
  58.5 0.2 fusion.237
  58.7 0.5 collective-permute-start.8
  59.1 0.8 %collective-permute-done.8 = f32[1,32]{1,0:T(1,128)S(1)} collective-permute-done((f32[1,32]{1,0:T(1,128)S(1)}, f32[1,32]{1,0:T(1,128)S(1)}, u32[]{:S(2)}, u32[]{:S(2)}) %collective-permute-start.8) | collective-permute-done | bytes 160 | tf_op jit(solution)/shard_map/ppermute | solution.py:76
  60.0 1.5 %collective-permute-start.9 = (f32[1,32]{1,0:T(1,128)S(1)}, f32[1,32]{1,0:T(1,128)S(1)}, u32[]{:S(2)}, u32[]{:S(2)}) collective-permute-start(f32[1,32]{1,0:T(1,128)S(1)} %bitcast_add_fusion), channel_id=1, source_target_pairs={{0,2},{1,3},{2,0},{3,1},{4,6},{5,7},{6,4},{7,5},{8,10},{9,11},{10,... | collective-permute-start | bytes 392 | tf_op jit(solution)/shard_map/ppermute | solution.py:76
  61.4 2.1 %collective-permute-done.9 = f32[1,32]{1,0:T(1,128)S(1)} collective-permute-done((f32[1,32]{1,0:T(1,128)S(1)}, f32[1,32]{1,0:T(1,128)S(1)}, u32[]{:S(2)}, u32[]{:S(2)}) %collective-permute-start.9) | collective-permute-done | bytes 160 | tf_op jit(solution)/shard_map/ppermute | solution.py:76
  63.5 1.0 %broadcast_divide_fusion = f32[32,32,128]{2,1,0:T(8,128)} fusion(f32[32]{0:T(128)S(1)} %add_bitcast_fusion.2, f32[32,64,128]{2,1,0:T(8,128)S(1)} %convolution_bitcast_fusion), kind=kLoop, calls=%fused_computation.234 | loop fusion | flops 524288 | bytes 1572992 | tf_op jit(solution)/shard_map/div | solution.py:226
  (94 shorter events, 2.3 us)
Async XLA Ops:
  0.0 13.3 %copy-start = (s32[4,32,2]{1,2,0:T(2,128)S(1)}, s32[4,32,2]{1,2,0:T(2,128)}, u32[]{:S(2)}) copy-start(s32[4,32,2]{1,2,0:T(2,128)} %param.12) | copy-start | bytes 3076
  0.0 11.8 %copy-start.1 = (s32[16,2]{0,1:T(2,128)S(1)}, s32[16,2]{0,1:T(2,128)}, u32[]{:S(2)}) copy-start(s32[16,2]{0,1:T(2,128)} %param.9) | copy-start | bytes 388
  0.0 23.5 %copy-start.2 = (f32[16]{0:T(128)S(1)}, f32[16]{0:T(128)}, u32[]{:S(2)}) copy-start(f32[16]{0:T(128)} %param.10) | copy-start | bytes 196
  0.0 23.5 %copy-start.3 = (f32[16]{0:T(128)S(1)}, f32[16]{0:T(128)}, u32[]{:S(2)}) copy-start(f32[16]{0:T(128)} %param.11) | copy-start | bytes 196
  4.4 20.6 %collective-permute-start.2 = (f32[40,512]{1,0:T(8,128)S(1)}, f32[40,512]{1,0:T(8,128)S(1)}, u32[]{:S(2)}, u32[]{:S(2)}) collective-permute-start(f32[40,512]{1,0:T(8,128)S(1)} %get-tuple-element.96), channel_id=1, source_target_pairs={{0,12},{1,13},{2,14},{3,15},{4,8},{5,9},{6,10},{7,11},{8,4},{9,5},... | collective-permute-start | bytes 245768 | tf_op jit(solution)/shard_map/ppermute | solution.py:76
  9.6 15.4 %collective-permute-start.1 = (f32[40,512]{1,0:T(8,128)S(1)}, f32[40,512]{1,0:T(8,128)S(1)}, u32[]{:S(2)}, u32[]{:S(2)}) collective-permute-start(f32[40,512]{1,0:T(8,128)S(1)} %get-tuple-element.95), channel_id=1, source_target_pairs={{0,8},{1,9},{2,10},{3,11},{4,12},{5,13},{6,14},{7,15},{8,0},{9,1},... | collective-permute-start | bytes 245768 | tf_op jit(solution)/shard_map/ppermute | solution.py:76
  9.6 15.4 %collective-permute-start = (f32[40,512]{1,0:T(8,128)S(1)}, f32[40,512]{1,0:T(8,128)S(1)}, u32[]{:S(2)}, u32[]{:S(2)}) collective-permute-start(f32[40,512]{1,0:T(8,128)S(1)} %get-tuple-element.94), channel_id=1, source_target_pairs={{0,4},{1,5},{2,6},{3,7},{4,0},{5,1},{6,2},{7,3},{8,12},{9,13},{10,... | collective-permute-start | bytes 245768 | tf_op jit(solution)/shard_map/ppermute | solution.py:76
  25.2 7.9 %collective-permute-start.3 = (f32[136,512]{1,0:T(8,128)S(1)}, f32[136,512]{1,0:T(8,128)S(1)}, u32[]{:S(2)}, u32[]{:S(2)}) collective-permute-start(f32[136,512]{1,0:T(8,128)S(1)} %pad_maximum_fusion.10), channel_id=1, source_target_pairs={{0,2},{1,3},{2,0},{3,1},{4,6},{5,7},{6,4},{7,5},{8,10},{9,11},{10,... | collective-permute-start | bytes 835592 | tf_op jit(solution)/shard_map/ppermute | solution.py:76
  33.3 2.0 %collective-permute-start.4 = (f32[272,512]{1,0:T(8,128)S(1)}, f32[272,512]{1,0:T(8,128)S(1)}, u32[]{:S(2)}, u32[]{:S(2)}) collective-permute-start(f32[272,512]{1,0:T(8,128)S(1)} %pad_maximum_fusion.5), channel_id=1, source_target_pairs={{0,1},{1,0},{2,3},{3,2},{4,5},{5,4},{6,7},{7,6},{8,9},{9,8},{10,11... | collective-permute-start | bytes 1671176 | tf_op jit(solution)/shard_map/ppermute | solution.py:76
  49.4 2.5 %collective-permute-start.5 = (f32[32,8,128]{2,1,0:T(8,128)S(1)}, f32[32,8,128]{2,1,0:T(8,128)S(1)}, u32[]{:S(2)}, u32[]{:S(2)}) collective-permute-start(f32[32,8,128]{2,1,0:T(8,128)S(1)} %bitcast.161), channel_id=1, source_target_pairs={{0,1},{1,0},{2,3},{3,2},{4,5},{5,4},{6,7},{7,6},{8,9},{9,8},{10,11... | collective-permute-start | bytes 393224 | tf_op jit(solution)/shard_map/ppermute | solution.py:76
  49.7 6.4 %collective-permute-start.6 = (f32[32,8,128]{2,1,0:T(8,128)S(1)}, f32[32,8,128]{2,1,0:T(8,128)S(1)}, u32[]{:S(2)}, u32[]{:S(2)}) collective-permute-start(f32[32,8,128]{2,1,0:T(8,128)S(1)} %bitcast.162), channel_id=1, source_target_pairs={{0,2},{1,3},{2,0},{3,1},{4,6},{5,7},{6,4},{7,5},{8,10},{9,11},{10,... | collective-permute-start | bytes 393224 | tf_op jit(solution)/shard_map/ppermute | solution.py:76
  51.3 6.4 %collective-permute-start.7 = (f32[32,8,128]{2,1,0:T(8,128)S(1)}, f32[32,8,128]{2,1,0:T(8,128)S(1)}, u32[]{:S(2)}, u32[]{:S(2)}) collective-permute-start(f32[32,8,128]{2,1,0:T(8,128)S(1)} %bitcast.163), channel_id=1, source_target_pairs={{0,3},{1,2},{2,1},{3,0},{4,7},{5,6},{6,5},{7,4},{8,11},{9,10},{10,... | collective-permute-start | bytes 393224 | tf_op jit(solution)/shard_map/ppermute | solution.py:76
  58.7 1.3 %collective-permute-start.8 = (f32[1,32]{1,0:T(1,128)S(1)}, f32[1,32]{1,0:T(1,128)S(1)}, u32[]{:S(2)}, u32[]{:S(2)}) collective-permute-start(f32[1,32]{1,0:T(1,128)S(1)} %bitcast.166), channel_id=1, source_target_pairs={{0,1},{1,0},{2,3},{3,2},{4,5},{5,4},{6,7},{7,6},{8,9},{9,8},{10,11... | collective-permute-start | bytes 392 | tf_op jit(solution)/shard_map/ppermute | solution.py:76
  60.0 3.6 %collective-permute-start.9 = (f32[1,32]{1,0:T(1,128)S(1)}, f32[1,32]{1,0:T(1,128)S(1)}, u32[]{:S(2)}, u32[]{:S(2)}) collective-permute-start(f32[1,32]{1,0:T(1,128)S(1)} %bitcast_add_fusion), channel_id=1, source_target_pairs={{0,2},{1,3},{2,0},{3,1},{4,6},{5,7},{6,4},{7,5},{8,10},{9,11},{10,... | collective-permute-start | bytes 392 | tf_op jit(solution)/shard_map/ppermute | solution.py:76

commit v2 on v1

v2 whole, which is shorter than its diff:
```python
import functools

import jax
import jax.numpy as jnp
import numpy as np
from jax import lax
from jax.experimental import pallas as pl
from jax.experimental.pallas import tpu as pltpu
from jax.sharding import PartitionSpec as P


CROP = 256
TILE = 128
MAX_TILT = 16

VMEM = pl.BlockSpec(memory_space=pltpu.VMEM)
HBM = pl.BlockSpec(memory_space=pltpu.HBM)


def half_turn_fit():
    nodes = 0.25 * (0.5 + 0.5 * np.cos(np.pi * (np.arange(64) + 0.5) / 64))
    root = np.sqrt(nodes)
    fit = np.polynomial.chebyshev.Chebyshev.fit
    sine = fit(nodes, np.sin(np.pi * root) / root, 4, domain=[0, 0.25])
    cosine = fit(nodes, np.cos(np.pi * root), 4, domain=[0, 0.25])
    power = np.polynomial.Polynomial
    return (
        [float(c) for c in sine.convert(kind=power).coef],
        [float(c) for c in cosine.convert(kind=power).coef],
    )


SIN_FIT, COS_FIT = half_turn_fit()


def horner(coefs, value):
    total = coefs[-1]
    for coef in coefs[-2::-1]:
        total = total * value + coef
    return total


def cis_part(part):
    square = part * part
    sine = part * horner(SIN_FIT, square)
    cosine = horner(COS_FIT, square)
    return 1.0 - 2.0 * sine * sine, 2.0 * sine * cosine


def cis_turns(turns):
    return cis_part(turns - jnp.floor(turns + 0.5))


def cis_index(index, period):
    part = ((index + period // 2) & (period - 1)) - period // 2
    return cis_part(part.astype(jnp.float32) * (1.0 / period))


def mul(a, b):
    return a[0] * b[0] - a[1] * b[1], a[0] * b[1] + a[1] * b[0]


def split(value):
    high = value.astype(jnp.bfloat16)
    return high, (value - high.astype(jnp.float32)).astype(jnp.bfloat16)


def dot3(left, right):
    wide = jnp.concatenate((left[0], left[1], left[0]), 1)
    tall = jnp.concatenate((right[0], right[0], right[1]), 0)
    return jnp.dot(wide, tall, preferred_element_type=jnp.float32)


def combine(both, rows, cols):
    return (
        both[:rows, :cols] - both[rows:, cols:],
        both[:rows, cols:] + both[rows:, :cols],
    )


def iota(shape, axis):
    return lax.broadcasted_iota(jnp.int32, shape, axis)


class Sizes:
    def __init__(self, devices, potential, beam_count):
        self.rows, self.length = potential[1], potential[2]
        self.beams = beam_count
        self.per_side = CROP // TILE
        self.tiles = self.per_side * self.per_side
        self.group = devices // self.tiles
        self.own = beam_count // self.group
        self.out_rows = self.tiles * TILE // devices
        self.span = self.group * self.rows
        self.half = self.length // 2
        self.pieces = self.length // TILE
        self.piece_rows = self.rows // self.pieces
        self.block = self.tiles * self.rows + self.piece_rows
        self.kept = min(-(-(self.length // 3 + MAX_TILT) // 64) * 64, self.half)
        self.freqs = 2 * self.kept
        self.chunk = min(self.group, max(1, 128 // (self.rows * self.tiles)))

    def frequency(self, position):
        kept = self.kept
        return jnp.where(position < kept, 2 * position - kept, 2 * (position - kept) - kept + 1)

    def grid_row(self, place, tile, member):
        ordinal = place // (self.rows * self.tiles // 2)
        slot = (place // self.rows) % (self.tiles // 2)
        return (
            self.span * (tile ^ slot)
            + self.rows * (member ^ ordinal)
            + place % self.rows
        )

    def tile_row(self, place, member, anchor_row):
        across = self.group * self.piece_rows
        ordinal = (place % across) // self.piece_rows
        residue = (
            self.rows * (member ^ ordinal)
            + self.piece_rows * (place // across)
            + place % self.piece_rows
        )
        return (residue - anchor_row) & (self.span - 1)

    def anchors(self, anchor_ref):
        device = lax.axis_index("beam").astype(jnp.int32)
        tile, member = device // self.group, device % self.group
        anchor_row = anchor_ref[0] + TILE * (tile // self.per_side)
        anchor_col = anchor_ref[1] + TILE * (tile % self.per_side)
        return tile, member, anchor_row, anchor_col


def put(ref, index, value, row, col):
    high, low = split(value)
    rows, cols = value.shape
    ref[index, 0, row:row + rows, col:col + cols] = high
    ref[index, 1, row:row + rows, col:col + cols] = low


def fetch(pairs, sem_ref):
    copies = [pltpu.make_async_copy(src, dst, sem_ref.at[n]) for n, (src, dst) in enumerate(pairs)]
    for copy in copies:
        copy.start()
    for copy in copies:
        copy.wait()


def pack_kernel(sizes, anchor_hbm, potential_hbm, same_ref, other_ref, anchor_ref, potential_ref, sem_ref):
    fetch(((anchor_hbm, anchor_ref), (potential_hbm, potential_ref)), sem_ref)
    tile = sizes.anchors(anchor_ref)[0]
    window = pltpu.roll(potential_ref[1], sizes.length - anchor_ref[1], 1)
    first, second = window[:, :TILE], window[:, TILE:2 * TILE]
    left = tile % sizes.per_side == 0
    rows, step = sizes.rows, sizes.piece_rows
    for ref, value in ((same_ref, jnp.where(left, first, second)), (other_ref, jnp.where(left, second, first))):
        ref[:rows] = potential_ref[0]
        for q in range(sizes.pieces):
            ref[rows:, q * TILE:(q + 1) * TILE] = value[q * step:(q + 1) * step]


def hold_kernel(sizes, anchor_hbm, *refs):
    got, (out_ref, anchor_ref, sem_ref) = refs[:-3], refs[-3:]
    fetch(((anchor_hbm, anchor_ref),), sem_ref)
    tile, member, anchor_row, _ = sizes.anchors(anchor_ref)
    rows, step = sizes.rows, sizes.piece_rows
    shape = (step, sizes.length)
    inside = step * (iota(shape, 1) // TILE) + iota(shape, 0)
    wanted = (anchor_row + ((rows * member + inside - anchor_row) & (sizes.span - 1))) // sizes.span
    piece = got[0][rows:]
    for shift, ref in enumerate(got):
        out_ref[shift * rows:(shift + 1) * rows] = ref[:rows]
        if shift:
            piece = jnp.where(wanted == (tile ^ shift), ref[rows:], piece)
    out_ref[len(got) * rows:] = piece


def column_tables(sizes):
    def both(angle, valid):
        pair = np.concatenate((np.cos(angle) * valid, np.sin(angle) * valid), 1).astype(np.float32)
        high = pair.astype(jnp.bfloat16)
        return np.stack((high, (pair - high.astype(np.float32)).astype(jnp.bfloat16)))

    half, kept = sizes.half, sizes.kept
    cols = np.arange(half)
    out = []
    for parity in range(2):
        position = cols + parity * (sizes.freqs - half)
        freq = 2 * (position - parity * kept) - kept + parity
        valid = (position < kept) if parity == 0 else (position >= kept)
        turns = (cols[:, None] * freq[None, :]) % sizes.length / sizes.length
        out.append(both(-2 * np.pi * turns, valid[None, :] * 1.0))
    cells = np.arange(TILE)
    last = both(-2 * np.pi * ((cells[:, None] * cells[None, :]) % TILE) / TILE, 1.0)
    return np.stack(out), last[None]


def tables_kernel(sizes, probes, halves, *refs):
    sources, refs = refs[:5], refs[5:]
    (rows_ref, left_ref, right_ref, mask_ref, last_y_ref, weights_ref), refs = refs[:6], refs[6:]
    fetch(tuple(zip(sources, refs[:5])), refs[5])
    anchor_ref, tilts_ref, aperture_ref, aberration_ref, spots_ref = refs[:5]
    tile, member, anchor_row, anchor_col = sizes.anchors(anchor_ref)
    half, kept, freqs, length = sizes.half, sizes.kept, sizes.freqs, sizes.length
    for parity in range(2):
        shape = (kept, half)
        freq = 2 * iota(shape, 0) - kept + parity
        place = sizes.grid_row(iota((1, half), 1), tile, member)
        pair = cis_index(-freq * place, length)
        for part in range(2):
            put(rows_ref, parity, pair[part], part * kept, 0)
    scale = 1.0 / (length * length)
    shape = (TILE, freqs)
    spot_y = anchor_row + sizes.tile_row(iota((TILE, 1), 0), member, anchor_row)
    freq_lane = sizes.frequency(iota((1, freqs), 1))
    freq_row = sizes.frequency(iota((freqs, 1), 0))
    spot_x = anchor_col + iota((1, TILE), 1)
    for b in range(sizes.own):
        beam = member * sizes.own + b
        ky = freq_lane + tilts_ref[0, beam]
        kx = freq_row + tilts_ref[1, beam]
        pair = cis_index(ky * (2 * spot_y - ky), 2 * length)
        for part in range(2):
            put(left_ref, b, pair[part] * scale, part * TILE, 0)
        pair = cis_index(kx * (2 * spot_x - kx), 2 * length)
        for part in range(2):
            put(right_ref, b, pair[part], 0, part * TILE)
        ky = freq_row + tilts_ref[0, beam]
        kx = freq_lane + tilts_ref[1, beam]
        limit = (length * length + 8) // 9
        mask_ref[b] = jnp.where(ky * ky < limit - kx * kx, 1.0, 0.0).astype(jnp.bfloat16)
    shape = (TILE, TILE)
    pair = cis_index(-iota(shape, 0) * sizes.tile_row(iota((1, TILE), 1), member, anchor_row), TILE)
    for part in range(2):
        put(last_y_ref, 0, pair[part], part * TILE, 0)
    some = sizes.own // halves
    lane = iota((1, 2 * sizes.beams), 1)
    beam = (
        (member ^ ((lane // (2 * some)) % sizes.group)) * sizes.own
        + some * (lane // (2 * some * sizes.group))
        + (lane // 2) % some
    )
    tilt_y, tilt_x = jnp.zeros_like(lane), jnp.zeros_like(lane)
    amplitude, phase = jnp.zeros(lane.shape, jnp.float32), jnp.zeros(lane.shape, jnp.float32)
    for b in range(sizes.beams):
        here = beam == b
        tilt_y = jnp.where(here, tilts_ref[0, b], tilt_y)
        tilt_x = jnp.where(here, tilts_ref[1, b], tilt_x)
        amplitude = jnp.where(here, aperture_ref[b], amplitude)
        phase = jnp.where(here, aberration_ref[b], phase)
    spots = jnp.transpose(jnp.concatenate((spots_ref[tile], jnp.zeros((6, probes), jnp.int32)), 0))
    index = (
        (anchor_row + spots[:, 0:1]) * tilt_y + (anchor_col + spots[:, 1:2]) * tilt_x
    ) & (length - 1)
    cosine, sine = cis_turns(phase * (0.5 / np.pi) - index.astype(jnp.float32) * (1.0 / length))
    even = lane % 2 == 0
    weights_ref[:probes] = amplitude * jnp.where(even, cosine, -sine)
    weights_ref[probes:] = amplitude * jnp.where(even, sine, cosine)


def spread_block(sizes, block_refs, cols_ref):
    part = sizes.tiles * sizes.rows // 2
    pairs = len(block_refs) * part
    half = sizes.half
    block = jnp.concatenate([ref[:part] for ref in block_refs] + [ref[part:2 * part] for ref in block_refs], 0)
    pieces = [ref[2 * part:] for ref in block_refs]
    wave = cis_turns(block * (0.5 / np.pi))
    folds = []
    for value in wave:
        even, odd = value[:pairs] + value[pairs:], value[:pairs] - value[pairs:]
        stack = jnp.concatenate((even, odd), 0)
        folds.append((stack[:, :half] + stack[:, half:], stack[:, :half] - stack[:, half:]))
    done = []
    for parity in range(2):
        left = split(jnp.concatenate((folds[0][parity], folds[1][parity]), 0))
        done.append(combine(dot3(left, (cols_ref[parity, 0], cols_ref[parity, 1])), 2 * pairs, half))
    shift = sizes.freqs - half
    out = []
    for c in range(2):
        low, high = done[0][c], done[1][c]
        if shift:
            out.append(jnp.concatenate((low[:, :shift], low[:, shift:] + high[:, :half - shift], high[:, half - shift:]), 1))
        else:
            out.append(low + high)
    return out, pieces


def put_pieces(sizes, ref, first, pieces):
    step = sizes.piece_rows
    for o, piece in enumerate(pieces):
        ref[(first + o) * step:(first + o + 1) * step] = piece


def spread_kernel(sizes, *refs):
    block_refs, (cols_ref, out_ref, pieces_ref) = refs[:-3], refs[-3:]
    done, pieces = spread_block(sizes, block_refs, cols_ref)
    put_pieces(sizes, pieces_ref, 0, pieces)
    pairs = out_ref.shape[2]
    for parity in range(2):
        for c in range(2):
            put(out_ref, parity, done[c][parity * pairs:(parity + 1) * pairs], 0, c * sizes.freqs)


def spectrum_kernel(sizes, earlier, *refs):
    spread_refs, pieces_refs = refs[:earlier], refs[earlier:2 * earlier]
    refs = refs[2 * earlier:]
    block_refs, (cols_ref, rows_ref, out_ref, slice_ref, pieces_ref) = refs[:-5], refs[-5:]
    done, pieces = spread_block(sizes, block_refs, cols_ref)
    start = 0
    for ref in pieces_refs:
        pieces_ref[start:start + ref.shape[0]] = ref[...]
        start += ref.shape[0]
    put_pieces(sizes, pieces_ref, start // sizes.piece_rows, pieces)
    one = cis_turns(pieces_ref[...] * (0.5 / np.pi))
    for c in range(2):
        slice_ref[c] = jnp.concatenate([one[c][:, q * TILE:(q + 1) * TILE] for q in range(sizes.pieces)], 0)
    pairs = done[0].shape[0] // 2
    freqs, kept = sizes.freqs, sizes.kept
    for parity in range(2):
        mine = split(jnp.concatenate([c[parity * pairs:(parity + 1) * pairs] for c in done], 1))
        right = [
            jnp.concatenate([ref[parity, part] for ref in spread_refs] + [mine[part]], 0) for part in range(2)
        ]
        both = dot3((rows_ref[parity, 0], rows_ref[parity, 1]), right)
        pair = combine(both, kept, freqs)
        for c in range(2):
            high, low = split(pair[c])
            out_ref[0, parity * kept:(parity + 1) * kept, c * freqs:(c + 1) * freqs] = high
            out_ref[1, parity * kept:(parity + 1) * kept, c * freqs:(c + 1) * freqs] = low


def beams_kernel(sizes, spectrum_ref, left_ref, right_ref, mask_ref, last_x_ref, last_y_ref, slice_ref, out_ref):
    freqs = sizes.freqs
    mask = jnp.concatenate((mask_ref[0], mask_ref[0]), 1)
    masked = (spectrum_ref[0] * mask, spectrum_ref[1] * mask)
    field = combine(dot3((left_ref[0, 0], left_ref[0, 1]), masked), TILE, freqs)
    field = split(jnp.concatenate(field, 0))
    field = combine(dot3(field, (right_ref[0, 0], right_ref[0, 1])), TILE, TILE)
    field = mul(field, (slice_ref[0], slice_ref[1]))
    field = split(jnp.concatenate(field, 0))
    field = combine(dot3(field, (last_x_ref[0, 0], last_x_ref[0, 1])), TILE, TILE)
    field = split(jnp.concatenate(field, 1))
    field = combine(dot3((last_y_ref[0, 0], last_y_ref[0, 1]), field), TILE, TILE)
    out_ref[0, 0] = field[0]
    out_ref[0, 1] = field[1]


def probes_kernel(sizes, probes, weights_ref, fields_ref, out_ref, sums_ref):
    inner = fields_ref.shape[0] // sizes.out_rows
    high, low = split(weights_ref[...])
    total = jnp.zeros((probes, TILE), jnp.float32)
    for row in range(sizes.out_rows):
        fields = split(fields_ref[pl.ds(row, inner, stride=sizes.out_rows), :])
        both = dot3((high, low), fields)
        intensity = both[:probes] * both[:probes] + both[probes:] * both[probes:]
        out_ref[row] = intensity
        total = total + intensity
    sums_ref[...] = jnp.broadcast_to(jnp.sum(total, 1, keepdims=True), (probes, TILE))


def scale_kernel(intensity_ref, sums_ref, out_ref):
    level = sums_ref[...] * (1.0 / (TILE * TILE)) + 1e-06
    out_ref[...] = intensity_ref[...] / level[None]


def per_device(potential, beam_tilts, aperture, aberration, probe_spots, crop_anchor, *, devices):
    sizes = Sizes(devices, potential.shape, beam_tilts.shape[0])
    rows, length, group, tiles, own = sizes.rows, sizes.length, sizes.group, sizes.tiles, sizes.own
    half, kept, freqs = sizes.half, sizes.kept, sizes.freqs
    member = lax.axis_index("beam").astype(jnp.int32) % group
    probes = probe_spots.shape[1]
    halves = 2 if own % 2 == 0 else 1
    some = own // halves

    def swap(value, bits):
        return lax.ppermute(value, "beam", [(i, i ^ bits) for i in range(devices)])

    def call(kernel, outs, specs, **kwargs):
        return pl.pallas_call(
            kernel,
            out_shape=outs,
            in_specs=specs,
            out_specs=kwargs.pop("out_specs", jax.tree.map(lambda _: VMEM, outs)),
            compiler_params=pltpu.CompilerParams(vmem_limit_bytes=16 << 20),
            **kwargs,
        )

    def half_type(*shape):
        return jax.ShapeDtypeStruct(shape, jnp.bfloat16)

    def full_type(*shape):
        return jax.ShapeDtypeStruct(shape, jnp.float32)

    def estimate(flops, bytes_accessed):
        return pl.CostEstimate(flops=flops, bytes_accessed=bytes_accessed, transcendentals=0)

    same, other_side = call(
        functools.partial(pack_kernel, sizes),
        (full_type(rows + sizes.piece_rows, length),) * 2,
        [HBM, HBM],
        scratch_shapes=[
            pltpu.SMEM(crop_anchor.shape, jnp.int32),
            pltpu.VMEM(potential.shape, jnp.float32),
            pltpu.SemaphoreType.DMA((2,)),
        ],
        cost_estimate=estimate(1 << 16, 1 << 18),
    )(crop_anchor, potential)
    blocks = [same]
    for shift in range(1, tiles):
        sent = same if shift % sizes.per_side == 0 else other_side
        blocks.append(swap(sent, shift * group))
    col_table, last_x = (jnp.asarray(table) for table in column_tables(sizes))
    row_table, left, right, masks, last_y, weights = call(
        functools.partial(tables_kernel, sizes, probes, halves),
        (
            half_type(2, 2, 2 * kept, half),
            half_type(own, 2, 2 * TILE, freqs),
            half_type(own, 2, freqs, 2 * TILE),
            half_type(own, freqs, freqs),
            half_type(1, 2, 2 * TILE, TILE),
            full_type(2 * probes, 2 * sizes.beams),
        ),
        [HBM] * 5,
        scratch_shapes=[
            pltpu.SMEM(crop_anchor.shape, jnp.int32),
            pltpu.SMEM(beam_tilts.shape[::-1], jnp.int32),
            pltpu.SMEM(aperture.shape, jnp.float32),
            pltpu.SMEM(aberration.shape, jnp.float32),
            pltpu.VMEM((tiles, 2, probes), jnp.int32),
            pltpu.SemaphoreType.DMA((5,)),
        ],
        cost_estimate=estimate(1 << 22, 6 << 20),
    )(crop_anchor, beam_tilts.T, aperture, aberration, probe_spots.transpose(0, 2, 1))
    held = call(
        functools.partial(hold_kernel, sizes),
        full_type(sizes.block, length),
        [HBM] + [VMEM] * tiles,
        scratch_shapes=[pltpu.SMEM(crop_anchor.shape, jnp.int32), pltpu.SemaphoreType.DMA((1,))],
        cost_estimate=estimate(1 << 16, 1 << 19),
    )(crop_anchor, *blocks)
    gathered = {0: held}
    for bits in member_steps(group):
        for ordinal in list(gathered):
            gathered[ordinal ^ bits] = swap(gathered[ordinal], bits)
    chunks = [
        [gathered[o] for o in range(low, low + sizes.chunk)] for low in range(0, group, sizes.chunk)
    ]

    spreads, pieces = [], []
    pairs = sizes.chunk * rows * tiles // 2
    for chunk in chunks[:-1]:
        spread, piece = call(
            functools.partial(spread_kernel, sizes),
            (half_type(2, 2, pairs, 2 * freqs), full_type(sizes.chunk * sizes.piece_rows, length)),
            [VMEM] * (sizes.chunk + 1),
            cost_estimate=estimate(pairs * half * half * 48, 2 << 20),
        )(*chunk, col_table)
        spreads.append(spread)
        pieces.append(piece)
    spectrum, slice_one = call(
        functools.partial(spectrum_kernel, sizes, len(spreads)),
        (half_type(2, freqs, 2 * freqs), full_type(2, TILE, TILE)),
        [VMEM] * (2 * len(spreads) + sizes.chunk + 2),
        cost_estimate=estimate(3 << 30, 4 << 20),
        scratch_shapes=[pltpu.VMEM((group * sizes.piece_rows, length), jnp.float32)],
    )(*spreads, *pieces, *chunks[-1], col_table, row_table)

    arrived = []
    for h in range(halves):
        table = lambda *shape: pl.BlockSpec((1,) + shape, lambda i: (h * some + i, 0, 0, 0))
        whole = lambda *shape: pl.BlockSpec(shape, lambda i: (0,) * len(shape))
        fields = call(
            functools.partial(beams_kernel, sizes),
            full_type(some, 2, TILE, TILE),
            [
                whole(2, freqs, 2 * freqs),
                table(2, 2 * TILE, freqs),
                table(2, freqs, 2 * TILE),
                pl.BlockSpec((1, freqs, freqs), lambda i: (h * some + i, 0, 0)),
                whole(1, 2, TILE, 2 * TILE),
                whole(1, 2, 2 * TILE, TILE),
                whole(2, TILE, TILE),
            ],
            grid=(some,),
            out_specs=pl.BlockSpec((1, 2, TILE, TILE), lambda i: (i, 0, 0, 0)),
            cost_estimate=pl.CostEstimate(flops=some << 30, bytes_accessed=4 << 20, transcendentals=0),
        )(spectrum, left, right, masks, last_x, last_y, slice_one)
        fields = fields.reshape(2 * some, TILE, TILE)
        for other in range(group):
            start = (member ^ other) * sizes.out_rows
            block = lax.dynamic_slice_in_dim(fields, start, sizes.out_rows, 1)
            arrived.append(block if other == 0 else swap(block, other))
    arrived = jnp.concatenate(arrived, 0).reshape(2 * sizes.beams * sizes.out_rows, TILE)

    intensity, total = call(
        functools.partial(probes_kernel, sizes, probes),
        (full_type(sizes.out_rows, probes, TILE), full_type(probes, TILE)),
        [VMEM, VMEM],
        cost_estimate=pl.CostEstimate(flops=1 << 26, bytes_accessed=2 << 20, transcendentals=0),
    )(weights, arrived)
    bits = 1
    while bits < group:
        total = total + swap(total, bits)
        bits *= 2
    return call(
        scale_kernel,
        full_type(sizes.out_rows, probes, TILE),
        [VMEM, VMEM],
        cost_estimate=pl.CostEstimate(flops=1 << 18, bytes_accessed=1 << 20, transcendentals=0),
    )(intensity, total)


def member_steps(group):
    return [group >> (i + 1) for i in range(group.bit_length() - 1)]


def solution(mesh):
    placed = (P("groups", "beam", None), P(), P(), P(), P("groups", None, None), P("groups"))

    devices = mesh.shape["beam"]

    def body(*args):
        return per_device(*args, devices=devices)

    return jax.shard_map(
        body,
        mesh=mesh,
        in_specs=placed,
        out_specs=P(("groups", "beam"), None, None),
        check_vma=False,
    )
```

time: 64.9 us -> 61.6 us (0.949)
  other arithmetic: 19 us -> 0.01 us
  Pallas kernels: 0 us -> 18.7 us
  matrix products: 11 us -> 0 us
  waiting for transfers between devices: 15 us -> 23.3 us
  between operations: 4.1 us -> 0.15 us
  local copies, waits for them, and re-layouts: 3.89 us -> 6.59 us
  starting transfers between devices: 11.6 us -> 12.5 us
    pallas_call x0 -> x11, Pallas kernels: none -> 18.7 us  [the longest x2 7.1 us: per_device(): call(functools.partial(beams_kernel, sizes), full_type(some, 2, TILE, TIL...]
    dot_general x21 -> x0, matrix products: 11 us -> none  [the longest x20 10.3 us: dot(): jnp.dot(left, right, precision=PRECISE, preferred_element_type=jnp.float32)]
    mul x11 -> x0, other arithmetic: 10.9 us -> none  [the longest x2 5.76 us: per_device(): 2 * kx[:, None] * spots_x[None, :] - (kx * kx)[:, None]]
    ppermute x10 -> x14, waiting for transfers between devices: 15 us -> 23.3 us  [swap(): return lax.ppermute(value, 'beam', [(i, i ^ bits) for i in range(devices)])]
    unnamed x12 -> x25, local copies, waits for them, and re-layouts: 0.34 us -> 6.53 us
    sub x20 -> x0, other arithmetic: 4.54 us -> none  [the longest x5 3.62 us: cis_turns(): return (1.0 - 2.0 * sine * sine, 2.0 * sine * cosine)]
    slice x14 -> x0, local copies, waits for them, and re-layouts: 3.05 us -> none  [the longest x1 1.38 us: per_device(): anchor_row = crop_anchor[0] + TILE * (my_tile // per_side)]
    div x1 -> x0, other arithmetic: 0.95 us -> none  [per_device(): return intensity / (level[None, :, None] + 1e-06)]
  transfers between devices with their start and end apart: 10 -> 14, of which waited for: 6 -> 8; matrix products, arithmetic and copies ran while one was open for 24% -> 0% of each run, Pallas kernels for 0% -> 17%
where the time goes in v2:
time: 61.6 us; the launch traced here: 61.3 us
  waiting for transfers between devices  23.3 us (38%)
  Pallas kernels  18.7 us (30%)
  starting transfers between devices  12.5 us (20%)
  local copies, waits for them, and re-layouts  6.59 us (11%)
    ppermute x14, waiting for transfers between devices, swap(): return lax.ppermute(value, 'beam', [(i, i ^ bits) for i in range(devices)])  23.3 us
    ppermute x14, starting transfers between devices, swap(): return lax.ppermute(value, 'beam', [(i, i ^ bits) for i in range(devices)])  12.5 us
    pallas_call x2, Pallas kernels, per_device(): call(functools.partial(beams_kernel, sizes), full_type(some, 2, TILE, TIL...  7.1 us
    unnamed x25, local copies, waits for them, and re-layouts  6.53 us
    pallas_call x1, Pallas kernels, per_device(): call(functools.partial(tables_kernel, sizes, probes, halves), (half_type(...  4.56 us
    pallas_call x3, Pallas kernels, per_device(): call(functools.partial(spread_kernel, sizes), (half_type(2, 2, pairs, 2 *...  2.49 us
    pallas_call x1, Pallas kernels, per_device(): call(functools.partial(spectrum_kernel, sizes, len(spreads)), (half_type(...  1.89 us
  transfers between devices with their start and end apart: 14, of which 8 were waited for; matrix products, arithmetic and copies ran while one was open for 0% of the time, Pallas kernels for 17%

profile of v2, /device:TPU:0, one launch (start us, length us, event | category | flops | bytes accessed | tf_op | source)
XLA Modules:
  0.0 61.3 jit_solution(3116316975147970869)
XLA Ops:
  0.0 0.0 copy-start.2
  0.0 0.9 %copy-done.2 = f32[2,32,512]{2,1,0:T(8,128)S(1)} copy-done((f32[2,32,512]{2,1,0:T(8,128)S(1)}, f32[2,32,512]{2,1,0:T(8,128)}, u32[]{:S(2)}) %copy-start.2) | copy-done | bytes 131096
  0.9 0.0 copy-start.3
  0.9 0.7 %copy-done.3 = s32[2]{0:T(128)S(1)} copy-done((s32[2]{0:T(128)S(1)}, s32[2]{0:T(128)}, u32[]{:S(2)}) %copy-start.3) | copy-done | bytes 32
  1.6 0.6 %shard_map.83 = (f32[40,512]{1,0:T(8,128)S(1)}, f32[40,512]{1,0:T(8,128)S(1)}) custom-call(s32[2]{0:T(128)S(1)} %copy-done.3, f32[2,32,512]{2,1,0:T(8,128)S(1)} %copy-done.2), custom_call_target="tpu_custom_call" | custom-call | flops 65536 | bytes 262144 | tf_op jit(solution)/shard_map/pallas_call | solution.py:397
  2.2 3.1 %collective-permute-start = (f32[40,512]{1,0:T(8,128)S(1)}, f32[40,512]{1,0:T(8,128)S(1)}, u32[]{:S(2)}, u32[]{:S(2)}) collective-permute-start(f32[40,512]{1,0:T(8,128)S(1)} %get-tuple-element.25), channel_id=1, source_target_pairs={{0,4},{1,5},{2,6},{3,7},{4,0},{5,1},{6,2},{7,3},{8,12},{9,13},{10,... | collective-permute-start | bytes 245768 | tf_op jit(solution)/shard_map/ppermute | solution.py:376
  5.3 2.6 %collective-permute-start.1 = (f32[40,512]{1,0:T(8,128)S(1)}, f32[40,512]{1,0:T(8,128)S(1)}, u32[]{:S(2)}, u32[]{:S(2)}) collective-permute-start(f32[40,512]{1,0:T(8,128)S(1)} %get-tuple-element.24.refs_0_), channel_id=1, source_target_pairs={{0,8},{1,9},{2,10},{3,11},{4,12},{5,13},{6,14},{7,15},{8,0},{9,1},... | collective-permute-start | bytes 245768 | tf_op jit(solution)/shard_map/ppermute | solution.py:376
  7.9 0.0 collective-permute-start.2
  7.9 0.0 collective-permute-done.refs_1_
  7.9 6.6 %collective-permute-done.1.refs_2_ = f32[40,512]{1,0:T(8,128)S(1)} collective-permute-done((f32[40,512]{1,0:T(8,128)S(1)}, f32[40,512]{1,0:T(8,128)S(1)}, u32[]{:S(2)}, u32[]{:S(2)}) %collective-permute-start.1) | collective-permute-done | bytes 81952 | tf_op jit(solution)/shard_map/ppermute | solution.py:376
  14.5 0.0 collective-permute-done.2.refs_3_
  14.5 0.6 shard_map.84.refs_0_
  15.1 1.6 %collective-permute-start.4 = (f32[136,512]{1,0:T(8,128)S(1)}, f32[136,512]{1,0:T(8,128)S(1)}, u32[]{:S(2)}, u32[]{:S(2)}) collective-permute-start(f32[136,512]{1,0:T(8,128)S(1)} %shard_map.84.refs_0_), channel_id=1, source_target_pairs={{0,2},{1,3},{2,0},{3,1},{4,6},{5,7},{6,4},{7,5},{8,10},{9,11},{10,... | collective-permute-start | bytes 835592 | tf_op jit(solution)/shard_map/ppermute | solution.py:376
  16.7 0.0 collective-permute-start.3
  16.7 5.1 %collective-permute-done.4.refs_0_ = f32[136,512]{1,0:T(8,128)S(1)} collective-permute-done((f32[136,512]{1,0:T(8,128)S(1)}, f32[136,512]{1,0:T(8,128)S(1)}, u32[]{:S(2)}, u32[]{:S(2)}) %collective-permute-start.4) | collective-permute-done | bytes 278560 | tf_op jit(solution)/shard_map/ppermute | solution.py:376
  21.7 0.0 collective-permute-start.5
  21.7 0.0 copy-start.4
  21.7 0.7 %copy-done.4 = s32[2]{0:T(128)S(1)} copy-done((s32[2]{0:T(128)S(1)}, s32[2]{0:T(128)}, u32[]{:S(2)}) %copy-start.4) | copy-done | bytes 32
  22.4 0.0 copy-start.5
  22.4 0.7 %copy-done.5 = s32[4,32,2]{1,2,0:T(2,128)S(1)} copy-done((s32[4,32,2]{1,2,0:T(2,128)S(1)}, s32[4,32,2]{1,2,0:T(2,128)}, u32[]{:S(2)}) %copy-start.5) | copy-done | bytes 1048
  23.1 0.0 copy-start.6
  23.1 0.7 %copy-done.6 = s32[16,2]{0,1:T(2,128)S(1)} copy-done((s32[16,2]{0,1:T(2,128)S(1)}, s32[16,2]{0,1:T(2,128)}, u32[]{:S(2)}) %copy-start.6) | copy-done | bytes 152
  23.8 0.0 copy-start.7
  23.8 0.7 %copy-done.7 = f32[16]{0:T(128)S(1)} copy-done((f32[16]{0:T(128)S(1)}, f32[16]{0:T(128)}, u32[]{:S(2)}) %copy-start.7) | copy-done | bytes 88
  24.4 0.0 copy-start.8
  24.4 0.7 %copy-done.8 = f32[16]{0:T(128)S(1)} copy-done((f32[16]{0:T(128)S(1)}, f32[16]{0:T(128)}, u32[]{:S(2)}) %copy-start.8) | copy-done | bytes 88
  25.1 4.6 %shard_map.82 = (bf16[2,2,384,256]{3,2,1,0:T(8,128)(2,1)S(1)}, bf16[4,2,256,384]{3,2,1,0:T(8,128)(2,1)S(1)}, bf16[4,2,384,256]{3,2,1,0:T(8,128)(2,1)S(1)}, bf16[...) custom-call(s32[2]{0:T(128)S(1)} %copy-done.4, s32[2,16]{1,0:T(2,128)S(1)} %bitcast.9, ...), custom_call_target="tpu_custom_call" | custom-call | flops 4194304 | bytes 6291456 | tf_op jit(solution)/shard_map/pallas_call | solution.py:413
  29.7 0.0 copy-start
  29.7 1.2 %copy-done = bf16[2,2,256,512]{3,2,1,0:T(8,128)(2,1)S(1)} copy-done((bf16[2,2,256,512]{3,2,1,0:T(8,128)(2,1)S(1)}, bf16[2,2,256,512]{3,2,1,0:T(8,128)(2,1)}, u32[]{:S(2)}) %copy-start) | copy-done | bytes 1048600
  30.9 0.0 copy-start.1
  30.9 0.8 %shard_map.85 = (bf16[2,2,64,768]{3,2,1,0:T(8,128)(2,1)S(1)}, f32[8,512]{1,0:T(8,128)S(1)}) custom-call(f32[136,512]{1,0:T(8,128)S(1)} %shard_map.84.refs_0_, bf16[2,2,256,512]{3,2,1,0:T(8,128)(2,1)S(1)} %copy-done), custom_call_target="tpu_custom_call" | custom-call | flops 201326592 | bytes 2097152 | tf_op jit(solution)/shard_map/pallas_call | solution.py:452
  31.7 0.4 copy-done.1
  32.1 0.8 %shard_map.87 = (bf16[2,2,64,768]{3,2,1,0:T(8,128)(2,1)S(1)}, f32[8,512]{1,0:T(8,128)S(1)}) custom-call(f32[136,512]{1,0:T(8,128)S(1)} %collective-permute-done.4.refs_0_, bf16[2,2,256,512]{3,2,1,0:T(8,128)(2,1)S(1)} %copy-done.1), custom_call_target="tpu_custom_call" | custom-call | flops 201326592 | bytes 2097152 | tf_op jit(solution)/shard_map/pallas_call | solution.py:452
  32.9 0.0 collective-permute-done.3.refs_0_
  33.0 0.8 %shard_map.86 = (bf16[2,2,64,768]{3,2,1,0:T(8,128)(2,1)S(1)}, f32[8,512]{1,0:T(8,128)S(1)}) custom-call(f32[136,512]{1,0:T(8,128)S(1)} %collective-permute-done.3.refs_0_, bf16[2,2,256,512]{3,2,1,0:T(8,128)(2,1)S(1)} %copy-done.1), custom_call_target="tpu_custom_call" | custom-call | flops 201326592 | bytes 2097152 | tf_op jit(solution)/shard_map/pallas_call | solution.py:452
  33.8 0.0 collective-permute-done.5.refs_6_
  33.8 0.0 copy-start.9
  33.8 1.9 %shard_map.88 = (bf16[2,384,768]{2,1,0:T(8,128)(2,1)S(1)}, f32[2,128,128]{2,1,0:T(8,128)S(1)}) custom-call(bf16[2,2,64,768]{3,2,1,0:T(8,128)(2,1)S(1)} %get-tuple-element.26.refs_0_, bf16[2,2,64,768]{3,2,1,0:T(8,128)(2,1)S(1)} %get-tuple-element.27.refs_1_, bf16[2,2,64,768]{3,2,1,0:T(8,128)(2,1)S(1)} %get-tuple-element.28.refs_2_, ...), custom_call_target="tpu_custom_call" | custom-call | flops 3221225472 | bytes 4194304 | tf_op jit(solution)/shard_map/pallas_call | solution.py:460
  35.7 0.0 copy-done.9
  35.7 3.6 %shard_map.89 = f32[2,2,128,128]{3,2,1,0:T(8,128)S(1)} custom-call(bf16[2,384,768]{2,1,0:T(8,128)(2,1)S(1)} %get-tuple-element.33.spectrum_ref, bf16[4,2,256,384]{3,2,1,0:T(8,128)(2,1)S(1)} %get-tuple-element.34.left_ref, bf16[4,2,384,256]{3,2,1,0:T(8,128)(2,1)S(1)} %get-tuple-element.35.right_ref, bf16[4,384,384]{2,1,0:T(8,128)(2,1)S(1)} %get-tuple-element.36.mask_ref, ...), custom_call_target="tpu_custom_call" | custom-call | flops 2147483648 | bytes 4194304 | tf_op jit(solution)/shard_map/pallas_call | solution.py:472
  39.3 0.6 collective-permute-start.6
  39.9 3.5 %shard_map.90 = f32[2,2,128,128]{3,2,1,0:T(8,128)S(1)} custom-call(bf16[2,384,768]{2,1,0:T(8,128)(2,1)S(1)} %get-tuple-element.33.spectrum_ref, bf16[4,2,256,384]{3,2,1,0:T(8,128)(2,1)S(1)} %get-tuple-element.34.left_ref, bf16[4,2,384,256]{3,2,1,0:T(8,128)(2,1)S(1)} %get-tuple-element.35.right_ref, bf16[4,384,384]{2,1,0:T(8,128)(2,1)S(1)} %get-tuple-element.36.mask_ref, ...), custom_call_target="tpu_custom_call" | custom-call | flops 2147483648 | bytes 4194304 | tf_op jit(solution)/shard_map/pallas_call | solution.py:472
  43.5 1.6 %collective-permute-start.7 = (f32[4,32,128]{2,1,0:T(8,128)S(1)}, f32[4,32,128]{2,1,0:T(8,128)S(1)}, u32[]{:S(2)}, u32[]{:S(2)}) collective-permute-start(f32[4,32,128]{2,1,0:T(8,128)S(1)} %get-tuple-element.46), channel_id=1, source_target_pairs={{0,2},{1,3},{2,0},{3,1},{4,6},{5,7},{6,4},{7,5},{8,10},{9,11},{10,... | collective-permute-start | bytes 196616 | tf_op jit(solution)/shard_map/ppermute | solution.py:376
  45.0 0.0 collective-permute-start.8
  45.0 0.0 collective-permute-done.6
  45.0 2.8 %collective-permute-done.7 = f32[4,32,128]{2,1,0:T(8,128)S(1)} collective-permute-done((f32[4,32,128]{2,1,0:T(8,128)S(1)}, f32[4,32,128]{2,1,0:T(8,128)S(1)}, u32[]{:S(2)}, u32[]{:S(2)}) %collective-permute-start.7) | collective-permute-done | bytes 65568 | tf_op jit(solution)/shard_map/ppermute | solution.py:376
  47.8 1.5 %collective-permute-done.8 = f32[4,32,128]{2,1,0:T(8,128)S(1)} collective-permute-done((f32[4,32,128]{2,1,0:T(8,128)S(1)}, f32[4,32,128]{2,1,0:T(8,128)S(1)}, u32[]{:S(2)}, u32[]{:S(2)}) %collective-permute-start.8) | collective-permute-done | bytes 65568 | tf_op jit(solution)/shard_map/ppermute | solution.py:376
  49.4 0.1 collective-permute-start.9
  49.5 1.1 %collective-permute-start.10 = (f32[4,32,128]{2,1,0:T(8,128)S(1)}, f32[4,32,128]{2,1,0:T(8,128)S(1)}, u32[]{:S(2)}, u32[]{:S(2)}) collective-permute-start(f32[4,32,128]{2,1,0:T(8,128)S(1)} %get-tuple-element.42), channel_id=1, source_target_pairs={{0,2},{1,3},{2,0},{3,1},{4,6},{5,7},{6,4},{7,5},{8,10},{9,11},{10,... | collective-permute-start | bytes 196616 | tf_op jit(solution)/shard_map/ppermute | solution.py:376
  50.6 0.7 %collective-permute-start.11 = (f32[4,32,128]{2,1,0:T(8,128)S(1)}, f32[4,32,128]{2,1,0:T(8,128)S(1)}, u32[]{:S(2)}, u32[]{:S(2)}) collective-permute-start(f32[4,32,128]{2,1,0:T(8,128)S(1)} %get-tuple-element.41), channel_id=1, source_target_pairs={{0,3},{1,2},{2,1},{3,0},{4,7},{5,6},{6,5},{7,4},{8,11},{9,10},{10,... | collective-permute-start | bytes 196616 | tf_op jit(solution)/shard_map/ppermute | solution.py:376
  51.3 0.0 collective-permute-done.9
  51.3 3.0 %collective-permute-done.10 = f32[4,32,128]{2,1,0:T(8,128)S(1)} collective-permute-done((f32[4,32,128]{2,1,0:T(8,128)S(1)}, f32[4,32,128]{2,1,0:T(8,128)S(1)}, u32[]{:S(2)}, u32[]{:S(2)}) %collective-permute-start.10) | collective-permute-done | bytes 65568 | tf_op jit(solution)/shard_map/ppermute | solution.py:376
  54.3 0.6 %collective-permute-done.11 = f32[4,32,128]{2,1,0:T(8,128)S(1)} collective-permute-done((f32[4,32,128]{2,1,0:T(8,128)S(1)}, f32[4,32,128]{2,1,0:T(8,128)S(1)}, u32[]{:S(2)}, u32[]{:S(2)}) %collective-permute-start.11) | collective-permute-done | bytes 65568 | tf_op jit(solution)/shard_map/ppermute | solution.py:376
  55.0 0.5 shard_map.91
  55.5 0.2 collective-permute-start.12
  55.7 1.0 %collective-permute-done.12 = f32[32,128]{1,0:T(8,128)S(1)} collective-permute-done((f32[32,128]{1,0:T(8,128)S(1)}, f32[32,128]{1,0:T(8,128)S(1)}, u32[]{:S(2)}, u32[]{:S(2)}) %collective-permute-start.12) | collective-permute-done | bytes 16416 | tf_op jit(solution)/shard_map/ppermute | solution.py:376
  56.7 1.0 %collective-permute-start.13 = (f32[32,128]{1,0:T(8,128)S(1)}, f32[32,128]{1,0:T(8,128)S(1)}, u32[]{:S(2)}, u32[]{:S(2)}) collective-permute-start(f32[32,128]{1,0:T(8,128)S(1)} %add.31), channel_id=1, source_target_pairs={{0,2},{1,3},{2,0},{3,1},{4,6},{5,7},{6,4},{7,5},{8,10},{9,11},{10,... | collective-permute-start | bytes 49160 | tf_op jit(solution)/shard_map/ppermute | solution.py:376
  57.7 2.8 %collective-permute-done.13 = f32[32,128]{1,0:T(8,128)S(1)} collective-permute-done((f32[32,128]{1,0:T(8,128)S(1)}, f32[32,128]{1,0:T(8,128)S(1)}, u32[]{:S(2)}, u32[]{:S(2)}) %collective-permute-start.13) | collective-permute-done | bytes 16416 | tf_op jit(solution)/shard_map/ppermute | solution.py:376
  60.4 0.8 %shard_map.92 = f32[32,32,128]{2,1,0:T(8,128)} custom-call(f32[32,32,128]{2,1,0:T(8,128)S(1)} %get-tuple-element.39.intensity_ref, f32[32,128]{1,0:T(8,128)S(1)} %add.32.sums_ref), custom_call_target="tpu_custom_call" | custom-call | flops 262144 | bytes 1048576 | tf_op jit(solution)/shard_map/pallas_call | solution.py:505
  (10 shorter events, 0.1 us)
Async XLA Ops:
  0.0 0.9 %copy-start.2 = (f32[2,32,512]{2,1,0:T(8,128)S(1)}, f32[2,32,512]{2,1,0:T(8,128)}, u32[]{:S(2)}) copy-start(f32[2,32,512]{2,1,0:T(8,128)} %potential_hbm.1) | copy-start | bytes 393220
  0.9 0.7 %copy-start.3 = (s32[2]{0:T(128)S(1)}, s32[2]{0:T(128)}, u32[]{:S(2)}) copy-start(s32[2]{0:T(128)} %anchor_hbm.3) | copy-start | bytes 28
  2.2 5.7 %collective-permute-start = (f32[40,512]{1,0:T(8,128)S(1)}, f32[40,512]{1,0:T(8,128)S(1)}, u32[]{:S(2)}, u32[]{:S(2)}) collective-permute-start(f32[40,512]{1,0:T(8,128)S(1)} %get-tuple-element.25), channel_id=1, source_target_pairs={{0,4},{1,5},{2,6},{3,7},{4,0},{5,1},{6,2},{7,3},{8,12},{9,13},{10,... | collective-permute-start | bytes 245768 | tf_op jit(solution)/shard_map/ppermute | solution.py:376
  5.3 9.2 %collective-permute-start.1 = (f32[40,512]{1,0:T(8,128)S(1)}, f32[40,512]{1,0:T(8,128)S(1)}, u32[]{:S(2)}, u32[]{:S(2)}) collective-permute-start(f32[40,512]{1,0:T(8,128)S(1)} %get-tuple-element.24.refs_0_), channel_id=1, source_target_pairs={{0,8},{1,9},{2,10},{3,11},{4,12},{5,13},{6,14},{7,15},{8,0},{9,1},... | collective-permute-start | bytes 245768 | tf_op jit(solution)/shard_map/ppermute | solution.py:376
  7.9 6.6 %collective-permute-start.2 = (f32[40,512]{1,0:T(8,128)S(1)}, f32[40,512]{1,0:T(8,128)S(1)}, u32[]{:S(2)}, u32[]{:S(2)}) collective-permute-start(f32[40,512]{1,0:T(8,128)S(1)} %get-tuple-element.25), channel_id=1, source_target_pairs={{0,12},{1,13},{2,14},{3,15},{4,8},{5,9},{6,10},{7,11},{8,4},{9,5},... | collective-permute-start | bytes 245768 | tf_op jit(solution)/shard_map/ppermute | solution.py:376
  15.1 6.6 %collective-permute-start.4 = (f32[136,512]{1,0:T(8,128)S(1)}, f32[136,512]{1,0:T(8,128)S(1)}, u32[]{:S(2)}, u32[]{:S(2)}) collective-permute-start(f32[136,512]{1,0:T(8,128)S(1)} %shard_map.84.refs_0_), channel_id=1, source_target_pairs={{0,2},{1,3},{2,0},{3,1},{4,6},{5,7},{6,4},{7,5},{8,10},{9,11},{10,... | collective-permute-start | bytes 835592 | tf_op jit(solution)/shard_map/ppermute | solution.py:376
  16.7 16.3 %collective-permute-start.3 = (f32[136,512]{1,0:T(8,128)S(1)}, f32[136,512]{1,0:T(8,128)S(1)}, u32[]{:S(2)}, u32[]{:S(2)}) collective-permute-start(f32[136,512]{1,0:T(8,128)S(1)} %shard_map.84.refs_0_), channel_id=1, source_target_pairs={{0,1},{1,0},{2,3},{3,2},{4,5},{5,4},{6,7},{7,6},{8,9},{9,8},{10,11... | collective-permute-start | bytes 835592 | tf_op jit(solution)/shard_map/ppermute | solution.py:376
  21.7 12.0 %collective-permute-start.5 = (f32[136,512]{1,0:T(8,128)S(1)}, f32[136,512]{1,0:T(8,128)S(1)}, u32[]{:S(2)}, u32[]{:S(2)}) collective-permute-start(f32[136,512]{1,0:T(8,128)S(1)} %collective-permute-done.4.refs_0_), channel_id=1, source_target_pairs={{0,1},{1,0},{2,3},{3,2},{4,5},{5,4},{6,7},{7,6},{8,9},{9,8},{10,11... | collective-permute-start | bytes 835592 | tf_op jit(solution)/shard_map/ppermute | solution.py:376
  21.7 0.7 %copy-start.4 = (s32[2]{0:T(128)S(1)}, s32[2]{0:T(128)}, u32[]{:S(2)}) copy-start(s32[2]{0:T(128)} %anchor_hbm.3) | copy-start | bytes 28
  22.4 0.7 %copy-start.5 = (s32[4,32,2]{1,2,0:T(2,128)S(1)}, s32[4,32,2]{1,2,0:T(2,128)}, u32[]{:S(2)}) copy-start(s32[4,32,2]{1,2,0:T(2,128)} %param.12) | copy-start | bytes 3076
  23.1 0.7 %copy-start.6 = (s32[16,2]{0,1:T(2,128)S(1)}, s32[16,2]{0,1:T(2,128)}, u32[]{:S(2)}) copy-start(s32[16,2]{0,1:T(2,128)} %param.9) | copy-start | bytes 388
  23.8 0.7 %copy-start.7 = (f32[16]{0:T(128)S(1)}, f32[16]{0:T(128)}, u32[]{:S(2)}) copy-start(f32[16]{0:T(128)} %refs_2_.1) | copy-start | bytes 196
  24.4 0.7 %copy-start.8 = (f32[16]{0:T(128)S(1)}, f32[16]{0:T(128)}, u32[]{:S(2)}) copy-start(f32[16]{0:T(128)} %refs_3_.1) | copy-start | bytes 196
  29.7 1.2 %copy-start = (bf16[2,2,256,512]{3,2,1,0:T(8,128)(2,1)S(1)}, bf16[2,2,256,512]{3,2,1,0:T(8,128)(2,1)}, u32[]{:S(2)}) copy-start(bf16[2,2,256,512]{3,2,1,0:T(8,128)(2,1)} %constant.31.clone.refs_1_.refs_7_) | copy-start | bytes 3145732
  30.9 1.2 %copy-start.1 = (bf16[2,2,256,512]{3,2,1,0:T(8,128)(2,1)S(1)}, bf16[2,2,256,512]{3,2,1,0:T(8,128)(2,1)}, u32[]{:S(2)}) copy-start(bf16[2,2,256,512]{3,2,1,0:T(8,128)(2,1)} %constant.31.clone.refs_1_.refs_7_) | copy-start | bytes 3145732
  33.8 1.9 %copy-start.9 = (bf16[1,2,128,256]{3,2,1,0:T(8,128)(2,1)S(1)}, bf16[1,2,128,256]{3,2,1,0:T(8,128)(2,1)}, u32[]{:S(2)}) copy-start(bf16[1,2,128,256]{3,2,1,0:T(8,128)(2,1)} %constant.32.clone.last_x_ref) | copy-start | bytes 393220
  39.3 5.7 %collective-permute-start.6 = (f32[4,32,128]{2,1,0:T(8,128)S(1)}, f32[4,32,128]{2,1,0:T(8,128)S(1)}, u32[]{:S(2)}, u32[]{:S(2)}) collective-permute-start(f32[4,32,128]{2,1,0:T(8,128)S(1)} %get-tuple-element.47), channel_id=1, source_target_pairs={{0,1},{1,0},{2,3},{3,2},{4,5},{5,4},{6,7},{7,6},{8,9},{9,8},{10,11... | collective-permute-start | bytes 196616 | tf_op jit(solution)/shard_map/ppermute | solution.py:376
  43.5 4.3 %collective-permute-start.7 = (f32[4,32,128]{2,1,0:T(8,128)S(1)}, f32[4,32,128]{2,1,0:T(8,128)S(1)}, u32[]{:S(2)}, u32[]{:S(2)}) collective-permute-start(f32[4,32,128]{2,1,0:T(8,128)S(1)} %get-tuple-element.46), channel_id=1, source_target_pairs={{0,2},{1,3},{2,0},{3,1},{4,6},{5,7},{6,4},{7,5},{8,10},{9,11},{10,... | collective-permute-start | bytes 196616 | tf_op jit(solution)/shard_map/ppermute | solution.py:376
  45.0 4.3 %collective-permute-start.8 = (f32[4,32,128]{2,1,0:T(8,128)S(1)}, f32[4,32,128]{2,1,0:T(8,128)S(1)}, u32[]{:S(2)}, u32[]{:S(2)}) collective-permute-start(f32[4,32,128]{2,1,0:T(8,128)S(1)} %get-tuple-element.45), channel_id=1, source_target_pairs={{0,3},{1,2},{2,1},{3,0},{4,7},{5,6},{6,5},{7,4},{8,11},{9,10},{10,... | collective-permute-start | bytes 196616 | tf_op jit(solution)/shard_map/ppermute | solution.py:376
  49.4 1.9 %collective-permute-start.9 = (f32[4,32,128]{2,1,0:T(8,128)S(1)}, f32[4,32,128]{2,1,0:T(8,128)S(1)}, u32[]{:S(2)}, u32[]{:S(2)}) collective-permute-start(f32[4,32,128]{2,1,0:T(8,128)S(1)} %get-tuple-element.43), channel_id=1, source_target_pairs={{0,1},{1,0},{2,3},{3,2},{4,5},{5,4},{6,7},{7,6},{8,9},{9,8},{10,11... | collective-permute-start | bytes 196616 | tf_op jit(solution)/shard_map/ppermute | solution.py:376
  49.5 4.8 %collective-permute-start.10 = (f32[4,32,128]{2,1,0:T(8,128)S(1)}, f32[4,32,128]{2,1,0:T(8,128)S(1)}, u32[]{:S(2)}, u32[]{:S(2)}) collective-permute-start(f32[4,32,128]{2,1,0:T(8,128)S(1)} %get-tuple-element.42), channel_id=1, source_target_pairs={{0,2},{1,3},{2,0},{3,1},{4,6},{5,7},{6,4},{7,5},{8,10},{9,11},{10,... | collective-permute-start | bytes 196616 | tf_op jit(solution)/shard_map/ppermute | solution.py:376
  50.6 4.4 %collective-permute-start.11 = (f32[4,32,128]{2,1,0:T(8,128)S(1)}, f32[4,32,128]{2,1,0:T(8,128)S(1)}, u32[]{:S(2)}, u32[]{:S(2)}) collective-permute-start(f32[4,32,128]{2,1,0:T(8,128)S(1)} %get-tuple-element.41), channel_id=1, source_target_pairs={{0,3},{1,2},{2,1},{3,0},{4,7},{5,6},{6,5},{7,4},{8,11},{9,10},{10,... | collective-permute-start | bytes 196616 | tf_op jit(solution)/shard_map/ppermute | solution.py:376
  55.5 1.2 %collective-permute-start.12 = (f32[32,128]{1,0:T(8,128)S(1)}, f32[32,128]{1,0:T(8,128)S(1)}, u32[]{:S(2)}, u32[]{:S(2)}) collective-permute-start(f32[32,128]{1,0:T(8,128)S(1)} %get-tuple-element.40), channel_id=1, source_target_pairs={{0,1},{1,0},{2,3},{3,2},{4,5},{5,4},{6,7},{7,6},{8,9},{9,8},{10,11... | collective-permute-start | bytes 49160 | tf_op jit(solution)/shard_map/ppermute | solution.py:376
  56.7 3.7 %collective-permute-start.13 = (f32[32,128]{1,0:T(8,128)S(1)}, f32[32,128]{1,0:T(8,128)S(1)}, u32[]{:S(2)}, u32[]{:S(2)}) collective-permute-start(f32[32,128]{1,0:T(8,128)S(1)} %add.31), channel_id=1, source_target_pairs={{0,2},{1,3},{2,0},{3,1},{4,6},{5,7},{6,4},{7,5},{8,10},{9,11},{10,... | collective-permute-start | bytes 49160 | tf_op jit(solution)/shard_map/ppermute | solution.py:376

commit v3 on v2

--- a/solution.py
+++ b/solution.py
@@ -12,6 +12,7 @@
 CROP = 256
 TILE = 128
 MAX_TILT = 16
+STRIP = 32
 
 VMEM = pl.BlockSpec(memory_space=pltpu.VMEM)
 HBM = pl.BlockSpec(memory_space=pltpu.HBM)
@@ -202,33 +203,48 @@
     anchor_ref, tilts_ref, aperture_ref, aberration_ref, spots_ref = refs[:5]
     tile, member, anchor_row, anchor_col = sizes.anchors(anchor_ref)
     half, kept, freqs, length = sizes.half, sizes.kept, sizes.freqs, sizes.length
-    for parity in range(2):
-        shape = (kept, half)
-        freq = 2 * iota(shape, 0) - kept + parity
-        place = sizes.grid_row(iota((1, half), 1), tile, member)
+    place = sizes.grid_row(iota((1, half), 1), tile, member)
+    step = cis_index(-place, length)
+    for top in range(0, kept, STRIP):
+        freq = 2 * (iota((STRIP, 1), 0) + top) - kept
         pair = cis_index(-freq * place, length)
-        for part in range(2):
-            put(rows_ref, parity, pair[part], part * kept, 0)
+        for parity in range(2):
+            for part in range(2):
+                put(rows_ref, parity, pair[part], part * kept + top, 0)
+            pair = mul(pair, step)
     scale = 1.0 / (length * length)
-    shape = (TILE, freqs)
-    spot_y = anchor_row + sizes.tile_row(iota((TILE, 1), 0), member, anchor_row)
     freq_lane = sizes.frequency(iota((1, freqs), 1))
-    freq_row = sizes.frequency(iota((freqs, 1), 0))
     spot_x = anchor_col + iota((1, TILE), 1)
-    for b in range(sizes.own):
-        beam = member * sizes.own + b
-        ky = freq_lane + tilts_ref[0, beam]
-        kx = freq_row + tilts_ref[1, beam]
-        pair = cis_index(ky * (2 * spot_y - ky), 2 * length)
-        for part in range(2):
-            put(left_ref, b, pair[part] * scale, part * TILE, 0)
-        pair = cis_index(kx * (2 * spot_x - kx), 2 * length)
-        for part in range(2):
-            put(right_ref, b, pair[part], 0, part * TILE)
-        ky = freq_row + tilts_ref[0, beam]
-        kx = freq_lane + tilts_ref[1, beam]
-        limit = (length * length + 8) // 9
-        mask_ref[b] = jnp.where(ky * ky < limit - kx * kx, 1.0, 0.0).astype(jnp.bfloat16)
+    limit = (length * length + 8) // 9
+    beams = [member * sizes.own + b for b in range(sizes.own)]
+    tilt_y = [tilts_ref[0, beam] for beam in beams]
+    tilt_x = [tilts_ref[1, beam] for beam in beams]
+    chirps = []
+    for t in tilt_y:
+        ky = freq_lane + t
+        chirps.append(cis_index(-ky * ky, 2 * length))
+    for top in range(0, TILE, STRIP):
+        spot_y = anchor_row + sizes.tile_row(iota((STRIP, 1), 0) + top, member, anchor_row)
+        common = [value * scale for value in cis_index(freq_lane * spot_y, length)]
+        for b in range(sizes.own):
+            pair = mul(mul(common, chirps[b]), cis_index(tilt_y[b] * spot_y, length))
+            for part in range(2):
+                put(left_ref, b, pair[part], part * TILE + top, 0)
+    starts = [cis_index(t * spot_x, length) for t in tilt_x]
+    squares = []
+    for t in tilt_x:
+        kx = freq_lane + t
+        squares.append(limit - kx * kx)
+    for top in range(0, freqs, STRIP):
+        freq_row = sizes.frequency(iota((STRIP, 1), 0) + top)
+        common = cis_index(freq_row * spot_x, length)
+        for b in range(sizes.own):
+            kx = freq_row + tilt_x[b]
+            pair = mul(mul(common, cis_index(-kx * kx, 2 * length)), starts[b])
+            for part in range(2):
+                put(right_ref, b, pair[part], top, part * TILE)
+            ky = freq_row + tilt_y[b]
+            mask_ref[b, top:top + STRIP] = jnp.where(ky * ky < squares[b], 1.0, 0.0).astype(jnp.bfloat16)
     shape = (TILE, TILE)
     pair = cis_index(-iota(shape, 0) * sizes.tile_row(iota((1, TILE), 1), member, anchor_row), TILE)
     for part in range(2):
@@ -329,37 +345,54 @@
             out_ref[1, parity * kept:(parity + 1) * kept, c * freqs:(c + 1) * freqs] = low
 
 
-def beams_kernel(sizes, spectrum_ref, left_ref, right_ref, mask_ref, last_x_ref, last_y_ref, slice_ref, out_ref):
+def beams_kernel(sizes, first, spectrum_ref, left_ref, right_ref, mask_ref, last_x_ref, last_y_ref, slice_ref, *refs):
+    out_refs, field_ref = refs[:-1], refs[-1]
     freqs = sizes.freqs
-    mask = jnp.concatenate((mask_ref[0], mask_ref[0]), 1)
-    masked = (spectrum_ref[0] * mask, spectrum_ref[1] * mask)
-    field = combine(dot3((left_ref[0, 0], left_ref[0, 1]), masked), TILE, freqs)
-    field = split(jnp.concatenate(field, 0))
-    field = combine(dot3(field, (right_ref[0, 0], right_ref[0, 1])), TILE, TILE)
-    field = mul(field, (slice_ref[0], slice_ref[1]))
-    field = split(jnp.concatenate(field, 0))
-    field = combine(dot3(field, (last_x_ref[0, 0], last_x_ref[0, 1])), TILE, TILE)
-    field = split(jnp.concatenate(field, 1))
-    field = combine(dot3((last_y_ref[0, 0], last_y_ref[0, 1]), field), TILE, TILE)
-    out_ref[0, 0] = field[0]
-    out_ref[0, 1] = field[1]
-
-
-def probes_kernel(sizes, probes, weights_ref, fields_ref, out_ref, sums_ref):
+    some = field_ref.shape[0] // 2
+    member = lax.axis_index("beam").astype(jnp.int32) % sizes.group
+    for b in range(some):
+        mask = mask_ref[first + b]
+        mask = jnp.concatenate((mask, mask), 1)
+        masked = (spectrum_ref[0] * mask, spectrum_ref[1] * mask)
+        field = combine(dot3((left_ref[first + b, 0], left_ref[first + b, 1]), masked), TILE, freqs)
+        field = split(jnp.concatenate(field, 0))
+        field = combine(dot3(field, (right_ref[first + b, 0], right_ref[first + b, 1])), TILE, TILE)
+        field = mul(field, (slice_ref[0], slice_ref[1]))
+        field = split(jnp.concatenate(field, 0))
+        field = combine(dot3(field, (last_x_ref[0, 0], last_x_ref[0, 1])), TILE, TILE)
+        field = split(jnp.concatenate(field, 1))
+        field = combine(dot3((last_y_ref[0, 0], last_y_ref[0, 1]), field), TILE, TILE)
+        for c in range(2):
+            field_ref[2 * b + c] = field[c]
+    for other, out_ref in enumerate(out_refs):
+        start = pl.multiple_of((member ^ other) * sizes.out_rows, sizes.out_rows)
+        for n in range(2 * some):
+            out_ref[n * sizes.out_rows:(n + 1) * sizes.out_rows] = field_ref[n, pl.ds(start, sizes.out_rows), :]
+
+
+def probes_kernel(sizes, probes, weights_ref, *refs):
+    field_refs, (out_ref, sums_ref, fields_ref) = refs[:-3], refs[-3:]
+    count = field_refs[0].shape[0]
+    for n, ref in enumerate(field_refs):
+        fields_ref[n * count:(n + 1) * count] = ref[...]
     inner = fields_ref.shape[0] // sizes.out_rows
-    high, low = split(weights_ref[...])
+    weights = split(weights_ref[...])
     total = jnp.zeros((probes, TILE), jnp.float32)
     for row in range(sizes.out_rows):
         fields = split(fields_ref[pl.ds(row, inner, stride=sizes.out_rows), :])
-        both = dot3((high, low), fields)
+        both = dot3(weights, fields)
         intensity = both[:probes] * both[:probes] + both[probes:] * both[probes:]
         out_ref[row] = intensity
         total = total + intensity
     sums_ref[...] = jnp.broadcast_to(jnp.sum(total, 1, keepdims=True), (probes, TILE))
 
 
-def scale_kernel(intensity_ref, sums_ref, out_ref):
-    level = sums_ref[...] * (1.0 / (TILE * TILE)) + 1e-06
+def scale_kernel(intensity_ref, *refs):
+    sums_refs, out_ref = refs[:-1], refs[-1]
+    level = sums_refs[0][...]
+    for ref in sums_refs[1:]:
+        level = level + ref[...]
+    level = level * (1.0 / (TILE * TILE)) + 1e-06
     out_ref[...] = intensity_ref[...] / level[None]
 
 
@@ -467,47 +500,38 @@
 
     arrived = []
     for h in range(halves):
-        table = lambda *shape: pl.BlockSpec((1,) + shape, lambda i: (h * some + i, 0, 0, 0))
-        whole = lambda *shape: pl.BlockSpec(shape, lambda i: (0,) * len(shape))
         fields = call(
-            functools.partial(beams_kernel, sizes),
-            full_type(some, 2, TILE, TILE),
-            [
-                whole(2, freqs, 2 * freqs),
-                table(2, 2 * TILE, freqs),
-                table(2, freqs, 2 * TILE),
-                pl.BlockSpec((1, freqs, freqs), lambda i: (h * some + i, 0, 0)),
-                whole(1, 2, TILE, 2 * TILE),
-                whole(1, 2, 2 * TILE, TILE),
-                whole(2, TILE, TILE),
-            ],
-            grid=(some,),
-            out_specs=pl.BlockSpec((1, 2, TILE, TILE), lambda i: (i, 0, 0, 0)),
-            cost_estimate=pl.CostEstimate(flops=some << 30, bytes_accessed=4 << 20, transcendentals=0),
+            functools.partial(beams_kernel, sizes, h * some),
+            (full_type(2 * some * sizes.out_rows, TILE),) * group,
+            [VMEM] * 7,
+            scratch_shapes=[pltpu.VMEM((2 * some, TILE, TILE), jnp.float32)],
+            cost_estimate=estimate(some << 30, 4 << 20),
         )(spectrum, left, right, masks, last_x, last_y, slice_one)
-        fields = fields.reshape(2 * some, TILE, TILE)
-        for other in range(group):
-            start = (member ^ other) * sizes.out_rows
-            block = lax.dynamic_slice_in_dim(fields, start, sizes.out_rows, 1)
-            arrived.append(block if other == 0 else swap(block, other))
-    arrived = jnp.concatenate(arrived, 0).reshape(2 * sizes.beams * sizes.out_rows, TILE)
+        arrived.append(fields[0])
+        for other in range(1, group):
+            arrived.append(swap(fields[other], other))
 
     intensity, total = call(
         functools.partial(probes_kernel, sizes, probes),
         (full_type(sizes.out_rows, probes, TILE), full_type(probes, TILE)),
-        [VMEM, VMEM],
-        cost_estimate=pl.CostEstimate(flops=1 << 26, bytes_accessed=2 << 20, transcendentals=0),
-    )(weights, arrived)
-    bits = 1
-    while bits < group:
-        total = total + swap(total, bits)
-        bits *= 2
+        [VMEM] * (1 + len(arrived)),
+        scratch_shapes=[pltpu.VMEM((2 * sizes.beams * sizes.out_rows, TILE), jnp.float32)],
+        cost_estimate=estimate(1 << 26, 2 << 20),
+    )(weights, *arrived)
+    totals = [total]
+    if group <= 4:
+        for other in range(1, group):
+            totals.append(swap(total, other))
+    else:
+        for bits in member_steps(group):
+            total = total + swap(total, bits)
+        totals = [total]
     return call(
         scale_kernel,
         full_type(sizes.out_rows, probes, TILE),
-        [VMEM, VMEM],
-        cost_estimate=pl.CostEstimate(flops=1 << 18, bytes_accessed=1 << 20, transcendentals=0),
-    )(intensity, total)
+        [VMEM] * (1 + len(totals)),
+        cost_estimate=estimate(1 << 18, 1 << 20),
+    )(intensity, *totals)
 
 
 def member_steps(group):

time: 61.6 us -> 56.4 us (0.916)
  waiting for transfers between devices: 23.3 us -> 18.7 us
  Pallas kernels: 18.7 us -> 17.4 us
  starting transfers between devices: 12.5 us -> 13.7 us
  local copies, waits for them, and re-layouts: 6.59 us -> 5.85 us
    ppermute x14 -> x15, waiting for transfers between devices: 23.3 us -> 18.7 us  [swap(): return lax.ppermute(value, 'beam', [(i, i ^ bits) for i in range(devices)])]
    ppermute x14 -> x15, starting transfers between devices: 12.5 us -> 13.7 us  [swap(): return lax.ppermute(value, 'beam', [(i, i ^ bits) for i in range(devices)])]
    pallas_call x3, Pallas kernels: 7.94 us -> 7.08 us  [the longest x2 6.24 us: per_device(): call(functools.partial(beams_kernel, sizes, h * some), (full_type(2 * som...]
    unnamed x25 -> x18, local copies, waits for them, and re-layouts: 6.53 us -> 5.85 us
  transfers between devices with their start and end apart: 14 -> 15, of which waited for: 8 -> 10; matrix products, arithmetic and copies ran while one was open for 0% -> 0% of each run, Pallas kernels for 17% -> 17%
where the time goes in v3:
time: 56.4 us; the launch traced here: 55.8 us
  waiting for transfers between devices  18.7 us (33%)
  Pallas kernels  17.4 us (31%)
  starting transfers between devices  13.7 us (24%)
  local copies, waits for them, and re-layouts  5.85 us (10%)
    ppermute x15, waiting for transfers between devices, swap(): return lax.ppermute(value, 'beam', [(i, i ^ bits) for i in range(devices)])  18.7 us
    ppermute x15, starting transfers between devices, swap(): return lax.ppermute(value, 'beam', [(i, i ^ bits) for i in range(devices)])  13.7 us
    pallas_call x2, Pallas kernels, per_device(): call(functools.partial(beams_kernel, sizes, h * some), (full_type(2 * som...  6.24 us
    unnamed x18, local copies, waits for them, and re-layouts  5.85 us
    pallas_call x1, Pallas kernels, per_device(): call(functools.partial(tables_kernel, sizes, probes, halves), (half_type(...  4.11 us
    pallas_call x3, Pallas kernels, per_device(): call(functools.partial(spread_kernel, sizes), (half_type(2, 2, pairs, 2 *...  2.49 us
    pallas_call x1, Pallas kernels, per_device(): call(functools.partial(spectrum_kernel, sizes, len(spreads)), (half_type(...  1.89 us
  transfers between devices with their start and end apart: 15, of which 10 were waited for; matrix products, arithmetic and copies ran while one was open for 0% of the time, Pallas kernels for 17%

profile of v3, /device:TPU:0, one launch (start us, length us, event | category | flops | bytes accessed | tf_op | source)
XLA Modules:
  0.0 55.8 jit_solution(1244770999015489911)
XLA Ops:
  0.0 0.0 copy-start.2
  0.0 0.9 %copy-done.2 = f32[2,32,512]{2,1,0:T(8,128)S(1)} copy-done((f32[2,32,512]{2,1,0:T(8,128)S(1)}, f32[2,32,512]{2,1,0:T(8,128)}, u32[]{:S(2)}) %copy-start.2) | copy-done | bytes 131096
  0.9 0.0 copy-start.3
  0.9 0.7 %copy-done.3 = s32[2]{0:T(128)S(1)} copy-done((s32[2]{0:T(128)S(1)}, s32[2]{0:T(128)}, u32[]{:S(2)}) %copy-start.3) | copy-done | bytes 32
  1.6 0.6 %shard_map.83 = (f32[40,512]{1,0:T(8,128)S(1)}, f32[40,512]{1,0:T(8,128)S(1)}) custom-call(s32[2]{0:T(128)S(1)} %copy-done.3, f32[2,32,512]{2,1,0:T(8,128)S(1)} %copy-done.2), custom_call_target="tpu_custom_call" | custom-call | flops 65536 | bytes 262144 | tf_op jit(solution)/shard_map/pallas_call | solution.py:430
  2.2 4.1 %collective-permute-start.1 = (f32[40,512]{1,0:T(8,128)S(1)}, f32[40,512]{1,0:T(8,128)S(1)}, u32[]{:S(2)}, u32[]{:S(2)}) collective-permute-start(f32[40,512]{1,0:T(8,128)S(1)} %get-tuple-element.32.refs_0_), channel_id=1, source_target_pairs={{0,8},{1,9},{2,10},{3,11},{4,12},{5,13},{6,14},{7,15},{8,0},{9,1},... | collective-permute-start | bytes 245768 | tf_op jit(solution)/shard_map/ppermute | solution.py:409
  6.3 1.3 %collective-permute-start.2 = (f32[40,512]{1,0:T(8,128)S(1)}, f32[40,512]{1,0:T(8,128)S(1)}, u32[]{:S(2)}, u32[]{:S(2)}) collective-permute-start(f32[40,512]{1,0:T(8,128)S(1)} %get-tuple-element.33), channel_id=1, source_target_pairs={{0,12},{1,13},{2,14},{3,15},{4,8},{5,9},{6,10},{7,11},{8,4},{9,5},... | collective-permute-start | bytes 245768 | tf_op jit(solution)/shard_map/ppermute | solution.py:409
  7.7 0.2 collective-permute-start
  7.9 4.1 %collective-permute-done.1.refs_2_ = f32[40,512]{1,0:T(8,128)S(1)} collective-permute-done((f32[40,512]{1,0:T(8,128)S(1)}, f32[40,512]{1,0:T(8,128)S(1)}, u32[]{:S(2)}, u32[]{:S(2)}) %collective-permute-start.1) | collective-permute-done | bytes 81952 | tf_op jit(solution)/shard_map/ppermute | solution.py:409
  12.0 1.0 %collective-permute-done.2.refs_3_ = f32[40,512]{1,0:T(8,128)S(1)} collective-permute-done((f32[40,512]{1,0:T(8,128)S(1)}, f32[40,512]{1,0:T(8,128)S(1)}, u32[]{:S(2)}, u32[]{:S(2)}) %collective-permute-start.2) | collective-permute-done | bytes 81952 | tf_op jit(solution)/shard_map/ppermute | solution.py:409
  13.0 0.5 collective-permute-done.refs_1_
  13.5 0.6 %shard_map.84.refs_0_ = f32[136,512]{1,0:T(8,128)S(1)} custom-call(s32[2]{0:T(128)S(1)} %copy-done.3, f32[40,512]{1,0:T(8,128)S(1)} %get-tuple-element.32.refs_0_, f32[40,512]{1,0:T(8,128)S(1)} %collective-permute-done.refs_1_, f32[40,512]{1,0:T(8,128)S(1)} %collective-permute-done.1.refs_2_, f32[40,512]{1,0:T(8,128)S(1)} %collective-permute-done.2.refs_3_), custom_call_target="tpu_custom_call" | custom-call | flops 65536 | bytes 524288 | tf_op jit(solution)/shard_map/pallas_call | solution.py:467
  14.1 1.7 %collective-permute-start.4 = (f32[136,512]{1,0:T(8,128)S(1)}, f32[136,512]{1,0:T(8,128)S(1)}, u32[]{:S(2)}, u32[]{:S(2)}) collective-permute-start(f32[136,512]{1,0:T(8,128)S(1)} %shard_map.84.refs_0_), channel_id=1, source_target_pairs={{0,2},{1,3},{2,0},{3,1},{4,6},{5,7},{6,4},{7,5},{8,10},{9,11},{10,... | collective-permute-start | bytes 835592 | tf_op jit(solution)/shard_map/ppermute | solution.py:409
  15.9 0.0 collective-permute-start.3
  15.9 5.6 %collective-permute-done.4.refs_0_ = f32[136,512]{1,0:T(8,128)S(1)} collective-permute-done((f32[136,512]{1,0:T(8,128)S(1)}, f32[136,512]{1,0:T(8,128)S(1)}, u32[]{:S(2)}, u32[]{:S(2)}) %collective-permute-start.4) | collective-permute-done | bytes 278560 | tf_op jit(solution)/shard_map/ppermute | solution.py:409
  21.5 0.0 collective-permute-start.5
  21.5 0.0 copy-start.4
  21.5 0.7 %copy-done.4 = s32[4,32,2]{1,2,0:T(2,128)S(1)} copy-done((s32[4,32,2]{1,2,0:T(2,128)S(1)}, s32[4,32,2]{1,2,0:T(2,128)}, u32[]{:S(2)}) %copy-start.4) | copy-done | bytes 1048
  22.2 0.0 copy-start.5
  22.2 0.7 %copy-done.5 = s32[16,2]{0,1:T(2,128)S(1)} copy-done((s32[16,2]{0,1:T(2,128)S(1)}, s32[16,2]{0,1:T(2,128)}, u32[]{:S(2)}) %copy-start.5) | copy-done | bytes 152
  22.9 0.0 copy-start.6
  22.9 0.7 %copy-done.6 = f32[16]{0:T(128)S(1)} copy-done((f32[16]{0:T(128)S(1)}, f32[16]{0:T(128)}, u32[]{:S(2)}) %copy-start.6) | copy-done | bytes 88
  23.5 0.0 copy-start.7
  23.5 0.7 %copy-done.7 = f32[16]{0:T(128)S(1)} copy-done((f32[16]{0:T(128)S(1)}, f32[16]{0:T(128)}, u32[]{:S(2)}) %copy-start.7) | copy-done | bytes 88
  24.2 4.1 %shard_map.82 = (bf16[2,2,384,256]{3,2,1,0:T(8,128)(2,1)S(1)}, bf16[4,2,256,384]{3,2,1,0:T(8,128)(2,1)S(1)}, bf16[4,2,384,256]{3,2,1,0:T(8,128)(2,1)S(1)}, bf16[...) custom-call(s32[2]{0:T(128)S(1)} %copy-done.3, s32[2,16]{1,0:T(2,128)S(1)} %bitcast.3, ...), custom_call_target="tpu_custom_call" | custom-call | flops 4194304 | bytes 6291456 | tf_op jit(solution)/shard_map/pallas_call | solution.py:446
  28.3 0.0 copy-start
  28.3 1.2 %copy-done = bf16[2,2,256,512]{3,2,1,0:T(8,128)(2,1)S(1)} copy-done((bf16[2,2,256,512]{3,2,1,0:T(8,128)(2,1)S(1)}, bf16[2,2,256,512]{3,2,1,0:T(8,128)(2,1)}, u32[]{:S(2)}) %copy-start) | copy-done | bytes 1048600
  29.5 0.0 copy-start.1
  29.5 0.8 %shard_map.85 = (bf16[2,2,64,768]{3,2,1,0:T(8,128)(2,1)S(1)}, f32[8,512]{1,0:T(8,128)S(1)}) custom-call(f32[136,512]{1,0:T(8,128)S(1)} %shard_map.84.refs_0_, bf16[2,2,256,512]{3,2,1,0:T(8,128)(2,1)S(1)} %copy-done), custom_call_target="tpu_custom_call" | custom-call | flops 201326592 | bytes 2097152 | tf_op jit(solution)/shard_map/pallas_call | solution.py:485
  30.4 0.4 copy-done.1
  30.8 0.8 %shard_map.87 = (bf16[2,2,64,768]{3,2,1,0:T(8,128)(2,1)S(1)}, f32[8,512]{1,0:T(8,128)S(1)}) custom-call(f32[136,512]{1,0:T(8,128)S(1)} %collective-permute-done.4.refs_0_, bf16[2,2,256,512]{3,2,1,0:T(8,128)(2,1)S(1)} %copy-done.1), custom_call_target="tpu_custom_call" | custom-call | flops 201326592 | bytes 2097152 | tf_op jit(solution)/shard_map/pallas_call | solution.py:485
  31.6 0.0 collective-permute-done.3.refs_0_
  31.6 0.8 %shard_map.86 = (bf16[2,2,64,768]{3,2,1,0:T(8,128)(2,1)S(1)}, f32[8,512]{1,0:T(8,128)S(1)}) custom-call(f32[136,512]{1,0:T(8,128)S(1)} %collective-permute-done.3.refs_0_, bf16[2,2,256,512]{3,2,1,0:T(8,128)(2,1)S(1)} %copy-done.1), custom_call_target="tpu_custom_call" | custom-call | flops 201326592 | bytes 2097152 | tf_op jit(solution)/shard_map/pallas_call | solution.py:485
  32.4 0.0 collective-permute-done.5.refs_6_
  32.5 0.0 copy-start.8
  32.5 1.9 %shard_map.88 = (bf16[2,384,768]{2,1,0:T(8,128)(2,1)S(1)}, f32[2,128,128]{2,1,0:T(8,128)S(1)}) custom-call(bf16[2,2,64,768]{3,2,1,0:T(8,128)(2,1)S(1)} %get-tuple-element.34.refs_0_, bf16[2,2,64,768]{3,2,1,0:T(8,128)(2,1)S(1)} %get-tuple-element.35.refs_1_, bf16[2,2,64,768]{3,2,1,0:T(8,128)(2,1)S(1)} %get-tuple-element.36.refs_2_, ...), custom_call_target="tpu_custom_call" | custom-call | flops 3221225472 | bytes 4194304 | tf_op jit(solution)/shard_map/pallas_call | solution.py:493
  34.4 0.0 copy-done.8
  34.4 3.1 %shard_map.90 = (f32[128,128]{1,0:T(8,128)S(1)}, f32[128,128]{1,0:T(8,128)S(1)}, f32[128,128]{1,0:T(8,128)S(1)}, f32[128,128]{1,0:T(8,128)S(1)}) custom-call(bf16[2,384,768]{2,1,0:T(8,128)(2,1)S(1)} %get-tuple-element.41.spectrum_ref, bf16[4,2,256,384]{3,2,1,0:T(8,128)(2,1)S(1)} %get-tuple-element.42.left_ref, ...), custom_call_target="tpu_custom_call" | custom-call | flops 2147483648 | bytes 4194304 | tf_op jit(solution)/shard_map/pallas_call | solution.py:503
  37.5 0.6 %collective-permute-start.9 = (f32[128,128]{1,0:T(8,128)S(1)}, f32[128,128]{1,0:T(8,128)S(1)}, u32[]{:S(2)}, u32[]{:S(2)}) collective-permute-start(f32[128,128]{1,0:T(8,128)S(1)} %get-tuple-element.52), channel_id=1, source_target_pairs={{0,1},{1,0},{2,3},{3,2},{4,5},{5,4},{6,7},{7,6},{8,9},{9,8},{10,11... | collective-permute-start | bytes 196616 | tf_op jit(solution)/shard_map/ppermute | solution.py:409
  38.1 3.1 %shard_map.89 = (f32[128,128]{1,0:T(8,128)S(1)}, f32[128,128]{1,0:T(8,128)S(1)}, f32[128,128]{1,0:T(8,128)S(1)}, f32[128,128]{1,0:T(8,128)S(1)}) custom-call(bf16[2,384,768]{2,1,0:T(8,128)(2,1)S(1)} %get-tuple-element.41.spectrum_ref, bf16[4,2,256,384]{3,2,1,0:T(8,128)(2,1)S(1)} %get-tuple-element.42.left_ref, ...), custom_call_target="tpu_custom_call" | custom-call | flops 2147483648 | bytes 4194304 | tf_op jit(solution)/shard_map/pallas_call | solution.py:503
  41.2 1.7 %collective-permute-start.10 = (f32[128,128]{1,0:T(8,128)S(1)}, f32[128,128]{1,0:T(8,128)S(1)}, u32[]{:S(2)}, u32[]{:S(2)}) collective-permute-start(f32[128,128]{1,0:T(8,128)S(1)} %get-tuple-element.53), channel_id=1, source_target_pairs={{0,2},{1,3},{2,0},{3,1},{4,6},{5,7},{6,4},{7,5},{8,10},{9,11},{10,... | collective-permute-start | bytes 196616 | tf_op jit(solution)/shard_map/ppermute | solution.py:409
  42.9 0.0 collective-permute-start.11
  42.9 0.5 collective-permute-start.6
  43.4 1.6 %collective-permute-start.7 = (f32[128,128]{1,0:T(8,128)S(1)}, f32[128,128]{1,0:T(8,128)S(1)}, u32[]{:S(2)}, u32[]{:S(2)}) collective-permute-start(f32[128,128]{1,0:T(8,128)S(1)} %get-tuple-element.49), channel_id=1, source_target_pairs={{0,2},{1,3},{2,0},{3,1},{4,6},{5,7},{6,4},{7,5},{8,10},{9,11},{10,... | collective-permute-start | bytes 196616 | tf_op jit(solution)/shard_map/ppermute | solution.py:409
  45.0 0.0 collective-permute-done.9.refs_5_
  45.0 0.0 collective-permute-start.8
  45.0 0.5 collective-permute-done.10.refs_6_
  45.5 1.8 %collective-permute-done.11.refs_7_ = f32[128,128]{1,0:T(8,128)S(1)} collective-permute-done((f32[128,128]{1,0:T(8,128)S(1)}, f32[128,128]{1,0:T(8,128)S(1)}, u32[]{:S(2)}, u32[]{:S(2)}) %collective-permute-start.11) | collective-permute-done | bytes 65568 | tf_op jit(solution)/shard_map/ppermute | solution.py:409
  47.3 0.0 collective-permute-done.6.refs_1_
  47.3 1.2 %collective-permute-done.7.refs_2_ = f32[128,128]{1,0:T(8,128)S(1)} collective-permute-done((f32[128,128]{1,0:T(8,128)S(1)}, f32[128,128]{1,0:T(8,128)S(1)}, u32[]{:S(2)}, u32[]{:S(2)}) %collective-permute-start.7) | collective-permute-done | bytes 65568 | tf_op jit(solution)/shard_map/ppermute | solution.py:409
  48.5 1.5 %collective-permute-done.8.refs_3_ = f32[128,128]{1,0:T(8,128)S(1)} collective-permute-done((f32[128,128]{1,0:T(8,128)S(1)}, f32[128,128]{1,0:T(8,128)S(1)}, u32[]{:S(2)}, u32[]{:S(2)}) %collective-permute-start.8) | collective-permute-done | bytes 65568 | tf_op jit(solution)/shard_map/ppermute | solution.py:409
  50.0 0.6 %shard_map.91 = (f32[32,32,128]{2,1,0:T(8,128)S(1)}, f32[32,128]{1,0:T(8,128)S(1)}) custom-call(f32[64,32]{1,0:T(8,128)S(1)} %get-tuple-element.31.weights_ref, f32[128,128]{1,0:T(8,128)S(1)} %get-tuple-element.47.refs_0_, f32[128,128]{1,0:T(8,128)S(1)} %collective-permute-done.6.refs_1_, f32[128,128]{1,0:T(8,128)S(1)} %collective-permute-done.7.refs_2_, ...), custom_call_target="tpu_custom_call" | custom-call | flops 67108864 | bytes 2097152 | tf_op jit(solution)/shard_map/pallas_call | solution.py:514
  50.6 0.6 %collective-permute-start.14 = (f32[32,128]{1,0:T(8,128)S(1)}, f32[32,128]{1,0:T(8,128)S(1)}, u32[]{:S(2)}, u32[]{:S(2)}) collective-permute-start(f32[32,128]{1,0:T(8,128)S(1)} %get-tuple-element.56.refs_0_), channel_id=1, source_target_pairs={{0,3},{1,2},{2,1},{3,0},{4,7},{5,6},{6,5},{7,4},{8,11},{9,10},{10,... | collective-permute-start | bytes 49160 | tf_op jit(solution)/shard_map/ppermute | solution.py:409
  51.2 1.1 %collective-permute-start.13 = (f32[32,128]{1,0:T(8,128)S(1)}, f32[32,128]{1,0:T(8,128)S(1)}, u32[]{:S(2)}, u32[]{:S(2)}) collective-permute-start(f32[32,128]{1,0:T(8,128)S(1)} %get-tuple-element.56.refs_0_), channel_id=1, source_target_pairs={{0,2},{1,3},{2,0},{3,1},{4,6},{5,7},{6,4},{7,5},{8,10},{9,11},{10,... | collective-permute-start | bytes 49160 | tf_op jit(solution)/shard_map/ppermute | solution.py:409
  52.3 0.2 collective-permute-start.12
  52.5 1.3 %collective-permute-done.14.refs_3_ = f32[32,128]{1,0:T(8,128)S(1)} collective-permute-done((f32[32,128]{1,0:T(8,128)S(1)}, f32[32,128]{1,0:T(8,128)S(1)}, u32[]{:S(2)}, u32[]{:S(2)}) %collective-permute-start.14) | collective-permute-done | bytes 16416 | tf_op jit(solution)/shard_map/ppermute | solution.py:409
  53.8 1.2 %collective-permute-done.13.refs_2_ = f32[32,128]{1,0:T(8,128)S(1)} collective-permute-done((f32[32,128]{1,0:T(8,128)S(1)}, f32[32,128]{1,0:T(8,128)S(1)}, u32[]{:S(2)}, u32[]{:S(2)}) %collective-permute-start.13) | collective-permute-done | bytes 16416 | tf_op jit(solution)/shard_map/ppermute | solution.py:409
  54.9 0.0 collective-permute-done.12.refs_1_
  54.9 0.8 %shard_map.92 = f32[32,32,128]{2,1,0:T(8,128)} custom-call(f32[32,32,128]{2,1,0:T(8,128)S(1)} %get-tuple-element.55.intensity_ref, f32[32,128]{1,0:T(8,128)S(1)} %get-tuple-element.56.refs_0_, f32[32,128]{1,0:T(8,128)S(1)} %collective-permute-done.12.refs_1_, f32[32,128]{1,0:T(8,128)S(1)} %collective-permute-done.13.refs_2_, ...), custom_call_target="tpu_custom_call" | custom-call | flops 262144 | bytes 1048576 | tf_op jit(solution)/shard_map/pallas_call | solution.py:529
Async XLA Ops:
  0.0 0.9 %copy-start.2 = (f32[2,32,512]{2,1,0:T(8,128)S(1)}, f32[2,32,512]{2,1,0:T(8,128)}, u32[]{:S(2)}) copy-start(f32[2,32,512]{2,1,0:T(8,128)} %potential_hbm.1) | copy-start | bytes 393220
  0.9 0.7 %copy-start.3 = (s32[2]{0:T(128)S(1)}, s32[2]{0:T(128)}, u32[]{:S(2)}) copy-start(s32[2]{0:T(128)} %anchor_hbm.3) | copy-start | bytes 28
  2.2 9.8 %collective-permute-start.1 = (f32[40,512]{1,0:T(8,128)S(1)}, f32[40,512]{1,0:T(8,128)S(1)}, u32[]{:S(2)}, u32[]{:S(2)}) collective-permute-start(f32[40,512]{1,0:T(8,128)S(1)} %get-tuple-element.32.refs_0_), channel_id=1, source_target_pairs={{0,8},{1,9},{2,10},{3,11},{4,12},{5,13},{6,14},{7,15},{8,0},{9,1},... | collective-permute-start | bytes 245768 | tf_op jit(solution)/shard_map/ppermute | solution.py:409
  6.3 6.7 %collective-permute-start.2 = (f32[40,512]{1,0:T(8,128)S(1)}, f32[40,512]{1,0:T(8,128)S(1)}, u32[]{:S(2)}, u32[]{:S(2)}) collective-permute-start(f32[40,512]{1,0:T(8,128)S(1)} %get-tuple-element.33), channel_id=1, source_target_pairs={{0,12},{1,13},{2,14},{3,15},{4,8},{5,9},{6,10},{7,11},{8,4},{9,5},... | collective-permute-start | bytes 245768 | tf_op jit(solution)/shard_map/ppermute | solution.py:409
  7.7 5.8 %collective-permute-start = (f32[40,512]{1,0:T(8,128)S(1)}, f32[40,512]{1,0:T(8,128)S(1)}, u32[]{:S(2)}, u32[]{:S(2)}) collective-permute-start(f32[40,512]{1,0:T(8,128)S(1)} %get-tuple-element.33), channel_id=1, source_target_pairs={{0,4},{1,5},{2,6},{3,7},{4,0},{5,1},{6,2},{7,3},{8,12},{9,13},{10,... | collective-permute-start | bytes 245768 | tf_op jit(solution)/shard_map/ppermute | solution.py:409
  14.1 7.4 %collective-permute-start.4 = (f32[136,512]{1,0:T(8,128)S(1)}, f32[136,512]{1,0:T(8,128)S(1)}, u32[]{:S(2)}, u32[]{:S(2)}) collective-permute-start(f32[136,512]{1,0:T(8,128)S(1)} %shard_map.84.refs_0_), channel_id=1, source_target_pairs={{0,2},{1,3},{2,0},{3,1},{4,6},{5,7},{6,4},{7,5},{8,10},{9,11},{10,... | collective-permute-start | bytes 835592 | tf_op jit(solution)/shard_map/ppermute | solution.py:409
  15.9 15.7 %collective-permute-start.3 = (f32[136,512]{1,0:T(8,128)S(1)}, f32[136,512]{1,0:T(8,128)S(1)}, u32[]{:S(2)}, u32[]{:S(2)}) collective-permute-start(f32[136,512]{1,0:T(8,128)S(1)} %shard_map.84.refs_0_), channel_id=1, source_target_pairs={{0,1},{1,0},{2,3},{3,2},{4,5},{5,4},{6,7},{7,6},{8,9},{9,8},{10,11... | collective-permute-start | bytes 835592 | tf_op jit(solution)/shard_map/ppermute | solution.py:409
  21.5 10.9 %collective-permute-start.5 = (f32[136,512]{1,0:T(8,128)S(1)}, f32[136,512]{1,0:T(8,128)S(1)}, u32[]{:S(2)}, u32[]{:S(2)}) collective-permute-start(f32[136,512]{1,0:T(8,128)S(1)} %collective-permute-done.4.refs_0_), channel_id=1, source_target_pairs={{0,1},{1,0},{2,3},{3,2},{4,5},{5,4},{6,7},{7,6},{8,9},{9,8},{10,11... | collective-permute-start | bytes 835592 | tf_op jit(solution)/shard_map/ppermute | solution.py:409
  21.5 0.7 %copy-start.4 = (s32[4,32,2]{1,2,0:T(2,128)S(1)}, s32[4,32,2]{1,2,0:T(2,128)}, u32[]{:S(2)}) copy-start(s32[4,32,2]{1,2,0:T(2,128)} %param.12) | copy-start | bytes 3076
  22.2 0.7 %copy-start.5 = (s32[16,2]{0,1:T(2,128)S(1)}, s32[16,2]{0,1:T(2,128)}, u32[]{:S(2)}) copy-start(s32[16,2]{0,1:T(2,128)} %param.9) | copy-start | bytes 388
  22.9 0.7 %copy-start.6 = (f32[16]{0:T(128)S(1)}, f32[16]{0:T(128)}, u32[]{:S(2)}) copy-start(f32[16]{0:T(128)} %refs_2_.1) | copy-start | bytes 196
  23.5 0.7 %copy-start.7 = (f32[16]{0:T(128)S(1)}, f32[16]{0:T(128)}, u32[]{:S(2)}) copy-start(f32[16]{0:T(128)} %refs_3_.1) | copy-start | bytes 196
  28.3 1.2 %copy-start = (bf16[2,2,256,512]{3,2,1,0:T(8,128)(2,1)S(1)}, bf16[2,2,256,512]{3,2,1,0:T(8,128)(2,1)}, u32[]{:S(2)}) copy-start(bf16[2,2,256,512]{3,2,1,0:T(8,128)(2,1)} %constant.4.clone.refs_1_.refs_7_) | copy-start | bytes 3145732
  29.5 1.2 %copy-start.1 = (bf16[2,2,256,512]{3,2,1,0:T(8,128)(2,1)S(1)}, bf16[2,2,256,512]{3,2,1,0:T(8,128)(2,1)}, u32[]{:S(2)}) copy-start(bf16[2,2,256,512]{3,2,1,0:T(8,128)(2,1)} %constant.4.clone.refs_1_.refs_7_) | copy-start | bytes 3145732
  32.5 1.9 %copy-start.8 = (bf16[1,2,128,256]{3,2,1,0:T(8,128)(2,1)S(1)}, bf16[1,2,128,256]{3,2,1,0:T(8,128)(2,1)}, u32[]{:S(2)}) copy-start(bf16[1,2,128,256]{3,2,1,0:T(8,128)(2,1)} %constant.5.clone.last_x_ref) | copy-start | bytes 393220
  37.5 7.5 %collective-permute-start.9 = (f32[128,128]{1,0:T(8,128)S(1)}, f32[128,128]{1,0:T(8,128)S(1)}, u32[]{:S(2)}, u32[]{:S(2)}) collective-permute-start(f32[128,128]{1,0:T(8,128)S(1)} %get-tuple-element.52), channel_id=1, source_target_pairs={{0,1},{1,0},{2,3},{3,2},{4,5},{5,4},{6,7},{7,6},{8,9},{9,8},{10,11... | collective-permute-start | bytes 196616 | tf_op jit(solution)/shard_map/ppermute | solution.py:409
  41.2 4.3 %collective-permute-start.10 = (f32[128,128]{1,0:T(8,128)S(1)}, f32[128,128]{1,0:T(8,128)S(1)}, u32[]{:S(2)}, u32[]{:S(2)}) collective-permute-start(f32[128,128]{1,0:T(8,128)S(1)} %get-tuple-element.53), channel_id=1, source_target_pairs={{0,2},{1,3},{2,0},{3,1},{4,6},{5,7},{6,4},{7,5},{8,10},{9,11},{10,... | collective-permute-start | bytes 196616 | tf_op jit(solution)/shard_map/ppermute | solution.py:409
  42.9 4.4 %collective-permute-start.11 = (f32[128,128]{1,0:T(8,128)S(1)}, f32[128,128]{1,0:T(8,128)S(1)}, u32[]{:S(2)}, u32[]{:S(2)}) collective-permute-start(f32[128,128]{1,0:T(8,128)S(1)} %get-tuple-element.54), channel_id=1, source_target_pairs={{0,3},{1,2},{2,1},{3,0},{4,7},{5,6},{6,5},{7,4},{8,11},{9,10},{10,... | collective-permute-start | bytes 196616 | tf_op jit(solution)/shard_map/ppermute | solution.py:409
  42.9 4.4 %collective-permute-start.6 = (f32[128,128]{1,0:T(8,128)S(1)}, f32[128,128]{1,0:T(8,128)S(1)}, u32[]{:S(2)}, u32[]{:S(2)}) collective-permute-start(f32[128,128]{1,0:T(8,128)S(1)} %get-tuple-element.48), channel_id=1, source_target_pairs={{0,1},{1,0},{2,3},{3,2},{4,5},{5,4},{6,7},{7,6},{8,9},{9,8},{10,11... | collective-permute-start | bytes 196616 | tf_op jit(solution)/shard_map/ppermute | solution.py:409
  43.4 5.1 %collective-permute-start.7 = (f32[128,128]{1,0:T(8,128)S(1)}, f32[128,128]{1,0:T(8,128)S(1)}, u32[]{:S(2)}, u32[]{:S(2)}) collective-permute-start(f32[128,128]{1,0:T(8,128)S(1)} %get-tuple-element.49), channel_id=1, source_target_pairs={{0,2},{1,3},{2,0},{3,1},{4,6},{5,7},{6,4},{7,5},{8,10},{9,11},{10,... | collective-permute-start | bytes 196616 | tf_op jit(solution)/shard_map/ppermute | solution.py:409
  45.0 5.0 %collective-permute-start.8 = (f32[128,128]{1,0:T(8,128)S(1)}, f32[128,128]{1,0:T(8,128)S(1)}, u32[]{:S(2)}, u32[]{:S(2)}) collective-permute-start(f32[128,128]{1,0:T(8,128)S(1)} %get-tuple-element.50), channel_id=1, source_target_pairs={{0,3},{1,2},{2,1},{3,0},{4,7},{5,6},{6,5},{7,4},{8,11},{9,10},{10,... | collective-permute-start | bytes 196616 | tf_op jit(solution)/shard_map/ppermute | solution.py:409
  50.6 3.2 %collective-permute-start.14 = (f32[32,128]{1,0:T(8,128)S(1)}, f32[32,128]{1,0:T(8,128)S(1)}, u32[]{:S(2)}, u32[]{:S(2)}) collective-permute-start(f32[32,128]{1,0:T(8,128)S(1)} %get-tuple-element.56.refs_0_), channel_id=1, source_target_pairs={{0,3},{1,2},{2,1},{3,0},{4,7},{5,6},{6,5},{7,4},{8,11},{9,10},{10,... | collective-permute-start | bytes 49160 | tf_op jit(solution)/shard_map/ppermute | solution.py:409
  51.2 3.7 %collective-permute-start.13 = (f32[32,128]{1,0:T(8,128)S(1)}, f32[32,128]{1,0:T(8,128)S(1)}, u32[]{:S(2)}, u32[]{:S(2)}) collective-permute-start(f32[32,128]{1,0:T(8,128)S(1)} %get-tuple-element.56.refs_0_), channel_id=1, source_target_pairs={{0,2},{1,3},{2,0},{3,1},{4,6},{5,7},{6,4},{7,5},{8,10},{9,11},{10,... | collective-permute-start | bytes 49160 | tf_op jit(solution)/shard_map/ppermute | solution.py:409
  52.3 2.7 %collective-permute-start.12 = (f32[32,128]{1,0:T(8,128)S(1)}, f32[32,128]{1,0:T(8,128)S(1)}, u32[]{:S(2)}, u32[]{:S(2)}) collective-permute-start(f32[32,128]{1,0:T(8,128)S(1)} %get-tuple-element.56.refs_0_), channel_id=1, source_target_pairs={{0,1},{1,0},{2,3},{3,2},{4,5},{5,4},{6,7},{7,6},{8,9},{9,8},{10,11... | collective-permute-start | bytes 49160 | tf_op jit(solution)/shard_map/ppermute | solution.py:409

commit v4 on v3

--- a/solution.py
+++ b/solution.py
@@ -53,8 +53,7 @@
 
 
 def cis_index(index, period):
-    part = ((index + period // 2) & (period - 1)) - period // 2
-    return cis_part(part.astype(jnp.float32) * (1.0 / period))
+    return cis_turns(index.astype(jnp.float32) * (1.0 / period))
 
 
 def mul(a, b):
@@ -90,7 +89,10 @@
         self.per_side = CROP // TILE
         self.tiles = self.per_side * self.per_side
         self.group = devices // self.tiles
-        self.own = beam_count // self.group
+        self.share = 1
+        while self.share < self.group and beam_count // self.share > 8:
+            self.share *= 2
+        self.own = beam_count // self.share
         self.out_rows = self.tiles * TILE // devices
         self.span = self.group * self.rows
         self.half = self.length // 2
@@ -196,82 +198,107 @@
     return np.stack(out), last[None]
 
 
-def tables_kernel(sizes, probes, halves, *refs):
-    sources, refs = refs[:5], refs[5:]
-    (rows_ref, left_ref, right_ref, mask_ref, last_y_ref, weights_ref), refs = refs[:6], refs[6:]
-    fetch(tuple(zip(sources, refs[:5])), refs[5])
-    anchor_ref, tilts_ref, aperture_ref, aberration_ref, spots_ref = refs[:5]
+def whole(value):
+    return value.astype(jnp.float32)
+
+
+def early_tables_kernel(sizes, probes, halves, anchor_hbm, small_hbm, *refs):
+    (rows_ref, left_ref, last_y_ref, incident_ref, weights_ref), (anchor_ref, small_ref, spots_ref, sem_ref) = refs[:5], refs[5:]
+    fetch(((anchor_hbm, anchor_ref), (small_hbm, small_ref), (small_hbm, spots_ref)), sem_ref)
     tile, member, anchor_row, anchor_col = sizes.anchors(anchor_ref)
     half, kept, freqs, length = sizes.half, sizes.kept, sizes.freqs, sizes.length
-    place = sizes.grid_row(iota((1, half), 1), tile, member)
+    place = whole(sizes.grid_row(iota((1, half), 1), tile, member))
     step = cis_index(-place, length)
     for top in range(0, kept, STRIP):
-        freq = 2 * (iota((STRIP, 1), 0) + top) - kept
+        freq = whole(2 * (iota((STRIP, 1), 0) + top) - kept)
         pair = cis_index(-freq * place, length)
         for parity in range(2):
             for part in range(2):
                 put(rows_ref, parity, pair[part], part * kept + top, 0)
-            pair = mul(pair, step)
+            if parity == 0:
+                pair = mul(pair, step)
     scale = 1.0 / (length * length)
-    freq_lane = sizes.frequency(iota((1, freqs), 1))
-    spot_x = anchor_col + iota((1, TILE), 1)
-    limit = (length * length + 8) // 9
-    beams = [member * sizes.own + b for b in range(sizes.own)]
-    tilt_y = [tilts_ref[0, beam] for beam in beams]
-    tilt_x = [tilts_ref[1, beam] for beam in beams]
+    freq_lane = whole(sizes.frequency(iota((1, freqs), 1)))
+    beams = [(member % sizes.share) * sizes.own + b for b in range(sizes.own)]
+    tilt_y = [small_ref[0, beam] for beam in beams]
+    tilt_x = [small_ref[1, beam] for beam in beams]
     chirps = []
     for t in tilt_y:
         ky = freq_lane + t
-        chirps.append(cis_index(-ky * ky, 2 * length))
+        chirps.append([value * scale for value in cis_index(-ky * ky, 2 * length)])
+    lane = iota((1, TILE), 1)
+    packed = jnp.zeros((1, TILE), jnp.float32)
+    for b, t in enumerate(tilt_y):
+        packed = jnp.where(lane == b, t, packed)
+    spot_x = whole(anchor_col + lane)
+    starts = [cis_index(t * spot_x, length) for t in tilt_x]
     for top in range(0, TILE, STRIP):
-        spot_y = anchor_row + sizes.tile_row(iota((STRIP, 1), 0) + top, member, anchor_row)
-        common = [value * scale for value in cis_index(freq_lane * spot_y, length)]
+        spot_y = whole(anchor_row + sizes.tile_row(iota((STRIP, 1), 0) + top, member, anchor_row))
+        common = cis_index(freq_lane * spot_y, length)
+        turn = cis_index(packed * spot_y, length)
         for b in range(sizes.own):
-            pair = mul(mul(common, chirps[b]), cis_index(tilt_y[b] * spot_y, length))
+            pair = mul(common, chirps[b])
+            side = mul((turn[0][:, b:b + 1], turn[1][:, b:b + 1]), starts[b])
             for part in range(2):
                 put(left_ref, b, pair[part], part * TILE + top, 0)
-    starts = [cis_index(t * spot_x, length) for t in tilt_x]
-    squares = []
-    for t in tilt_x:
-        kx = freq_lane + t
-        squares.append(limit - kx * kx)
-    for top in range(0, freqs, STRIP):
-        freq_row = sizes.frequency(iota((STRIP, 1), 0) + top)
-        common = cis_index(freq_row * spot_x, length)
-        for b in range(sizes.own):
-            kx = freq_row + tilt_x[b]
-            pair = mul(mul(common, cis_index(-kx * kx, 2 * length)), starts[b])
-            for part in range(2):
-                put(right_ref, b, pair[part], top, part * TILE)
-            ky = freq_row + tilt_y[b]
-            mask_ref[b, top:top + STRIP] = jnp.where(ky * ky < squares[b], 1.0, 0.0).astype(jnp.bfloat16)
+                incident_ref[b, part, top:top + STRIP] = side[part]
     shape = (TILE, TILE)
-    pair = cis_index(-iota(shape, 0) * sizes.tile_row(iota((1, TILE), 1), member, anchor_row), TILE)
+    pair = cis_index(
+        -whole(iota(shape, 0)) * whole(sizes.tile_row(iota((1, TILE), 1), member, anchor_row)), TILE
+    )
     for part in range(2):
         put(last_y_ref, 0, pair[part], part * TILE, 0)
     some = sizes.own // halves
     lane = iota((1, 2 * sizes.beams), 1)
     beam = (
-        (member ^ ((lane // (2 * some)) % sizes.group)) * sizes.own
-        + some * (lane // (2 * some * sizes.group))
+        ((member % sizes.share) ^ ((lane // (2 * some)) % sizes.share)) * sizes.own
+        + some * (lane // (2 * some * sizes.share))
         + (lane // 2) % some
     )
-    tilt_y, tilt_x = jnp.zeros_like(lane), jnp.zeros_like(lane)
-    amplitude, phase = jnp.zeros(lane.shape, jnp.float32), jnp.zeros(lane.shape, jnp.float32)
+    zero = jnp.zeros(lane.shape, jnp.float32)
+    picked = [zero] * 4
     for b in range(sizes.beams):
         here = beam == b
-        tilt_y = jnp.where(here, tilts_ref[0, b], tilt_y)
-        tilt_x = jnp.where(here, tilts_ref[1, b], tilt_x)
-        amplitude = jnp.where(here, aperture_ref[b], amplitude)
-        phase = jnp.where(here, aberration_ref[b], phase)
-    spots = jnp.transpose(jnp.concatenate((spots_ref[tile], jnp.zeros((6, probes), jnp.int32)), 0))
-    index = (
-        (anchor_row + spots[:, 0:1]) * tilt_y + (anchor_col + spots[:, 1:2]) * tilt_x
-    ) & (length - 1)
-    cosine, sine = cis_turns(phase * (0.5 / np.pi) - index.astype(jnp.float32) * (1.0 / length))
+        picked = [jnp.where(here, small_ref[n, b], value) for n, value in enumerate(picked)]
+    spots = spots_ref[pl.ds(4 + 2 * tile, 2), :probes]
+    spots = jnp.transpose(jnp.concatenate((spots, jnp.zeros((6, probes), jnp.float32)), 0))
+    index = (whole(anchor_row) + spots[:, 0:1]) * picked[0] + (whole(anchor_col) + spots[:, 1:2]) * picked[1]
+    index = index * (1.0 / length)
+    index = index - jnp.floor(index)
+    cosine, sine = cis_turns(picked[3] * (0.5 / np.pi) - index)
     even = lane % 2 == 0
-    weights_ref[:probes] = amplitude * jnp.where(even, cosine, -sine)
-    weights_ref[probes:] = amplitude * jnp.where(even, sine, cosine)
+    weights_ref[:probes] = picked[2] * jnp.where(even, cosine, -sine)
+    weights_ref[probes:] = picked[2] * jnp.where(even, sine, cosine)
+
+
+def late_tables_kernel(sizes, anchor_hbm, small_hbm, right_ref, mask_ref, anchor_ref, small_ref, sem_ref):
+    fetch(((anchor_hbm, anchor_ref), (small_hbm, small_ref)), sem_ref)
+    _, member, _, anchor_col = sizes.anchors(anchor_ref)
+    freqs, length = sizes.freqs, sizes.length
+    beams = [(member % sizes.share) * sizes.own + b for b in range(sizes.own)]
+    lane = iota((1, TILE), 1)
+    spot_x = whole(anchor_col + lane)
+    packed_x, packed_y = jnp.zeros((1, TILE), jnp.float32), jnp.zeros((1, TILE), jnp.float32)
+    freq_lane = whole(sizes.frequency(iota((1, freqs), 1)))
+    limit = float((length * length + 8) // 9)
+    squares = []
+    for b, beam in enumerate(beams):
+        packed_y = jnp.where(lane == b, small_ref[0, beam], packed_y)
+        packed_x = jnp.where(lane == b, small_ref[1, beam], packed_x)
+        kx = freq_lane + small_ref[1, beam]
+        squares.append(limit - kx * kx)
+    for top in range(0, freqs, STRIP):
+        freq_row = whole(sizes.frequency(iota((STRIP, 1), 0) + top))
+        common = cis_index(freq_row * spot_x, length)
+        kx = freq_row + packed_x
+        chirp = cis_index(-kx * kx, 2 * length)
+        ky = freq_row + packed_y
+        square = ky * ky
+        for b in range(sizes.own):
+            pair = mul(common, (chirp[0][:, b:b + 1], chirp[1][:, b:b + 1]))
+            for part in range(2):
+                put(right_ref, b, pair[part], top, part * TILE)
+            mask_ref[b, top:top + STRIP] = jnp.where(square[:, b:b + 1] < squares[b], 1.0, 0.0).astype(jnp.bfloat16)
 
 
 def spread_block(sizes, block_refs, cols_ref):
@@ -345,45 +372,57 @@
             out_ref[1, parity * kept:(parity + 1) * kept, c * freqs:(c + 1) * freqs] = low
 
 
-def beams_kernel(sizes, first, spectrum_ref, left_ref, right_ref, mask_ref, last_x_ref, last_y_ref, slice_ref, *refs):
+def beams_kernel(sizes, first, spectrum_ref, left_ref, right_ref, mask_ref, last_x_ref, last_y_ref, slice_ref, incident_ref, *refs):
     out_refs, field_ref = refs[:-1], refs[-1]
     freqs = sizes.freqs
     some = field_ref.shape[0] // 2
     member = lax.axis_index("beam").astype(jnp.int32) % sizes.group
-    for b in range(some):
-        mask = mask_ref[first + b]
-        mask = jnp.concatenate((mask, mask), 1)
+    names = range(first, first + some)
+    fields = []
+    for b in names:
+        mask = jnp.concatenate((mask_ref[b], mask_ref[b]), 1)
         masked = (spectrum_ref[0] * mask, spectrum_ref[1] * mask)
-        field = combine(dot3((left_ref[first + b, 0], left_ref[first + b, 1]), masked), TILE, freqs)
-        field = split(jnp.concatenate(field, 0))
-        field = combine(dot3(field, (right_ref[first + b, 0], right_ref[first + b, 1])), TILE, TILE)
-        field = mul(field, (slice_ref[0], slice_ref[1]))
-        field = split(jnp.concatenate(field, 0))
+        field = combine(dot3((left_ref[b, 0], left_ref[b, 1]), masked), TILE, freqs)
+        fields.append(split(jnp.concatenate(field, 0)))
+    ends = []
+    for b, field in zip(names, fields):
+        field = combine(dot3(field, (right_ref[b, 0], right_ref[b, 1])), TILE, TILE)
+        field = mul(field, mul((slice_ref[0], slice_ref[1]), (incident_ref[b, 0], incident_ref[b, 1])))
+        ends.append(split(jnp.concatenate(field, 0)))
+    turned = []
+    for field in ends:
         field = combine(dot3(field, (last_x_ref[0, 0], last_x_ref[0, 1])), TILE, TILE)
-        field = split(jnp.concatenate(field, 1))
+        turned.append(split(jnp.concatenate(field, 1)))
+    for n, field in enumerate(turned):
         field = combine(dot3((last_y_ref[0, 0], last_y_ref[0, 1]), field), TILE, TILE)
         for c in range(2):
-            field_ref[2 * b + c] = field[c]
+            field_ref[2 * n + c] = field[c]
+    rows = sizes.out_rows
+    sets = sizes.group // sizes.share
     for other, out_ref in enumerate(out_refs):
-        start = pl.multiple_of((member ^ other) * sizes.out_rows, sizes.out_rows)
-        for n in range(2 * some):
-            out_ref[n * sizes.out_rows:(n + 1) * sizes.out_rows] = field_ref[n, pl.ds(start, sizes.out_rows), :]
+        for k in range(sets):
+            start = pl.multiple_of((member ^ other ^ (sizes.share * k)) * rows, rows)
+            for n in range(2 * some):
+                out_ref[k, n * rows:(n + 1) * rows] = field_ref[n, pl.ds(start, rows), :]
 
 
 def probes_kernel(sizes, probes, weights_ref, *refs):
     field_refs, (out_ref, sums_ref, fields_ref) = refs[:-3], refs[-3:]
-    count = field_refs[0].shape[0]
+    sets, count = field_refs[0].shape[:2]
     for n, ref in enumerate(field_refs):
-        fields_ref[n * count:(n + 1) * count] = ref[...]
-    inner = fields_ref.shape[0] // sizes.out_rows
+        for k in range(sets):
+            fields_ref[k, n * count:(n + 1) * count] = ref[k]
+    inner = fields_ref.shape[1] // sizes.out_rows
     weights = split(weights_ref[...])
     total = jnp.zeros((probes, TILE), jnp.float32)
-    for row in range(sizes.out_rows):
-        fields = split(fields_ref[pl.ds(row, inner, stride=sizes.out_rows), :])
-        both = dot3(weights, fields)
-        intensity = both[:probes] * both[:probes] + both[probes:] * both[probes:]
-        out_ref[row] = intensity
-        total = total + intensity
+    for k in range(sets):
+        for row in range(sizes.out_rows):
+            fields = split(fields_ref[k, pl.ds(row, inner, stride=sizes.out_rows), :])
+            both = dot3(weights, fields)
+            intensity = both[:probes] * both[:probes] + both[probes:] * both[probes:]
+            if k == 0:
+                out_ref[row] = intensity
+            total = total + intensity
     sums_ref[...] = jnp.broadcast_to(jnp.sum(total, 1, keepdims=True), (probes, TILE))
 
 
@@ -443,27 +482,28 @@
         sent = same if shift % sizes.per_side == 0 else other_side
         blocks.append(swap(sent, shift * group))
     col_table, last_x = (jnp.asarray(table) for table in column_tables(sizes))
-    row_table, left, right, masks, last_y, weights = call(
-        functools.partial(tables_kernel, sizes, probes, halves),
+    small = pack_small(sizes, beam_tilts, aperture, aberration, probe_spots)
+    fetched = [pltpu.SMEM(crop_anchor.shape, jnp.int32), pltpu.SMEM(small.shape, jnp.float32)]
+    row_table, left, last_y, incident, weights = call(
+        functools.partial(early_tables_kernel, sizes, probes, halves),
         (
             half_type(2, 2, 2 * kept, half),
             half_type(own, 2, 2 * TILE, freqs),
-            half_type(own, 2, freqs, 2 * TILE),
-            half_type(own, freqs, freqs),
             half_type(1, 2, 2 * TILE, TILE),
+            full_type(own, 2, TILE, TILE),
             full_type(2 * probes, 2 * sizes.beams),
         ),
-        [HBM] * 5,
-        scratch_shapes=[
-            pltpu.SMEM(crop_anchor.shape, jnp.int32),
-            pltpu.SMEM(beam_tilts.shape[::-1], jnp.int32),
-            pltpu.SMEM(aperture.shape, jnp.float32),
-            pltpu.SMEM(aberration.shape, jnp.float32),
-            pltpu.VMEM((tiles, 2, probes), jnp.int32),
-            pltpu.SemaphoreType.DMA((5,)),
-        ],
+        [HBM] * 2,
+        scratch_shapes=fetched + [pltpu.VMEM(small.shape, jnp.float32), pltpu.SemaphoreType.DMA((3,))],
         cost_estimate=estimate(1 << 22, 6 << 20),
-    )(crop_anchor, beam_tilts.T, aperture, aberration, probe_spots.transpose(0, 2, 1))
+    )(crop_anchor, small)
+    right, masks = call(
+        functools.partial(late_tables_kernel, sizes),
+        (half_type(own, 2, freqs, 2 * TILE), half_type(own, freqs, freqs)),
+        [HBM] * 2,
+        scratch_shapes=fetched + [pltpu.SemaphoreType.DMA((2,))],
+        cost_estimate=estimate(1 << 22, 6 << 20),
+    )(crop_anchor, small)
     held = call(
         functools.partial(hold_kernel, sizes),
         full_type(sizes.block, length),
@@ -499,31 +539,32 @@
     )(*spreads, *pieces, *chunks[-1], col_table, row_table)
 
     arrived = []
+    sets = group // sizes.share
     for h in range(halves):
         fields = call(
             functools.partial(beams_kernel, sizes, h * some),
-            (full_type(2 * some * sizes.out_rows, TILE),) * group,
-            [VMEM] * 7,
+            (full_type(sets, 2 * some * sizes.out_rows, TILE),) * sizes.share,
+            [VMEM] * 8,
             scratch_shapes=[pltpu.VMEM((2 * some, TILE, TILE), jnp.float32)],
             cost_estimate=estimate(some << 30, 4 << 20),
-        )(spectrum, left, right, masks, last_x, last_y, slice_one)
+        )(spectrum, left, right, masks, last_x, last_y, slice_one, incident)
         arrived.append(fields[0])
-        for other in range(1, group):
+        for other in range(1, sizes.share):
             arrived.append(swap(fields[other], other))
 
     intensity, total = call(
         functools.partial(probes_kernel, sizes, probes),
         (full_type(sizes.out_rows, probes, TILE), full_type(probes, TILE)),
         [VMEM] * (1 + len(arrived)),
-        scratch_shapes=[pltpu.VMEM((2 * sizes.beams * sizes.out_rows, TILE), jnp.float32)],
+        scratch_shapes=[pltpu.VMEM((sets, 2 * sizes.beams * sizes.out_rows, TILE), jnp.float32)],
         cost_estimate=estimate(1 << 26, 2 << 20),
     )(weights, *arrived)
     totals = [total]
-    if group <= 4:
-        for other in range(1, group):
+    if sizes.share <= 4:
+        for other in range(1, sizes.share):
             totals.append(swap(total, other))
     else:
-        for bits in member_steps(group):
+        for bits in member_steps(sizes.share):
             total = total + swap(total, bits)
         totals = [total]
     return call(
@@ -534,6 +575,20 @@
     )(intensity, *totals)
 
 
+def pack_small(sizes, beam_tilts, aperture, aberration, probe_spots):
+    probes = probe_spots.shape[1]
+    width = max(sizes.beams, probes)
+    spots = probe_spots.transpose(0, 2, 1).reshape(2 * sizes.tiles, probes).astype(jnp.float32)
+    beams = jnp.concatenate((beam_tilts.T.astype(jnp.float32), aperture[None], aberration[None]), 0)
+    return jnp.concatenate(
+        (
+            jnp.pad(beams, ((0, 0), (0, width - sizes.beams))),
+            jnp.pad(spots, ((0, 0), (0, width - probes))),
+        ),
+        0,
+    )
+
+
 def member_steps(group):
     return [group >> (i + 1) for i in range(group.bit_length() - 1)]
 

time: 56.4 us -> 47 us (0.83)
  waiting for transfers between devices: 18.7 us -> 12.6 us
  starting transfers between devices: 13.7 us -> 8.3 us
  Pallas kernels: 17.4 us -> 19.6 us
  other arithmetic: 0 us -> 2.06 us
  local copies, waits for them, and re-layouts: 5.85 us -> 4.01 us
    ppermute x15 -> x9, waiting for transfers between devices: 18.7 us -> 12.6 us  [swap(): return lax.ppermute(value, 'beam', [(i, i ^ bits) for i in range(devices)])]
    ppermute x15 -> x9, starting transfers between devices: 13.7 us -> 8.3 us  [swap(): return lax.ppermute(value, 'beam', [(i, i ^ bits) for i in range(devices)])]
    pallas_call x3 -> x4, Pallas kernels: 10.4 us -> 12.3 us  [the longest x2 7.19 us: per_device(): call(functools.partial(beams_kernel, sizes, h * some), (full_type(sets, 2...]
    unnamed x18 -> x12, local copies, waits for them, and re-layouts: 5.85 us -> 4.01 us
    convert_element_type x0 -> x2, other arithmetic: none -> 1.37 us  [the longest x1 0.69 us: pack_small(): probe_spots.transpose(0, 2, 1).reshape(2 * sizes.tiles, probes)]
    concatenate x0 -> x2, other arithmetic: none -> 0.69 us  [the longest x1 0.68 us: pack_small(): jnp.concatenate((beam_tilts.T.astype(jnp.float32), aperture[None], aberra...]
  transfers between devices with their start and end apart: 15 -> 9, of which waited for: 10 -> 5; matrix products, arithmetic and copies ran while one was open for 0% -> 4% of each run, Pallas kernels for 17% -> 16%
where the time goes in v4:
time: 47 us; the launch traced here: 46.7 us
  Pallas kernels  19.6 us (42%)
  waiting for transfers between devices  12.6 us (27%)
  starting transfers between devices  8.3 us (18%)
  local copies, waits for them, and re-layouts  4.01 us (9%)
  other arithmetic  2.06 us (4%)
    ppermute x9, waiting for transfers between devices, swap(): return lax.ppermute(value, 'beam', [(i, i ^ bits) for i in range(devices)])  12.6 us
    ppermute x9, starting transfers between devices, swap(): return lax.ppermute(value, 'beam', [(i, i ^ bits) for i in range(devices)])  8.3 us
    pallas_call x2, Pallas kernels, per_device(): call(functools.partial(beams_kernel, sizes, h * some), (full_type(sets, 2...  7.19 us
    unnamed x12, local copies, waits for them, and re-layouts  4.01 us
    pallas_call x1, Pallas kernels, per_device(): call(functools.partial(early_tables_kernel, sizes, probes, halves), (half...  2.6 us
    pallas_call x3, Pallas kernels, per_device(): call(functools.partial(spread_kernel, sizes), (half_type(2, 2, pairs, 2 *...  2.49 us
    pallas_call x1, Pallas kernels, per_device(): call(functools.partial(late_tables_kernel, sizes), (half_type(own, 2, fre...  2.48 us
    pallas_call x1, Pallas kernels, per_device(): call(functools.partial(spectrum_kernel, sizes, len(spreads)), (half_type(...  1.89 us
  transfers between devices with their start and end apart: 9, of which 5 were waited for; matrix products, arithmetic and copies ran while one was open for 4% of the time, Pallas kernels for 16%

profile of v4, /device:TPU:0, one launch (start us, length us, event | category | flops | bytes accessed | tf_op | source)
XLA Modules:
  0.0 46.7 jit_solution(5045641217219441203)
XLA Ops:
  0.0 0.0 copy-start.3
  0.0 0.9 %copy-done.3 = f32[2,32,512]{2,1,0:T(8,128)S(1)} copy-done((f32[2,32,512]{2,1,0:T(8,128)S(1)}, f32[2,32,512]{2,1,0:T(8,128)}, u32[]{:S(2)}) %copy-start.3) | copy-done | bytes 131096
  0.9 0.0 copy-start.4
  0.9 0.7 %copy-done.4 = s32[2]{0:T(128)S(1)} copy-done((s32[2]{0:T(128)S(1)}, s32[2]{0:T(128)}, u32[]{:S(2)}) %copy-start.4) | copy-done | bytes 32
  1.6 0.6 %shard_map.83 = (f32[40,512]{1,0:T(8,128)S(1)}, f32[40,512]{1,0:T(8,128)S(1)}) custom-call(s32[2]{0:T(128)S(1)} %copy-done.4, f32[2,32,512]{2,1,0:T(8,128)S(1)} %copy-done.3), custom_call_target="tpu_custom_call" | custom-call | flops 65536 | bytes 262144 | tf_op jit(solution)/shard_map/pallas_call | solution.py:469
  2.2 3.1 %collective-permute-start = (f32[40,512]{1,0:T(8,128)S(1)}, f32[40,512]{1,0:T(8,128)S(1)}, u32[]{:S(2)}, u32[]{:S(2)}) collective-permute-start(f32[40,512]{1,0:T(8,128)S(1)} %get-tuple-element.30), channel_id=1, source_target_pairs={{0,4},{1,5},{2,6},{3,7},{4,0},{5,1},{6,2},{7,3},{8,12},{9,13},{10,... | collective-permute-start | bytes 245768 | tf_op jit(solution)/shard_map/ppermute | solution.py:448
  5.3 2.6 %collective-permute-start.1 = (f32[40,512]{1,0:T(8,128)S(1)}, f32[40,512]{1,0:T(8,128)S(1)}, u32[]{:S(2)}, u32[]{:S(2)}) collective-permute-start(f32[40,512]{1,0:T(8,128)S(1)} %get-tuple-element.29.refs_0_), channel_id=1, source_target_pairs={{0,8},{1,9},{2,10},{3,11},{4,12},{5,13},{6,14},{7,15},{8,0},{9,1},... | collective-permute-start | bytes 245768 | tf_op jit(solution)/shard_map/ppermute | solution.py:448
  7.9 0.0 collective-permute-start.2
  7.9 0.0 collective-permute-done.refs_1_
  7.9 6.6 %collective-permute-done.1.refs_2_ = f32[40,512]{1,0:T(8,128)S(1)} collective-permute-done((f32[40,512]{1,0:T(8,128)S(1)}, f32[40,512]{1,0:T(8,128)S(1)}, u32[]{:S(2)}, u32[]{:S(2)}) %collective-permute-start.1) | collective-permute-done | bytes 81952 | tf_op jit(solution)/shard_map/ppermute | solution.py:448
  14.5 0.0 collective-permute-done.2.refs_3_
  14.5 0.6 %shard_map.84.refs_0_ = f32[136,512]{1,0:T(8,128)S(1)} custom-call(s32[2]{0:T(128)S(1)} %copy-done.4, f32[40,512]{1,0:T(8,128)S(1)} %get-tuple-element.29.refs_0_, f32[40,512]{1,0:T(8,128)S(1)} %collective-permute-done.refs_1_, f32[40,512]{1,0:T(8,128)S(1)} %collective-permute-done.1.refs_2_, f32[40,512]{1,0:T(8,128)S(1)} %collective-permute-done.2.refs_3_), custom_call_target="tpu_custom_call" | custom-call | flops 65536 | bytes 524288 | tf_op jit(solution)/shard_map/pallas_call | solution.py:507
  15.1 1.6 %collective-permute-start.4 = (f32[136,512]{1,0:T(8,128)S(1)}, f32[136,512]{1,0:T(8,128)S(1)}, u32[]{:S(2)}, u32[]{:S(2)}) collective-permute-start(f32[136,512]{1,0:T(8,128)S(1)} %shard_map.84.refs_0_), channel_id=1, source_target_pairs={{0,2},{1,3},{2,0},{3,1},{4,6},{5,7},{6,4},{7,5},{8,10},{9,11},{10,... | collective-permute-start | bytes 835592 | tf_op jit(solution)/shard_map/ppermute | solution.py:448
  16.7 0.0 collective-permute-start.3
  16.7 0.7 %convert_bitcast_fusion = f32[2,16]{1,0:T(2,128)S(1)} fusion(s32[16,2]{0,1:T(2,128)} %param.9), kind=kLoop, calls=%fused_computation.4 | loop fusion | flops 32 | bytes 256 | tf_op jit(solution)/shard_map/convert_element_type | solution.py:582
  17.4 0.7 %convert_element_type.19 = f32[4,32,2]{1,2,0:T(2,128)S(1)} convert(s32[4,32,2]{1,2,0:T(2,128)} %param.12) | non-fusion elementwise | flops 256 | bytes 2048 | tf_op jit(solution)/shard_map/convert_element_type | solution.py:581
  18.1 3.7 %collective-permute-done.4.refs_0_ = f32[136,512]{1,0:T(8,128)S(1)} collective-permute-done((f32[136,512]{1,0:T(8,128)S(1)}, f32[136,512]{1,0:T(8,128)S(1)}, u32[]{:S(2)}, u32[]{:S(2)}) %collective-permute-start.4) | collective-permute-done | bytes 278560 | tf_op jit(solution)/shard_map/ppermute | solution.py:448
  21.7 0.0 collective-permute-start.5
  21.7 0.7 %select_maximum_fusion = f32[4,32]{1,0:T(4,128)S(1)} fusion(f32[1,16]{1,0:T(1,128)} %bitcast.8, f32[1,16]{1,0:T(1,128)} %bitcast.9, f32[2,16]{1,0:T(2,128)S(1)} %convert_bitcast_fusion), kind=kLoop, calls=%fused_computation.1 | loop fusion | flops 768 | bytes 768 | tf_op jit(solution)/shard_map/concatenate | solution.py:582
  22.4 2.6 %shard_map.82 = (bf16[2,2,384,256]{3,2,1,0:T(8,128)(2,1)S(1)}, bf16[8,2,256,384]{3,2,1,0:T(8,128)(2,1)S(1)}, bf16[1,2,256,128]{3,2,1,0:T(8,128)(2,1)S(1)}, f32[8,2,128,128]{3,2,1,0:T(8,128)S(1)}, f32[64,32]{1,0:T(8,128)S(1)}) custom-call(s32[2]{0:T(128)S(1)} %copy-done.4, f32[12,32]{1,0:T(8,128)S(1)} %pad_maximum_fusion.small_hbm), custom_call_target="tpu_custom_call" | custom-call | flops 4194304 | bytes 6291456 | tf_op jit(solution)/shard_map/pallas_call | solution.py:487
  25.0 2.5 %shard_map.89 = (bf16[8,2,384,256]{3,2,1,0:T(8,128)(2,1)S(1)}, bf16[8,384,384]{2,1,0:T(8,128)(2,1)S(1)}) custom-call(s32[2]{0:T(128)S(1)} %copy-done.4, f32[12,32]{1,0:T(8,128)S(1)} %pad_maximum_fusion.small_hbm), custom_call_target="tpu_custom_call" | custom-call | flops 4194304 | bytes 6291456 | tf_op jit(solution)/shard_map/pallas_call | solution.py:500
  27.5 0.0 copy-start
  27.5 1.2 %copy-done = bf16[2,2,256,512]{3,2,1,0:T(8,128)(2,1)S(1)} copy-done((bf16[2,2,256,512]{3,2,1,0:T(8,128)(2,1)S(1)}, bf16[2,2,256,512]{3,2,1,0:T(8,128)(2,1)}, u32[]{:S(2)}) %copy-start) | copy-done | bytes 1048600
  28.8 0.0 copy-start.2
  28.8 0.8 %shard_map.85 = (bf16[2,2,64,768]{3,2,1,0:T(8,128)(2,1)S(1)}, f32[8,512]{1,0:T(8,128)S(1)}) custom-call(f32[136,512]{1,0:T(8,128)S(1)} %shard_map.84.refs_0_, bf16[2,2,256,512]{3,2,1,0:T(8,128)(2,1)S(1)} %copy-done), custom_call_target="tpu_custom_call" | custom-call | flops 201326592 | bytes 2097152 | tf_op jit(solution)/shard_map/pallas_call | solution.py:525
  29.6 0.0 copy-start.1
  29.6 1.2 %copy-done.1 = bf16[2,2,256,512]{3,2,1,0:T(8,128)(2,1)S(1)} copy-done((bf16[2,2,256,512]{3,2,1,0:T(8,128)(2,1)S(1)}, bf16[2,2,256,512]{3,2,1,0:T(8,128)(2,1)}, u32[]{:S(2)}) %copy-start.1) | copy-done | bytes 1048600
  30.8 0.8 %shard_map.87 = (bf16[2,2,64,768]{3,2,1,0:T(8,128)(2,1)S(1)}, f32[8,512]{1,0:T(8,128)S(1)}) custom-call(f32[136,512]{1,0:T(8,128)S(1)} %collective-permute-done.4.refs_0_, bf16[2,2,256,512]{3,2,1,0:T(8,128)(2,1)S(1)} %copy-done.1), custom_call_target="tpu_custom_call" | custom-call | flops 201326592 | bytes 2097152 | tf_op jit(solution)/shard_map/pallas_call | solution.py:525
  31.7 0.0 collective-permute-done.3.refs_0_
  31.7 0.8 %shard_map.86 = (bf16[2,2,64,768]{3,2,1,0:T(8,128)(2,1)S(1)}, f32[8,512]{1,0:T(8,128)S(1)}) custom-call(f32[136,512]{1,0:T(8,128)S(1)} %collective-permute-done.3.refs_0_, bf16[2,2,256,512]{3,2,1,0:T(8,128)(2,1)S(1)} %copy-done.1), custom_call_target="tpu_custom_call" | custom-call | flops 201326592 | bytes 2097152 | tf_op jit(solution)/shard_map/pallas_call | solution.py:525
  32.5 0.0 collective-permute-done.5.refs_6_
  32.5 0.0 copy-done.2
  32.5 0.0 copy-start.5
  32.5 1.9 %shard_map.88 = (bf16[2,384,768]{2,1,0:T(8,128)(2,1)S(1)}, f32[2,128,128]{2,1,0:T(8,128)S(1)}) custom-call(bf16[2,2,64,768]{3,2,1,0:T(8,128)(2,1)S(1)} %get-tuple-element.31.refs_0_, bf16[2,2,64,768]{3,2,1,0:T(8,128)(2,1)S(1)} %get-tuple-element.32.refs_1_, bf16[2,2,64,768]{3,2,1,0:T(8,128)(2,1)S(1)} %get-tuple-element.33.refs_2_, ...), custom_call_target="tpu_custom_call" | custom-call | flops 3221225472 | bytes 4194304 | tf_op jit(solution)/shard_map/pallas_call | solution.py:533
  34.4 0.0 copy-done.5
  34.4 3.5 %shard_map.90 = (f32[2,256,128]{2,1,0:T(8,128)S(1)}, f32[2,256,128]{2,1,0:T(8,128)S(1)}) custom-call(bf16[2,384,768]{2,1,0:T(8,128)(2,1)S(1)} %get-tuple-element.38.spectrum_ref, bf16[8,2,256,384]{3,2,1,0:T(8,128)(2,1)S(1)} %get-tuple-element.39.left_ref, bf16[8,2,384,256]{3,2,1,0:T(8,128)(2,1)S(1)} %get-tuple-element.40.right_ref, ...), custom_call_target="tpu_custom_call" | custom-call | flops 4294967296 | bytes 4194304 | tf_op jit(solution)/shard_map/pallas_call | solution.py:544
  37.9 3.7 %shard_map.91 = (f32[2,256,128]{2,1,0:T(8,128)S(1)}, f32[2,256,128]{2,1,0:T(8,128)S(1)}) custom-call(bf16[2,384,768]{2,1,0:T(8,128)(2,1)S(1)} %get-tuple-element.38.spectrum_ref, bf16[8,2,256,384]{3,2,1,0:T(8,128)(2,1)S(1)} %get-tuple-element.39.left_ref, bf16[8,2,384,256]{3,2,1,0:T(8,128)(2,1)S(1)} %get-tuple-element.40.right_ref, ...), custom_call_target="tpu_custom_call" | custom-call | flops 4294967296 | bytes 4194304 | tf_op jit(solution)/shard_map/pallas_call | solution.py:544
  41.7 0.6 %collective-permute-start.6 = (f32[2,256,128]{2,1,0:T(8,128)S(1)}, f32[2,256,128]{2,1,0:T(8,128)S(1)}, u32[]{:S(2)}, u32[]{:S(2)}) collective-permute-start(f32[2,256,128]{2,1,0:T(8,128)S(1)} %get-tuple-element.46), channel_id=1, source_target_pairs={{0,1},{1,0},{2,3},{3,2},{4,5},{5,4},{6,7},{7,6},{8,9},{9,8},{10,11... | collective-permute-start | bytes 786440 | tf_op jit(solution)/shard_map/ppermute | solution.py:448
  42.2 0.1 collective-permute-start.7
  42.3 1.1 %collective-permute-done.6.refs_1_ = f32[2,256,128]{2,1,0:T(8,128)S(1)} collective-permute-done((f32[2,256,128]{2,1,0:T(8,128)S(1)}, f32[2,256,128]{2,1,0:T(8,128)S(1)}, u32[]{:S(2)}, u32[]{:S(2)}) %collective-permute-start.6) | collective-permute-done | bytes 262176 | tf_op jit(solution)/shard_map/ppermute | solution.py:448
  43.4 0.4 collective-permute-done.7.refs_3_
  43.8 0.9 %shard_map.92 = (f32[32,32,128]{2,1,0:T(8,128)S(1)}, f32[32,128]{1,0:T(8,128)S(1)}) custom-call(f32[64,32]{1,0:T(8,128)S(1)} %get-tuple-element.28.weights_ref, f32[2,256,128]{2,1,0:T(8,128)S(1)} %get-tuple-element.45.refs_0_, f32[2,256,128]{2,1,0:T(8,128)S(1)} %collective-permute-done.6.refs_1_, f32[2,256,128]{2,1,0:T(8,128)S(1)} %get-tuple-element.47.refs_2_, ...), custom_call_target="tpu_custom_call" | custom-call | flops 67108864 | bytes 2097152 | tf_op jit(solution)/shard_map/pallas_call | solution.py:555
  44.7 0.4 collective-permute-start.8
  45.1 0.8 %collective-permute-done.8.refs_1_ = f32[32,128]{1,0:T(8,128)S(1)} collective-permute-done((f32[32,128]{1,0:T(8,128)S(1)}, f32[32,128]{1,0:T(8,128)S(1)}, u32[]{:S(2)}, u32[]{:S(2)}) %collective-permute-start.8) | collective-permute-done | bytes 16416 | tf_op jit(solution)/shard_map/ppermute | solution.py:448
  45.9 0.8 %shard_map.93 = f32[32,32,128]{2,1,0:T(8,128)} custom-call(f32[32,32,128]{2,1,0:T(8,128)S(1)} %get-tuple-element.49.intensity_ref, f32[32,128]{1,0:T(8,128)S(1)} %get-tuple-element.50.refs_0_, f32[32,128]{1,0:T(8,128)S(1)} %collective-permute-done.8.refs_1_), custom_call_target="tpu_custom_call" | custom-call | flops 262144 | bytes 1048576 | tf_op jit(solution)/shard_map/pallas_call | solution.py:570
  (1 shorter events, 0.0 us)
Async XLA Ops:
  0.0 0.9 %copy-start.3 = (f32[2,32,512]{2,1,0:T(8,128)S(1)}, f32[2,32,512]{2,1,0:T(8,128)}, u32[]{:S(2)}) copy-start(f32[2,32,512]{2,1,0:T(8,128)} %potential_hbm.1) | copy-start | bytes 393220
  0.9 0.7 %copy-start.4 = (s32[2]{0:T(128)S(1)}, s32[2]{0:T(128)}, u32[]{:S(2)}) copy-start(s32[2]{0:T(128)} %anchor_hbm.7) | copy-start | bytes 28
  2.2 5.7 %collective-permute-start = (f32[40,512]{1,0:T(8,128)S(1)}, f32[40,512]{1,0:T(8,128)S(1)}, u32[]{:S(2)}, u32[]{:S(2)}) collective-permute-start(f32[40,512]{1,0:T(8,128)S(1)} %get-tuple-element.30), channel_id=1, source_target_pairs={{0,4},{1,5},{2,6},{3,7},{4,0},{5,1},{6,2},{7,3},{8,12},{9,13},{10,... | collective-permute-start | bytes 245768 | tf_op jit(solution)/shard_map/ppermute | solution.py:448
  5.3 9.2 %collective-permute-start.1 = (f32[40,512]{1,0:T(8,128)S(1)}, f32[40,512]{1,0:T(8,128)S(1)}, u32[]{:S(2)}, u32[]{:S(2)}) collective-permute-start(f32[40,512]{1,0:T(8,128)S(1)} %get-tuple-element.29.refs_0_), channel_id=1, source_target_pairs={{0,8},{1,9},{2,10},{3,11},{4,12},{5,13},{6,14},{7,15},{8,0},{9,1},... | collective-permute-start | bytes 245768 | tf_op jit(solution)/shard_map/ppermute | solution.py:448
  7.9 6.6 %collective-permute-start.2 = (f32[40,512]{1,0:T(8,128)S(1)}, f32[40,512]{1,0:T(8,128)S(1)}, u32[]{:S(2)}, u32[]{:S(2)}) collective-permute-start(f32[40,512]{1,0:T(8,128)S(1)} %get-tuple-element.30), channel_id=1, source_target_pairs={{0,12},{1,13},{2,14},{3,15},{4,8},{5,9},{6,10},{7,11},{8,4},{9,5},... | collective-permute-start | bytes 245768 | tf_op jit(solution)/shard_map/ppermute | solution.py:448
  15.1 6.6 %collective-permute-start.4 = (f32[136,512]{1,0:T(8,128)S(1)}, f32[136,512]{1,0:T(8,128)S(1)}, u32[]{:S(2)}, u32[]{:S(2)}) collective-permute-start(f32[136,512]{1,0:T(8,128)S(1)} %shard_map.84.refs_0_), channel_id=1, source_target_pairs={{0,2},{1,3},{2,0},{3,1},{4,6},{5,7},{6,4},{7,5},{8,10},{9,11},{10,... | collective-permute-start | bytes 835592 | tf_op jit(solution)/shard_map/ppermute | solution.py:448
  16.7 15.0 %collective-permute-start.3 = (f32[136,512]{1,0:T(8,128)S(1)}, f32[136,512]{1,0:T(8,128)S(1)}, u32[]{:S(2)}, u32[]{:S(2)}) collective-permute-start(f32[136,512]{1,0:T(8,128)S(1)} %shard_map.84.refs_0_), channel_id=1, source_target_pairs={{0,1},{1,0},{2,3},{3,2},{4,5},{5,4},{6,7},{7,6},{8,9},{9,8},{10,11... | collective-permute-start | bytes 835592 | tf_op jit(solution)/shard_map/ppermute | solution.py:448
  21.7 10.8 %collective-permute-start.5 = (f32[136,512]{1,0:T(8,128)S(1)}, f32[136,512]{1,0:T(8,128)S(1)}, u32[]{:S(2)}, u32[]{:S(2)}) collective-permute-start(f32[136,512]{1,0:T(8,128)S(1)} %collective-permute-done.4.refs_0_), channel_id=1, source_target_pairs={{0,1},{1,0},{2,3},{3,2},{4,5},{5,4},{6,7},{7,6},{8,9},{9,8},{10,11... | collective-permute-start | bytes 835592 | tf_op jit(solution)/shard_map/ppermute | solution.py:448
  27.5 1.2 %copy-start = (bf16[2,2,256,512]{3,2,1,0:T(8,128)(2,1)S(1)}, bf16[2,2,256,512]{3,2,1,0:T(8,128)(2,1)}, u32[]{:S(2)}) copy-start(bf16[2,2,256,512]{3,2,1,0:T(8,128)(2,1)} %constant.7.clone.refs_1_.refs_7_) | copy-start | bytes 3145732
  28.8 3.8 %copy-start.2 = (bf16[2,2,256,512]{3,2,1,0:T(8,128)(2,1)S(1)}, bf16[2,2,256,512]{3,2,1,0:T(8,128)(2,1)}, u32[]{:S(2)}) copy-start(bf16[2,2,256,512]{3,2,1,0:T(8,128)(2,1)} %constant.7.clone.refs_1_.refs_7_) | copy-start | bytes 3145732
  29.6 1.2 %copy-start.1 = (bf16[2,2,256,512]{3,2,1,0:T(8,128)(2,1)S(1)}, bf16[2,2,256,512]{3,2,1,0:T(8,128)(2,1)}, u32[]{:S(2)}) copy-start(bf16[2,2,256,512]{3,2,1,0:T(8,128)(2,1)} %constant.7.clone.refs_1_.refs_7_) | copy-start | bytes 3145732
  32.5 1.9 %copy-start.5 = (bf16[1,2,128,256]{3,2,1,0:T(8,128)(2,1)S(1)}, bf16[1,2,128,256]{3,2,1,0:T(8,128)(2,1)}, u32[]{:S(2)}) copy-start(bf16[1,2,128,256]{3,2,1,0:T(8,128)(2,1)} %constant.8.clone.last_x_ref) | copy-start | bytes 393220
  41.7 1.7 %collective-permute-start.6 = (f32[2,256,128]{2,1,0:T(8,128)S(1)}, f32[2,256,128]{2,1,0:T(8,128)S(1)}, u32[]{:S(2)}, u32[]{:S(2)}) collective-permute-start(f32[2,256,128]{2,1,0:T(8,128)S(1)} %get-tuple-element.46), channel_id=1, source_target_pairs={{0,1},{1,0},{2,3},{3,2},{4,5},{5,4},{6,7},{7,6},{8,9},{9,8},{10,11... | collective-permute-start | bytes 786440 | tf_op jit(solution)/shard_map/ppermute | solution.py:448
  42.2 1.5 %collective-permute-start.7 = (f32[2,256,128]{2,1,0:T(8,128)S(1)}, f32[2,256,128]{2,1,0:T(8,128)S(1)}, u32[]{:S(2)}, u32[]{:S(2)}) collective-permute-start(f32[2,256,128]{2,1,0:T(8,128)S(1)} %get-tuple-element.48), channel_id=1, source_target_pairs={{0,1},{1,0},{2,3},{3,2},{4,5},{5,4},{6,7},{7,6},{8,9},{9,8},{10,11... | collective-permute-start | bytes 786440 | tf_op jit(solution)/shard_map/ppermute | solution.py:448
  44.7 1.2 %collective-permute-start.8 = (f32[32,128]{1,0:T(8,128)S(1)}, f32[32,128]{1,0:T(8,128)S(1)}, u32[]{:S(2)}, u32[]{:S(2)}) collective-permute-start(f32[32,128]{1,0:T(8,128)S(1)} %get-tuple-element.50.refs_0_), channel_id=1, source_target_pairs={{0,1},{1,0},{2,3},{3,2},{4,5},{5,4},{6,7},{7,6},{8,9},{9,8},{10,11... | collective-permute-start | bytes 49160 | tf_op jit(solution)/shard_map/ppermute | solution.py:448

commit v5 on v4

--- a/solution.py
+++ b/solution.py
@@ -149,10 +149,11 @@
         copy.wait()
 
 
-def pack_kernel(sizes, anchor_hbm, potential_hbm, same_ref, other_ref, anchor_ref, potential_ref, sem_ref):
-    fetch(((anchor_hbm, anchor_ref), (potential_hbm, potential_ref)), sem_ref)
-    tile = sizes.anchors(anchor_ref)[0]
-    window = pltpu.roll(potential_ref[1], sizes.length - anchor_ref[1], 1)
+def pack_kernel(sizes, anchor_ref, potential_ref, same_ref, other_ref):
+    tile = lax.axis_index("beam").astype(jnp.int32) // sizes.group
+    anchors = anchor_ref[...]
+    column = jnp.sum(jnp.where(iota(anchors.shape, 1) == 1, anchors, 0).astype(jnp.float32)).astype(jnp.int32)
+    window = pltpu.roll(potential_ref[1], sizes.length - column, 1)
     first, second = window[:, :TILE], window[:, TILE:2 * TILE]
     left = tile % sizes.per_side == 0
     rows, step = sizes.rows, sizes.piece_rows
@@ -162,19 +163,15 @@
             ref[rows:, q * TILE:(q + 1) * TILE] = value[q * step:(q + 1) * step]
 
 
-def hold_kernel(sizes, anchor_hbm, *refs):
-    got, (out_ref, anchor_ref, sem_ref) = refs[:-3], refs[-3:]
-    fetch(((anchor_hbm, anchor_ref),), sem_ref)
-    tile, member, anchor_row, _ = sizes.anchors(anchor_ref)
-    rows, step = sizes.rows, sizes.piece_rows
-    shape = (step, sizes.length)
-    inside = step * (iota(shape, 1) // TILE) + iota(shape, 0)
-    wanted = (anchor_row + ((rows * member + inside - anchor_row) & (sizes.span - 1))) // sizes.span
+def hold_kernel(sizes, choice_ref, *refs):
+    got, out_ref = refs[:-1], refs[-1]
+    rows = sizes.rows
+    choice = choice_ref[...]
     piece = got[0][rows:]
     for shift, ref in enumerate(got):
         out_ref[shift * rows:(shift + 1) * rows] = ref[:rows]
         if shift:
-            piece = jnp.where(wanted == (tile ^ shift), ref[rows:], piece)
+            piece = jnp.where(choice == shift, ref[rows:], piece)
     out_ref[len(got) * rows:] = piece
 
 
@@ -203,10 +200,15 @@
 
 
 def early_tables_kernel(sizes, probes, halves, anchor_hbm, small_hbm, *refs):
-    (rows_ref, left_ref, last_y_ref, incident_ref, weights_ref), (anchor_ref, small_ref, spots_ref, sem_ref) = refs[:5], refs[5:]
+    choice_ref, rows_ref, left_ref, last_y_ref, incident_ref, weights_ref = refs[:6]
+    anchor_ref, small_ref, spots_ref, sem_ref = refs[6:]
     fetch(((anchor_hbm, anchor_ref), (small_hbm, small_ref), (small_hbm, spots_ref)), sem_ref)
     tile, member, anchor_row, anchor_col = sizes.anchors(anchor_ref)
     half, kept, freqs, length = sizes.half, sizes.kept, sizes.freqs, sizes.length
+    shape = (sizes.piece_rows, length)
+    inside = sizes.piece_rows * (iota(shape, 1) // TILE) + iota(shape, 0)
+    residue = (sizes.rows * member + inside - anchor_row) & (sizes.span - 1)
+    choice_ref[...] = ((anchor_row + residue) // sizes.span) ^ tile
     place = whole(sizes.grid_row(iota((1, half), 1), tile, member))
     step = cis_index(-place, length)
     for top in range(0, kept, STRIP):
@@ -469,14 +471,9 @@
     same, other_side = call(
         functools.partial(pack_kernel, sizes),
         (full_type(rows + sizes.piece_rows, length),) * 2,
-        [HBM, HBM],
-        scratch_shapes=[
-            pltpu.SMEM(crop_anchor.shape, jnp.int32),
-            pltpu.VMEM(potential.shape, jnp.float32),
-            pltpu.SemaphoreType.DMA((2,)),
-        ],
+        [VMEM, VMEM],
         cost_estimate=estimate(1 << 16, 1 << 18),
-    )(crop_anchor, potential)
+    )(crop_anchor[None], potential)
     blocks = [same]
     for shift in range(1, tiles):
         sent = same if shift % sizes.per_side == 0 else other_side
@@ -484,9 +481,10 @@
     col_table, last_x = (jnp.asarray(table) for table in column_tables(sizes))
     small = pack_small(sizes, beam_tilts, aperture, aberration, probe_spots)
     fetched = [pltpu.SMEM(crop_anchor.shape, jnp.int32), pltpu.SMEM(small.shape, jnp.float32)]
-    row_table, left, last_y, incident, weights = call(
+    choice, row_table, left, last_y, incident, weights = call(
         functools.partial(early_tables_kernel, sizes, probes, halves),
         (
+            jax.ShapeDtypeStruct((sizes.piece_rows, length), jnp.int32),
             half_type(2, 2, 2 * kept, half),
             half_type(own, 2, 2 * TILE, freqs),
             half_type(1, 2, 2 * TILE, TILE),
@@ -507,10 +505,9 @@
     held = call(
         functools.partial(hold_kernel, sizes),
         full_type(sizes.block, length),
-        [HBM] + [VMEM] * tiles,
-        scratch_shapes=[pltpu.SMEM(crop_anchor.shape, jnp.int32), pltpu.SemaphoreType.DMA((1,))],
+        [VMEM] * (1 + tiles),
         cost_estimate=estimate(1 << 16, 1 << 19),
-    )(crop_anchor, *blocks)
+    )(choice, *blocks)
     gathered = {0: held}
     for bits in member_steps(group):
         for ordinal in list(gathered):

time: 47 us -> 45.4 us (0.966)
  Pallas kernels: 19.6 us -> 18.6 us
  waiting for transfers between devices: 12.6 us -> 12 us
    pallas_call x1, Pallas kernels: 0.59 us -> 0.02 us  [per_device(): call(functools.partial(hold_kernel, sizes), full_type(sizes.block, length...]
    ppermute x9, waiting for transfers between devices: 12.6 us -> 12 us  [swap(): return lax.ppermute(value, 'beam', [(i, i ^ bits) for i in range(devices)])]
  transfers between devices with their start and end apart: 9 -> 9, of which waited for: 5 -> 5; matrix products, arithmetic and copies ran while one was open for 4% -> 5% of each run, Pallas kernels for 16% -> 17%
where the time goes in v5:
time: 45.4 us; the launch traced here: 45.2 us
  Pallas kernels  18.6 us (41%)
  waiting for transfers between devices  12 us (26%)
  starting transfers between devices  8.3 us (18%)
  local copies, waits for them, and re-layouts  4.01 us (9%)
  other arithmetic  2.06 us (5%)
    ppermute x9, waiting for transfers between devices, swap(): return lax.ppermute(value, 'beam', [(i, i ^ bits) for i in range(devices)])  12 us
    ppermute x9, starting transfers between devices, swap(): return lax.ppermute(value, 'beam', [(i, i ^ bits) for i in range(devices)])  8.3 us
    pallas_call x2, Pallas kernels, per_device(): call(functools.partial(beams_kernel, sizes, h * some), (full_type(sets, 2...  7.2 us
    unnamed x12, local copies, waits for them, and re-layouts  4.01 us
    pallas_call x1, Pallas kernels, per_device(): call(functools.partial(early_tables_kernel, sizes, probes, halves), (jax....  2.61 us
    pallas_call x3, Pallas kernels, per_device(): call(functools.partial(spread_kernel, sizes), (half_type(2, 2, pairs, 2 *...  2.49 us
    pallas_call x1, Pallas kernels, per_device(): call(functools.partial(late_tables_kernel, sizes), (half_type(own, 2, fre...  2.48 us
    pallas_call x1, Pallas kernels, per_device(): call(functools.partial(spectrum_kernel, sizes, len(spreads)), (half_type(...  1.89 us
  transfers between devices with their start and end apart: 9, of which 5 were waited for; matrix products, arithmetic and copies ran while one was open for 5% of the time, Pallas kernels for 17%

profile of v5, /device:TPU:0, one launch (start us, length us, event | category | flops | bytes accessed | tf_op | source)
XLA Modules:
  0.0 45.2 jit_solution(8969387784387865949)
XLA Ops:
  0.0 0.0 copy-start.3
  0.0 0.9 %copy-done.3 = f32[2,32,512]{2,1,0:T(8,128)S(1)} copy-done((f32[2,32,512]{2,1,0:T(8,128)S(1)}, f32[2,32,512]{2,1,0:T(8,128)}, u32[]{:S(2)}) %copy-start.3) | copy-done | bytes 131096
  0.9 0.0 copy-start.4
  0.9 0.7 %copy-done.4 = s32[2]{0:T(128)S(1)} copy-done((s32[2]{0:T(128)S(1)}, s32[2]{0:T(128)}, u32[]{:S(2)}) %copy-start.4) | copy-done | bytes 32
  1.6 0.2 shard_map.83
  1.8 3.1 %collective-permute-start = (f32[40,512]{1,0:T(8,128)S(1)}, f32[40,512]{1,0:T(8,128)S(1)}, u32[]{:S(2)}, u32[]{:S(2)}) collective-permute-start(f32[40,512]{1,0:T(8,128)S(1)} %get-tuple-element.32), channel_id=1, source_target_pairs={{0,4},{1,5},{2,6},{3,7},{4,0},{5,1},{6,2},{7,3},{8,12},{9,13},{10,... | collective-permute-start | bytes 245768 | tf_op jit(solution)/shard_map/ppermute | solution.py:450
  4.9 2.5 %collective-permute-start.2 = (f32[40,512]{1,0:T(8,128)S(1)}, f32[40,512]{1,0:T(8,128)S(1)}, u32[]{:S(2)}, u32[]{:S(2)}) collective-permute-start(f32[40,512]{1,0:T(8,128)S(1)} %get-tuple-element.32), channel_id=1, source_target_pairs={{0,12},{1,13},{2,14},{3,15},{4,8},{5,9},{6,10},{7,11},{8,4},{9,5},... | collective-permute-start | bytes 245768 | tf_op jit(solution)/shard_map/ppermute | solution.py:450
  7.4 0.1 collective-permute-start.1
  7.5 0.7 %convert_element_type.19 = f32[4,32,2]{1,2,0:T(2,128)S(1)} convert(s32[4,32,2]{1,2,0:T(2,128)} %param.12) | non-fusion elementwise | flops 256 | bytes 2048 | tf_op jit(solution)/shard_map/convert_element_type | solution.py:578
  8.2 0.7 %convert_bitcast_fusion = f32[2,16]{1,0:T(2,128)S(1)} fusion(s32[16,2]{0,1:T(2,128)} %param.9), kind=kLoop, calls=%fused_computation.4 | loop fusion | flops 32 | bytes 256 | tf_op jit(solution)/shard_map/convert_element_type | solution.py:579
  8.9 0.7 %select_maximum_fusion = f32[4,32]{1,0:T(4,128)S(1)} fusion(f32[1,16]{1,0:T(1,128)} %bitcast.10, f32[1,16]{1,0:T(1,128)} %bitcast.11, f32[2,16]{1,0:T(2,128)S(1)} %convert_bitcast_fusion), kind=kLoop, calls=%fused_computation.1 | loop fusion | flops 768 | bytes 768 | tf_op jit(solution)/shard_map/concatenate | solution.py:579
  9.5 2.6 %shard_map.82 = (s32[8,512]{1,0:T(8,128)S(1)}, bf16[2,2,384,256]{3,2,1,0:T(8,128)(2,1)S(1)}, bf16[8,2,256,384]{3,2,1,0:T(8,128)(2,1)S(1)}, bf16[1,2,256,128]{3,2...) custom-call(s32[2]{0:T(128)S(1)} %copy-done.4, f32[12,32]{1,0:T(8,128)S(1)} %pad_maximum_fusion.small_hbm), custom_call_target="tpu_custom_call" | custom-call | flops 4194304 | bytes 6291456 | tf_op jit(solution)/shard_map/pallas_call | solution.py:484
  12.2 0.0 collective-permute-done.refs_1_
  12.2 2.9 %collective-permute-done.1.refs_2_ = f32[40,512]{1,0:T(8,128)S(1)} collective-permute-done((f32[40,512]{1,0:T(8,128)S(1)}, f32[40,512]{1,0:T(8,128)S(1)}, u32[]{:S(2)}, u32[]{:S(2)}) %collective-permute-start.1) | collective-permute-done | bytes 81952 | tf_op jit(solution)/shard_map/ppermute | solution.py:450
  15.0 0.0 collective-permute-done.2.refs_3_
  15.1 1.6 %collective-permute-start.4 = (f32[136,512]{1,0:T(8,128)S(1)}, f32[136,512]{1,0:T(8,128)S(1)}, u32[]{:S(2)}, u32[]{:S(2)}) collective-permute-start(f32[136,512]{1,0:T(8,128)S(1)} %shard_map.84.refs_0_), channel_id=1, source_target_pairs={{0,2},{1,3},{2,0},{3,1},{4,6},{5,7},{6,4},{7,5},{8,10},{9,11},{10,... | collective-permute-start | bytes 835592 | tf_op jit(solution)/shard_map/ppermute | solution.py:450
  16.6 0.0 collective-permute-start.3
  16.6 6.9 %collective-permute-done.4.refs_0_ = f32[136,512]{1,0:T(8,128)S(1)} collective-permute-done((f32[136,512]{1,0:T(8,128)S(1)}, f32[136,512]{1,0:T(8,128)S(1)}, u32[]{:S(2)}, u32[]{:S(2)}) %collective-permute-start.4) | collective-permute-done | bytes 278560 | tf_op jit(solution)/shard_map/ppermute | solution.py:450
  23.5 0.0 collective-permute-start.5
  23.5 2.5 %shard_map.89 = (bf16[8,2,384,256]{3,2,1,0:T(8,128)(2,1)S(1)}, bf16[8,384,384]{2,1,0:T(8,128)(2,1)S(1)}) custom-call(s32[2]{0:T(128)S(1)} %copy-done.4, f32[12,32]{1,0:T(8,128)S(1)} %pad_maximum_fusion.small_hbm), custom_call_target="tpu_custom_call" | custom-call | flops 4194304 | bytes 6291456 | tf_op jit(solution)/shard_map/pallas_call | solution.py:498
  26.0 0.0 copy-start
  26.0 1.2 %copy-done = bf16[2,2,256,512]{3,2,1,0:T(8,128)(2,1)S(1)} copy-done((bf16[2,2,256,512]{3,2,1,0:T(8,128)(2,1)S(1)}, bf16[2,2,256,512]{3,2,1,0:T(8,128)(2,1)}, u32[]{:S(2)}) %copy-start) | copy-done | bytes 1048600
  27.2 0.0 copy-start.2
  27.2 0.8 %shard_map.85 = (bf16[2,2,64,768]{3,2,1,0:T(8,128)(2,1)S(1)}, f32[8,512]{1,0:T(8,128)S(1)}) custom-call(f32[136,512]{1,0:T(8,128)S(1)} %shard_map.84.refs_0_, bf16[2,2,256,512]{3,2,1,0:T(8,128)(2,1)S(1)} %copy-done), custom_call_target="tpu_custom_call" | custom-call | flops 201326592 | bytes 2097152 | tf_op jit(solution)/shard_map/pallas_call | solution.py:522
  28.1 0.0 copy-start.1
  28.1 1.2 %copy-done.1 = bf16[2,2,256,512]{3,2,1,0:T(8,128)(2,1)S(1)} copy-done((bf16[2,2,256,512]{3,2,1,0:T(8,128)(2,1)S(1)}, bf16[2,2,256,512]{3,2,1,0:T(8,128)(2,1)}, u32[]{:S(2)}) %copy-start.1) | copy-done | bytes 1048600
  29.3 0.8 %shard_map.87 = (bf16[2,2,64,768]{3,2,1,0:T(8,128)(2,1)S(1)}, f32[8,512]{1,0:T(8,128)S(1)}) custom-call(f32[136,512]{1,0:T(8,128)S(1)} %collective-permute-done.4.refs_0_, bf16[2,2,256,512]{3,2,1,0:T(8,128)(2,1)S(1)} %copy-done.1), custom_call_target="tpu_custom_call" | custom-call | flops 201326592 | bytes 2097152 | tf_op jit(solution)/shard_map/pallas_call | solution.py:522
  30.1 0.0 collective-permute-done.3.refs_0_
  30.1 0.8 %shard_map.86 = (bf16[2,2,64,768]{3,2,1,0:T(8,128)(2,1)S(1)}, f32[8,512]{1,0:T(8,128)S(1)}) custom-call(f32[136,512]{1,0:T(8,128)S(1)} %collective-permute-done.3.refs_0_, bf16[2,2,256,512]{3,2,1,0:T(8,128)(2,1)S(1)} %copy-done.1), custom_call_target="tpu_custom_call" | custom-call | flops 201326592 | bytes 2097152 | tf_op jit(solution)/shard_map/pallas_call | solution.py:522
  31.0 0.0 collective-permute-done.5.refs_6_
  31.0 0.0 copy-done.2
  31.0 0.0 copy-start.5
  31.0 1.9 %shard_map.88 = (bf16[2,384,768]{2,1,0:T(8,128)(2,1)S(1)}, f32[2,128,128]{2,1,0:T(8,128)S(1)}) custom-call(bf16[2,2,64,768]{3,2,1,0:T(8,128)(2,1)S(1)} %get-tuple-element.33.refs_0_, bf16[2,2,64,768]{3,2,1,0:T(8,128)(2,1)S(1)} %get-tuple-element.34.refs_1_, bf16[2,2,64,768]{3,2,1,0:T(8,128)(2,1)S(1)} %get-tuple-element.35.refs_2_, ...), custom_call_target="tpu_custom_call" | custom-call | flops 3221225472 | bytes 4194304 | tf_op jit(solution)/shard_map/pallas_call | solution.py:530
  32.9 0.0 copy-done.5
  32.9 3.5 %shard_map.90 = (f32[2,256,128]{2,1,0:T(8,128)S(1)}, f32[2,256,128]{2,1,0:T(8,128)S(1)}) custom-call(bf16[2,384,768]{2,1,0:T(8,128)(2,1)S(1)} %get-tuple-element.40.spectrum_ref, bf16[8,2,256,384]{3,2,1,0:T(8,128)(2,1)S(1)} %get-tuple-element.41.left_ref, bf16[8,2,384,256]{3,2,1,0:T(8,128)(2,1)S(1)} %get-tuple-element.42.right_ref, ...), custom_call_target="tpu_custom_call" | custom-call | flops 4294967296 | bytes 4194304 | tf_op jit(solution)/shard_map/pallas_call | solution.py:541
  36.4 3.7 %shard_map.91 = (f32[2,256,128]{2,1,0:T(8,128)S(1)}, f32[2,256,128]{2,1,0:T(8,128)S(1)}) custom-call(bf16[2,384,768]{2,1,0:T(8,128)(2,1)S(1)} %get-tuple-element.40.spectrum_ref, bf16[8,2,256,384]{3,2,1,0:T(8,128)(2,1)S(1)} %get-tuple-element.41.left_ref, bf16[8,2,384,256]{3,2,1,0:T(8,128)(2,1)S(1)} %get-tuple-element.42.right_ref, ...), custom_call_target="tpu_custom_call" | custom-call | flops 4294967296 | bytes 4194304 | tf_op jit(solution)/shard_map/pallas_call | solution.py:541
  40.1 0.6 %collective-permute-start.6 = (f32[2,256,128]{2,1,0:T(8,128)S(1)}, f32[2,256,128]{2,1,0:T(8,128)S(1)}, u32[]{:S(2)}, u32[]{:S(2)}) collective-permute-start(f32[2,256,128]{2,1,0:T(8,128)S(1)} %get-tuple-element.48), channel_id=1, source_target_pairs={{0,1},{1,0},{2,3},{3,2},{4,5},{5,4},{6,7},{7,6},{8,9},{9,8},{10,11... | collective-permute-start | bytes 786440 | tf_op jit(solution)/shard_map/ppermute | solution.py:450
  40.7 0.1 collective-permute-start.7
  40.8 1.1 %collective-permute-done.6.refs_1_ = f32[2,256,128]{2,1,0:T(8,128)S(1)} collective-permute-done((f32[2,256,128]{2,1,0:T(8,128)S(1)}, f32[2,256,128]{2,1,0:T(8,128)S(1)}, u32[]{:S(2)}, u32[]{:S(2)}) %collective-permute-start.6) | collective-permute-done | bytes 262176 | tf_op jit(solution)/shard_map/ppermute | solution.py:450
  41.8 0.4 collective-permute-done.7.refs_3_
  42.2 0.9 %shard_map.92 = (f32[32,32,128]{2,1,0:T(8,128)S(1)}, f32[32,128]{1,0:T(8,128)S(1)}) custom-call(f32[64,32]{1,0:T(8,128)S(1)} %get-tuple-element.29.weights_ref, f32[2,256,128]{2,1,0:T(8,128)S(1)} %get-tuple-element.47.refs_0_, f32[2,256,128]{2,1,0:T(8,128)S(1)} %collective-permute-done.6.refs_1_, f32[2,256,128]{2,1,0:T(8,128)S(1)} %get-tuple-element.49.refs_2_, ...), custom_call_target="tpu_custom_call" | custom-call | flops 67108864 | bytes 2097152 | tf_op jit(solution)/shard_map/pallas_call | solution.py:552
  43.1 0.4 collective-permute-start.8
  43.5 0.8 %collective-permute-done.8.refs_1_ = f32[32,128]{1,0:T(8,128)S(1)} collective-permute-done((f32[32,128]{1,0:T(8,128)S(1)}, f32[32,128]{1,0:T(8,128)S(1)}, u32[]{:S(2)}, u32[]{:S(2)}) %collective-permute-start.8) | collective-permute-done | bytes 16416 | tf_op jit(solution)/shard_map/ppermute | solution.py:450
  44.4 0.8 %shard_map.93 = f32[32,32,128]{2,1,0:T(8,128)} custom-call(f32[32,32,128]{2,1,0:T(8,128)S(1)} %get-tuple-element.51.intensity_ref, f32[32,128]{1,0:T(8,128)S(1)} %get-tuple-element.52.refs_0_, f32[32,128]{1,0:T(8,128)S(1)} %collective-permute-done.8.refs_1_), custom_call_target="tpu_custom_call" | custom-call | flops 262144 | bytes 1048576 | tf_op jit(solution)/shard_map/pallas_call | solution.py:567
  (2 shorter events, 0.0 us)
Async XLA Ops:
  0.0 0.9 %copy-start.3 = (f32[2,32,512]{2,1,0:T(8,128)S(1)}, f32[2,32,512]{2,1,0:T(8,128)}, u32[]{:S(2)}) copy-start(f32[2,32,512]{2,1,0:T(8,128)} %potential_ref.1) | copy-start | bytes 393220
  0.9 0.7 %copy-start.4 = (s32[2]{0:T(128)S(1)}, s32[2]{0:T(128)}, u32[]{:S(2)}) copy-start(s32[2]{0:T(128)} %anchor_hbm.3) | copy-start | bytes 28
  1.8 10.4 %collective-permute-start = (f32[40,512]{1,0:T(8,128)S(1)}, f32[40,512]{1,0:T(8,128)S(1)}, u32[]{:S(2)}, u32[]{:S(2)}) collective-permute-start(f32[40,512]{1,0:T(8,128)S(1)} %get-tuple-element.32), channel_id=1, source_target_pairs={{0,4},{1,5},{2,6},{3,7},{4,0},{5,1},{6,2},{7,3},{8,12},{9,13},{10,... | collective-permute-start | bytes 245768 | tf_op jit(solution)/shard_map/ppermute | solution.py:450
  4.9 10.2 %collective-permute-start.2 = (f32[40,512]{1,0:T(8,128)S(1)}, f32[40,512]{1,0:T(8,128)S(1)}, u32[]{:S(2)}, u32[]{:S(2)}) collective-permute-start(f32[40,512]{1,0:T(8,128)S(1)} %get-tuple-element.32), channel_id=1, source_target_pairs={{0,12},{1,13},{2,14},{3,15},{4,8},{5,9},{6,10},{7,11},{8,4},{9,5},... | collective-permute-start | bytes 245768 | tf_op jit(solution)/shard_map/ppermute | solution.py:450
  7.4 7.7 %collective-permute-start.1 = (f32[40,512]{1,0:T(8,128)S(1)}, f32[40,512]{1,0:T(8,128)S(1)}, u32[]{:S(2)}, u32[]{:S(2)}) collective-permute-start(f32[40,512]{1,0:T(8,128)S(1)} %get-tuple-element.31.refs_0_), channel_id=1, source_target_pairs={{0,8},{1,9},{2,10},{3,11},{4,12},{5,13},{6,14},{7,15},{8,0},{9,1},... | collective-permute-start | bytes 245768 | tf_op jit(solution)/shard_map/ppermute | solution.py:450
  15.1 8.4 %collective-permute-start.4 = (f32[136,512]{1,0:T(8,128)S(1)}, f32[136,512]{1,0:T(8,128)S(1)}, u32[]{:S(2)}, u32[]{:S(2)}) collective-permute-start(f32[136,512]{1,0:T(8,128)S(1)} %shard_map.84.refs_0_), channel_id=1, source_target_pairs={{0,2},{1,3},{2,0},{3,1},{4,6},{5,7},{6,4},{7,5},{8,10},{9,11},{10,... | collective-permute-start | bytes 835592 | tf_op jit(solution)/shard_map/ppermute | solution.py:450
  16.6 13.5 %collective-permute-start.3 = (f32[136,512]{1,0:T(8,128)S(1)}, f32[136,512]{1,0:T(8,128)S(1)}, u32[]{:S(2)}, u32[]{:S(2)}) collective-permute-start(f32[136,512]{1,0:T(8,128)S(1)} %shard_map.84.refs_0_), channel_id=1, source_target_pairs={{0,1},{1,0},{2,3},{3,2},{4,5},{5,4},{6,7},{7,6},{8,9},{9,8},{10,11... | collective-permute-start | bytes 835592 | tf_op jit(solution)/shard_map/ppermute | solution.py:450
  23.5 7.5 %collective-permute-start.5 = (f32[136,512]{1,0:T(8,128)S(1)}, f32[136,512]{1,0:T(8,128)S(1)}, u32[]{:S(2)}, u32[]{:S(2)}) collective-permute-start(f32[136,512]{1,0:T(8,128)S(1)} %collective-permute-done.4.refs_0_), channel_id=1, source_target_pairs={{0,1},{1,0},{2,3},{3,2},{4,5},{5,4},{6,7},{7,6},{8,9},{9,8},{10,11... | collective-permute-start | bytes 835592 | tf_op jit(solution)/shard_map/ppermute | solution.py:450
  26.0 1.2 %copy-start = (bf16[2,2,256,512]{3,2,1,0:T(8,128)(2,1)S(1)}, bf16[2,2,256,512]{3,2,1,0:T(8,128)(2,1)}, u32[]{:S(2)}) copy-start(bf16[2,2,256,512]{3,2,1,0:T(8,128)(2,1)} %constant.7.clone.refs_1_.refs_7_) | copy-start | bytes 3145732
  27.2 3.8 %copy-start.2 = (bf16[2,2,256,512]{3,2,1,0:T(8,128)(2,1)S(1)}, bf16[2,2,256,512]{3,2,1,0:T(8,128)(2,1)}, u32[]{:S(2)}) copy-start(bf16[2,2,256,512]{3,2,1,0:T(8,128)(2,1)} %constant.7.clone.refs_1_.refs_7_) | copy-start | bytes 3145732
  28.1 1.2 %copy-start.1 = (bf16[2,2,256,512]{3,2,1,0:T(8,128)(2,1)S(1)}, bf16[2,2,256,512]{3,2,1,0:T(8,128)(2,1)}, u32[]{:S(2)}) copy-start(bf16[2,2,256,512]{3,2,1,0:T(8,128)(2,1)} %constant.7.clone.refs_1_.refs_7_) | copy-start | bytes 3145732
  31.0 1.9 %copy-start.5 = (bf16[1,2,128,256]{3,2,1,0:T(8,128)(2,1)S(1)}, bf16[1,2,128,256]{3,2,1,0:T(8,128)(2,1)}, u32[]{:S(2)}) copy-start(bf16[1,2,128,256]{3,2,1,0:T(8,128)(2,1)} %constant.8.clone.last_x_ref) | copy-start | bytes 393220
  40.1 1.7 %collective-permute-start.6 = (f32[2,256,128]{2,1,0:T(8,128)S(1)}, f32[2,256,128]{2,1,0:T(8,128)S(1)}, u32[]{:S(2)}, u32[]{:S(2)}) collective-permute-start(f32[2,256,128]{2,1,0:T(8,128)S(1)} %get-tuple-element.48), channel_id=1, source_target_pairs={{0,1},{1,0},{2,3},{3,2},{4,5},{5,4},{6,7},{7,6},{8,9},{9,8},{10,11... | collective-permute-start | bytes 786440 | tf_op jit(solution)/shard_map/ppermute | solution.py:450
  40.7 1.5 %collective-permute-start.7 = (f32[2,256,128]{2,1,0:T(8,128)S(1)}, f32[2,256,128]{2,1,0:T(8,128)S(1)}, u32[]{:S(2)}, u32[]{:S(2)}) collective-permute-start(f32[2,256,128]{2,1,0:T(8,128)S(1)} %get-tuple-element.50), channel_id=1, source_target_pairs={{0,1},{1,0},{2,3},{3,2},{4,5},{5,4},{6,7},{7,6},{8,9},{9,8},{10,11... | collective-permute-start | bytes 786440 | tf_op jit(solution)/shard_map/ppermute | solution.py:450
  43.1 1.2 %collective-permute-start.8 = (f32[32,128]{1,0:T(8,128)S(1)}, f32[32,128]{1,0:T(8,128)S(1)}, u32[]{:S(2)}, u32[]{:S(2)}) collective-permute-start(f32[32,128]{1,0:T(8,128)S(1)} %get-tuple-element.52.refs_0_), channel_id=1, source_target_pairs={{0,1},{1,0},{2,3},{3,2},{4,5},{5,4},{6,7},{7,6},{8,9},{9,8},{10,11... | collective-permute-start | bytes 49160 | tf_op jit(solution)/shard_map/ppermute | solution.py:450
